TPU v7x, 32 devices: a whole 2x2x4 slice. The times are simulated.
32 devices in a mesh: cells: 2 (over x), fh: 16 (over z, y, core).
Axes of the slice: x: 2, y: 2, z: 4, core: 2. Of those that a mesh axis runs over, the one named last changes fastest.
Arguments:
- received_time_rows: bfloat16 [4096, 3, 2, 4096], P(('cells', 'fh')), parts along dimension 0, may hold values from -24 to 24
- pilots: int32 [128], P('cells'), parts along dimension 0, may hold values from 0 to 63, as said below
- active_users: int32 [128], P('cells'), parts along dimension 0, may hold values 0 or 1
- allocation: int32 [256, 64], P(('cells', 'fh')), parts along dimension 0, may hold values 0 or 1
- loading: float32 [128], P('cells'), parts along dimension 0, may hold values from 0.25 to 4
Outputs:
- equalized: float32 [128, 1, 2, 4096], P(('cells', 'fh')), parts along dimension 0
There are 2 independent parts, one for each index of `cells`. A program takes and returns all parts, laid end to end along the dimension named above; each array names one. Nothing has to cross between parts.
Inputs may be any that keep to these rules, and one draw needn't show every extreme that they name: `pilots`: the 64 pilot sequences of a cell are distinct.
All inputs are finite; a program needn't handle non-finite values. No bound on the sum of `allocation` on one device may be relied on, other than what follows from the above.
Results may differ from a plain program's by a relative error of at most 0.0076.
Values may be sent and summed in bfloat16 or wider, within the bound.
No kernel may reach another device: no remote copies, remote signals or barrier semaphores. Data moves between devices by JAX's collectives and lax.ppermute only.
A program may use at most 128 MiB of HBM per device.

v0:
```python
import math

import jax
import jax.numpy as jnp
from jax import lax
from jax.sharding import PartitionSpec as P

SUBCARRIER_COUNT = 4096
PSYM = 2
B = 32
FA = 16
FB = 256


def dft_table(length):
    indices = jnp.arange(length, dtype=jnp.int32)
    phase_index = indices[:, None] * indices[None, :] % length
    angles = phase_index.astype(jnp.float32) * (2.0 * math.pi / length)
    cos_part = jnp.cos(angles)
    sin_part = jnp.sin(angles)
    layout = jnp.stack([jnp.stack([cos_part, -sin_part], 1), jnp.stack([sin_part, cos_part], 1)], 0)
    return layout.astype(jnp.bfloat16)


def twiddle_parts():
    inner_idx = jnp.arange(FA, dtype=jnp.int32)
    outer_idx = jnp.arange(FB, dtype=jnp.int32)
    phase_index = inner_idx[:, None] * outer_idx[None, :] % SUBCARRIER_COUNT
    angles = phase_index.astype(jnp.float32) * (2.0 * math.pi / SUBCARRIER_COUNT)
    factor = 1.0 / math.sqrt(SUBCARRIER_COUNT)
    return (jnp.cos(angles) * factor, jnp.sin(angles) * factor)


def spectra(samples):
    antennas_here = samples.shape[0]
    symbol_count = samples.shape[1]
    shaped = samples.reshape(antennas_here, symbol_count, 2, FA, FB)
    section_one = jnp.einsum(
        "ascnm,cndk->sdkma", shaped, dft_table(FA), preferred_element_type=jnp.float32
    )
    cos_part, sin_part = twiddle_parts()
    cos_part = cos_part[:, :, None]
    sin_part = sin_part[:, :, None]
    real_part = section_one[:, 0] * cos_part + section_one[:, 1] * sin_part
    imag_part = section_one[:, 1] * cos_part - section_one[:, 0] * sin_part
    section_one = jnp.stack([real_part, imag_part], 1).astype(jnp.bfloat16)
    section_two = jnp.einsum(
        "sckma,cmdj->sdkja", section_one, dft_table(FB), preferred_element_type=jnp.float32
    )
    return section_two.astype(jnp.bfloat16)


def split_blocks(spectrum):
    width_b = B // FA
    shape_in = spectrum.shape
    return spectrum.reshape(shape_in[0], 2, FA, shape_in[3] // width_b, width_b, shape_in[4])


def code_table(pilots):
    width_b = B // FA
    position = (
        jnp.arange(PSYM, dtype=jnp.int32)[:, None, None] * B
        + jnp.arange(FA, dtype=jnp.int32)[None, :, None]
        + FA * jnp.arange(width_b, dtype=jnp.int32)[None, None, :]
    )
    phase_index = pilots[:, None, None, None] * position[None] % (PSYM * B)
    angles = phase_index.astype(jnp.float32) * (2.0 * math.pi / (PSYM * B))
    factor = 1.0 / math.sqrt(PSYM * B)
    cos_part = jnp.cos(angles) * factor
    sin_part = jnp.sin(angles) * factor
    rows_real = jnp.stack([cos_part, sin_part], 2)
    rows_imag = jnp.stack([-sin_part, cos_part], 2)
    return jnp.stack([rows_real, rows_imag], 0).astype(jnp.bfloat16)


def block_terms(pilot_part, data_part, code_rows):
    channel = jnp.einsum(
        "tcarbm,dktcab->rdkm", pilot_part, code_rows, preferred_element_type=jnp.float32
    ).astype(jnp.bfloat16)
    gram = jnp.einsum("rdkm,relm->rdkel", channel, channel, preferred_element_type=jnp.float32)
    gram_real = gram[:, 0, :, 0] + gram[:, 1, :, 1]
    gram_imag = gram[:, 0, :, 1] - gram[:, 1, :, 0]
    matched = jnp.einsum(
        "rdkm,tcarbm->rdktcab", channel, data_part, preferred_element_type=jnp.float32
    )
    matched_real = matched[:, 0, :, :, 0] + matched[:, 1, :, :, 1]
    matched_imag = matched[:, 0, :, :, 1] - matched[:, 1, :, :, 0]
    blocks = matched_real.shape[0]
    user_count = matched_real.shape[1]
    matched_real = matched_real.reshape(blocks, user_count, -1)
    matched_imag = matched_imag.reshape(blocks, user_count, -1)
    left_half = jnp.stack([gram_real, gram_imag], 1)
    right_half = jnp.stack([matched_real, matched_imag], 1)
    return jnp.concatenate([left_half, right_half], 3)


def mmse_equalizer(packed_layout, served_users, loading, antennas):
    user_count = served_users.shape[1]
    pair_mask = served_users[:, :, None] * served_users[:, None, :]
    diagonal = jnp.eye(user_count, dtype=jnp.float32) * loading[None, :]
    sys_real = pair_mask * packed_layout[:, 0, :, :user_count] / antennas + diagonal[None]
    sys_imag = pair_mask * packed_layout[:, 1, :, :user_count] / antennas
    root_count = math.sqrt(antennas)
    side_real = served_users[:, :, None] * packed_layout[:, 0, :, user_count:] / root_count
    side_imag = served_users[:, :, None] * packed_layout[:, 1, :, user_count:] / root_count
    matrix = jnp.concatenate(
        [jnp.concatenate([sys_real, -sys_imag], 2), jnp.concatenate([sys_imag, sys_real], 2)], 1
    )
    right_side = jnp.concatenate([side_real, side_imag], 1)
    factor_low = jnp.linalg.cholesky(matrix)
    solved = jax.scipy.linalg.cho_solve((factor_low, True), right_side)
    blocks = solved.shape[0]
    solved = solved.reshape(blocks, 2, user_count, -1, FA, B // FA)
    solved = jnp.transpose(solved, (2, 3, 1, 0, 5, 4))
    return solved.reshape(user_count, solved.shape[1], 2, -1)


def on_device(received_time_rows, pilots, active_users, allocation, loading):
    spectrum = spectra(received_time_rows)
    code_rows = code_table(pilots)
    pilot_part = lax.all_to_all(spectrum[:PSYM], "fh", split_axis=3, concat_axis=4, tiled=True)
    data_part = lax.all_to_all(spectrum[PSYM:], "fh", split_axis=3, concat_axis=4, tiled=True)
    antenna_total = pilot_part.shape[4]
    packed_layout = block_terms(split_blocks(pilot_part), split_blocks(data_part), code_rows)
    served_users = active_users.astype(jnp.float32)[None, :] * allocation.astype(jnp.float32)
    result = mmse_equalizer(packed_layout, served_users, loading, antenna_total)
    return lax.all_to_all(result, "fh", split_axis=0, concat_axis=3, tiled=True)


def solution(mesh):
    return jax.shard_map(
        on_device,
        mesh=mesh,
        in_specs=(
            P(("cells", "fh"), None, None, None),
            P("cells"),
            P("cells"),
            P(("cells", "fh"), None),
            P("cells"),
        ),
        out_specs=P(("cells", "fh"), None, None, None),
        check_vma=False,
    )
```

profile of v0, /device:TPU:0, one launch (start us, length us, event | category | flops | bytes accessed | tf_op | source)
XLA Modules:
  0.0 409.8 jit_solution(7066106346783006127)
XLA Ops:
  0.0 0.1 negate_convert_fusion.2
  0.1 0.1 fusion.66
  0.1 0.1 sine_multiply_fusion.1
  0.2 1.1 negate_convert_fusion
  1.3 1.0 fusion.43
  2.3 10.8 %reshape.367 = bf16[128,3,2,16,256,1]{4,3,2,1,0,5:T(8,128)(2,1)} reshape(bf16[128,3,2,4096]{3,2,1,0:T(2,128)(2,1)} %param.5) | data formatting | bytes 12582912 | tf_op jit(solution)/shard_map/reshape | solution.py:37
  13.2 4.6 %convolution_bitcast_fusion = f32[3,2,16,256,128]{3,2,0,4,1:T(8,128)S(1)} fusion(bf16[128,3,2,16,256,1]{4,3,2,1,0,5:T(8,128)(2,1)} %reshape.367, bf16[1,16,2,16]{1,3,0,2:T(8,128)(2,1)S(1)} %get-tuple-element.19, bf16[1,16,2,16]{1,3,0,2:T(8,128)(2,1)S(1)} %get-tuple-element.18), kind=kOutput, calls=%fused_computation.8 | convolution fusion | flops 201330688 | bytes 18876416 | tf_op jit(solution)/shard_map/ascnm,cndk->sdkma/dot_general | solution.py:38
  17.8 2.2 add_convert_fusion
  20.0 3.2 pad_maximum_fusion
  23.2 9.2 %copy.113 = bf16[3,2,16,256,128]{4,3,1,2,0:T(8,128)(2,1)} copy(bf16[3,2,16,256,128]{3,2,0,4,1:T(8,128)(2,1)} %pad_maximum_fusion) | data formatting | bytes 12582912 | tf_op jit(solution)/shard_map/stack | solution.py:46
  32.4 6.5 %fusion = bf16[3,2,16,256,128]{4,3,2,0,1:T(8,128)(2,1)S(1)} fusion(bf16[3,2,16,256,128]{4,3,1,2,0:T(8,128)(2,1)} %copy.113, bf16[1,256,2,256]{1,3,0,2:T(8,128)(2,1)S(1)} %get-tuple-element.13, bf16[1,256,2,256]{1,3,0,2:T(8,128)(2,1)S(1)} %get-tuple-element.12), kind=kOutput, calls=%fused_computation.2 | convolution fusion | flops 3225419776 | bytes 13107200 | tf_op jit(solution)/shard_map/sckma,cmdj->sdkja/dot_general | solution.py:47
  38.9 0.0 copy-start
  39.0 2.7 copy-done
  41.6 0.1 slice.75
  41.8 2.7 copy.124
  44.5 7.4 %all-to-all-start.1 = ((bf16[1,2,16,256,128]{4,2,0,1,3:T(8,128)(2,1)}), bf16[1,2,16,256,128]{4,2,0,1,3:T(8,128)(2,1)S(1)}, u32[]{:S(2)}, u32[]{:S(2)}) async-start(bf16[1,2,16,256,128]{4,2,0,1,3:T(8,128)(2,1)} %copy.124), calls=%async_computation.1 | async-start | bytes 4194304 | tf_op jit(solution)/shard_map/all_to_all | solution.py:122
  51.9 0.0 slice-start
  51.9 2.2 slice-done
  54.1 4.7 %copy.114 = bf16[2,2,16,256,128]{4,2,0,1,3:T(8,128)(2,1)} copy(bf16[2,2,16,256,128]{4,3,2,0,1:T(8,128)(2,1)S(1)} %slice-done) | data formatting | bytes 8388608 | tf_op jit(solution)/shard_map/slice | solution.py:121
  58.7 0.0 copy-start.4
  58.7 0.0 copy-start.2
  58.8 0.0 copy-start.1
  58.8 0.0 copy-start.3
  58.8 34.2 %all-to-all-done.1 = bf16[1,2,16,256,128]{4,2,0,1,3:T(8,128)(2,1)S(1)} async-done(((bf16[1,2,16,256,128]{4,2,0,1,3:T(8,128)(2,1)}), bf16[1,2,16,256,128]{4,2,0,1,3:T(8,128)(2,1)S(1)}, u32[]{:S(2)}, u32[]{:S(2)}) %all-to-all-start.1) | async-done | bytes 2097184 | tf_op jit(solution)/shard_map/all_to_all | solution.py:122
  93.0 11.3 %all-to-all-start = ((bf16[2,2,16,256,128]{4,2,0,1,3:T(8,128)(2,1)}), bf16[2,2,16,256,128]{4,2,0,1,3:T(8,128)(2,1)}, u32[]{:S(2)}, u32[]{:S(2)}) async-start(bf16[2,2,16,256,128]{4,2,0,1,3:T(8,128)(2,1)} %copy.114), calls=%async_computation | async-start | bytes 8388608 | tf_op jit(solution)/shard_map/all_to_all | solution.py:121
  104.2 0.0 copy-done.4
  104.3 0.1 iota_add_fusion
  104.4 0.1 broadcast_add_fusion
  104.5 0.0 copy-done.2
  104.5 0.2 fusion.50
  104.7 0.0 copy-done.1
  104.8 0.0 copy-done.3
  104.8 0.1 fusion.49
  104.8 3.8 copy.191
  108.6 2.8 reshape.363
  111.5 70.5 %all-to-all-done = bf16[2,2,16,256,128]{4,2,0,1,3:T(8,128)(2,1)} async-done(((bf16[2,2,16,256,128]{4,2,0,1,3:T(8,128)(2,1)}), bf16[2,2,16,256,128]{4,2,0,1,3:T(8,128)(2,1)}, u32[]{:S(2)}, u32[]{:S(2)}) %all-to-all-start) | async-done | bytes 4194336 | tf_op jit(solution)/shard_map/all_to_all | solution.py:121
  181.9 9.0 %copy.190 = bf16[2,2,16,16,16,128]{5,3,2,4,1,0:T(8,128)(2,1)} copy(bf16[2,2,16,16,16,128]{5,2,0,1,4,3:T(8,128)(2,1)} %bitcast.23) | data formatting | bytes 8388608 | tf_op jit(solution)/shard_map/all_to_all | solution.py:121
  190.9 7.3 %reshape.362 = bf16[2,2,16,8,2,2048]{5,2,4,3,1,0:T(8,128)(2,1)} reshape(bf16[2,2,16,16,16,128]{5,4,2,3,1,0:T(8,128)(2,1)} %bitcast.138) | data formatting | bytes 8388608 | tf_op jit(solution)/shard_map/reshape | solution.py:56
  198.3 3.5 fusion.8
  201.7 2.1 fusion.3
  203.9 2.1 fusion.14
  206.0 0.1 copy.128
  206.1 0.1 copy.130
  206.2 0.2 fusion.71
  206.4 0.2 maximum_maximum_fusion
  206.6 0.2 copy.123
  206.8 0.2 fusion.25
  207.0 93.8 %custom-call.11 = f32[8,128,128]{2,1,0:T(8,128)S(1)} custom-call(f32[8,128,128]{2,1,0:T(8,128)S(1)} %fusion.25), custom_call_target="Cholesky" | custom-call | tf_op jit(solution)/shard_map/jit(cholesky)/cholesky | solution.py:110
  300.8 0.1 select_reduce_fusion
  300.9 0.1 compare_reduce_fusion
  301.0 0.1 select_bitcast_fusion
  301.1 78.6 %custom-call.12 = f32[8,1,128,128]{2,3,1,0:T(8,128)S(1)} custom-call(f32[8,1,128,128]{3,2,1,0:T(8,128)S(1)} %select_bitcast_fusion), custom_call_target="InvertDiagBlocksLowerTriangular" | custom-call | tf_op jit(solution)/shard_map/jit(_cho_solve)/vmap()/triangular_solve | solution.py:111
  379.7 0.1 fusion.41
  379.8 0.6 fusion.23
  380.4 0.9 fusion.21
  381.3 0.2 reshape.364
  381.5 0.1 copy.135
  381.7 27.4 %all_to_all.48 = f32[64,1,2,256]{3,2,1,0:T(2,128)S(1)} all-to-all(f32[64,1,2,256]{3,2,1,0:T(2,128)S(1)} %copy.135), channel_id=1, replica_groups=mesh['cells'=2,'fh'=16] {'fh'}, dimensions={0} | all-to-all | bytes 262144 | tf_op jit(solution)/shard_map/all_to_all | solution.py:127
  409.1 0.7 copy.161
  (11 shorter events, 0.2 us)
Async XLA Ops:
  38.9 2.7 copy-start
  44.5 48.5 %all-to-all-start.1 = ((bf16[1,2,16,256,128]{4,2,0,1,3:T(8,128)(2,1)}), bf16[1,2,16,256,128]{4,2,0,1,3:T(8,128)(2,1)S(1)}, u32[]{:S(2)}, u32[]{:S(2)}) async-start(bf16[1,2,16,256,128]{4,2,0,1,3:T(8,128)(2,1)} %copy.124), calls=%async_computation.1 | async-start | bytes 4194304 | tf_op jit(solution)/shard_map/all_to_all | solution.py:122
  51.9 2.2 slice-start
  58.7 45.5 %copy-start.4 = (s32[64]{0:T(128)S(1)}, s32[64]{0:T(128)}, u32[]{:S(2)}) copy-start(s32[64]{0:T(128)} %param.7) | copy-start | bytes 772
  58.7 45.7 %copy-start.2 = (s32[64]{0:T(128)S(1)}, s32[64]{0:T(128)}, u32[]{:S(2)}) copy-start(s32[64]{0:T(128)} %param.6) | copy-start | bytes 772
  58.8 46.0 %copy-start.1 = (s32[8,64]{1,0:T(8,128)S(1)}, s32[8,64]{1,0:T(8,128)}, u32[]{:S(2)}) copy-start(s32[8,64]{1,0:T(8,128)} %param.8) | copy-start | bytes 6148
  58.8 46.0 %copy-start.3 = (f32[64]{0:T(128)S(1)}, f32[64]{0:T(128)}, u32[]{:S(2)}) copy-start(f32[64]{0:T(128)} %param.9) | copy-start | bytes 772
  93.0 88.9 %all-to-all-start = ((bf16[2,2,16,256,128]{4,2,0,1,3:T(8,128)(2,1)}), bf16[2,2,16,256,128]{4,2,0,1,3:T(8,128)(2,1)}, u32[]{:S(2)}, u32[]{:S(2)}) async-start(bf16[2,2,16,256,128]{4,2,0,1,3:T(8,128)(2,1)} %copy.114), calls=%async_computation | async-start | bytes 8388608 | tf_op jit(solution)/shard_map/all_to_all | solution.py:121
where the time goes:
time: 411 us; the launch traced here: 410 us
  other arithmetic  182 us (44%)
  waiting for transfers between devices  105 us (26%)
  local copies, waits for them, and re-layouts  56.8 us (14%)
  blocking collectives  27.4 us (7%)
  matrix products  20.4 us (5%)
  starting transfers between devices  18.6 us (5%)
    another operation x4, other arithmetic, mmse_equalizer(): factor_low = jnp.linalg.cholesky(matrix)  94 us
    another operation x3, other arithmetic, mmse_equalizer(): solved = jax.scipy.linalg.cho_solve((factor_low, True), right_side)  78.7 us
    all_to_all x1, waiting for transfers between devices, on_device(): lax.all_to_all(spectrum[:PSYM], 'fh', split_axis=3, concat_axis=4, tiled=...  70.5 us
    all_to_all x1, waiting for transfers between devices, on_device(): lax.all_to_all(spectrum[PSYM:], 'fh', split_axis=3, concat_axis=4, tiled=...  34.2 us
    all_to_all x1, blocking collectives, on_device(): return lax.all_to_all(result, 'fh', split_axis=0, concat_axis=3, tiled=True)  27.4 us
    all_to_all x1, starting transfers between devices, on_device(): lax.all_to_all(spectrum[:PSYM], 'fh', split_axis=3, concat_axis=4, tiled=...  11.3 us
    reshape x1, local copies, waits for them, and re-layouts, spectra(): shaped = samples.reshape(antennas_here, symbol_count, 2, FA, FB)  10.8 us
    another operation x1, local copies, waits for them, and re-layouts, spectra(): section_one = jnp.stack([real_part, imag_part], 1).astype(jnp.bfloat16)  9.19 us
  transfers between devices with their start and end apart: 2, of which 2 were waited for; matrix products, arithmetic and copies ran while one was open for 3% of the time, Pallas kernels for 0%

commit v1 on v0

--- a/solution.py
+++ b/solution.py
@@ -3,6 +3,8 @@
 import jax
 import jax.numpy as jnp
 from jax import lax
+from jax.experimental import pallas as pl
+from jax.experimental.pallas import tpu as pltpu
 from jax.sharding import PartitionSpec as P
 
 SUBCARRIER_COUNT = 4096
@@ -10,6 +12,74 @@
 B = 32
 FA = 16
 FB = 256
+
+PANEL = 8
+PREC = lax.Precision.HIGHEST
+
+
+def _solve_body(a_ref, b_ref, x_ref, s_ref, lt_ref, l_ref):
+    nb, n, _ = a_ref.shape
+    s_ref[...] = a_ref[...]
+    x_ref[...] = b_ref[...]
+    lane = lax.broadcasted_iota(jnp.int32, (1, n), 1)
+
+    def panel(p, carry):
+        j0 = pl.multiple_of(p * PANEL, PANEL)
+        rows = [s_ref[b, pl.ds(j0, PANEL), :] for b in range(nb)]
+        xts = [x_ref[b] for b in range(nb)]
+        factors = [[] for b in range(nb)]
+        for t in range(PANEL):
+            j = j0 + t
+            hit = lane == j
+            keep = lane >= j
+            after = lane > j
+            for b in range(nb):
+                d = jnp.sum(jnp.where(hit, rows[b][t:t + 1, :], 0.0), axis=1, keepdims=True)
+                inv = 1.0 / jnp.sqrt(d)
+                l = jnp.where(keep, rows[b][t:t + 1, :], 0.0) * inv
+                col = jnp.sum(jnp.where(hit, rows[b], 0.0), axis=1, keepdims=True) * inv
+                rows[b] = rows[b] - col * l
+                y = jnp.sum(jnp.where(hit, xts[b], 0.0), axis=1, keepdims=True) * inv
+                xts[b] = jnp.where(hit, y, xts[b] - y * jnp.where(after, l, 0.0))
+                factors[b].append(l)
+        for b in range(nb):
+            block = jnp.concatenate(factors[b], axis=0)
+            lt_ref[b, pl.ds(j0, PANEL), :] = block
+            x_ref[b] = xts[b]
+            update = lax.dot_general(
+                block, block, (((0,), (0,)), ((), ())),
+                precision=PREC, preferred_element_type=jnp.float32)
+            s_ref[b] = s_ref[b] - update
+        return carry
+
+    lax.fori_loop(0, n // PANEL, panel, 0)
+    for b in range(nb):
+        l_ref[b] = jnp.transpose(lt_ref[b])
+
+    def backward(t, carry):
+        i = n - 1 - t
+        for b in range(nb):
+            lrow = l_ref[b, pl.ds(i, 1), :]
+            lii = jnp.sum(jnp.where(lane == i, lrow, 0.0), axis=1, keepdims=True)
+            yt = x_ref[b]
+            xi = jnp.sum(jnp.where(lane == i, yt, 0.0), axis=1, keepdims=True) / lii
+            x_ref[b] = jnp.where(lane == i, xi, yt - xi * jnp.where(lane < i, lrow, 0.0))
+        return carry
+
+    lax.fori_loop(0, n, backward, 0)
+
+
+def spd_solve_t(matrix, rhs_t):
+    nb, n, _ = matrix.shape
+    return pl.pallas_call(
+        _solve_body,
+        out_shape=jax.ShapeDtypeStruct(rhs_t.shape, jnp.float32),
+        scratch_shapes=[
+            pltpu.VMEM((nb, n, n), jnp.float32),
+            pltpu.VMEM((nb, n, n), jnp.float32),
+            pltpu.VMEM((nb, n, n), jnp.float32),
+        ],
+    )(matrix, rhs_t)
 
 
 def dft_table(length):
@@ -107,8 +177,7 @@
         [jnp.concatenate([sys_real, -sys_imag], 2), jnp.concatenate([sys_imag, sys_real], 2)], 1
     )
     right_side = jnp.concatenate([side_real, side_imag], 1)
-    factor_low = jnp.linalg.cholesky(matrix)
-    solved = jax.scipy.linalg.cho_solve((factor_low, True), right_side)
+    solved = jnp.swapaxes(spd_solve_t(matrix, jnp.swapaxes(right_side, 1, 2)), 1, 2)
     blocks = solved.shape[0]
     solved = solved.reshape(blocks, 2, user_count, -1, FA, B // FA)
     solved = jnp.transpose(solved, (2, 3, 1, 0, 5, 4))

time: 411 us -> 289 us (0.70)
  other arithmetic: 182 us -> 10.2 us
  Pallas kernels: 0 us -> 50.4 us
    another operation x13 -> x6, other arithmetic: 177 us -> 4.63 us  [the longest x4 94 us: mmse_equalizer(): factor_low = jnp.linalg.cholesky(matrix)]
    pallas_call x0 -> x1, Pallas kernels: none -> 50.4 us  [spd_solve_t(): pl.pallas_call(_solve_body, out_shape=jax.ShapeDtypeStruct(rhs_t.shape, j...]
  transfers between devices with their start and end apart: 2 -> 2, of which waited for: 2 -> 2; matrix products, arithmetic and copies ran while one was open for 3% -> 4% of each run, Pallas kernels for 0% -> 0%
where the time goes in v1:
time: 289 us; the launch traced here: 288 us
  waiting for transfers between devices  105 us (36%)
  local copies, waits for them, and re-layouts  57.4 us (20%)
  Pallas kernels  50.4 us (17%)
  blocking collectives  27.4 us (9%)
  matrix products  18.9 us (7%)
  starting transfers between devices  18.6 us (6%)
  other arithmetic  10.2 us (4%)
    all_to_all x1, waiting for transfers between devices, on_device(): lax.all_to_all(spectrum[:PSYM], 'fh', split_axis=3, concat_axis=4, tiled=...  70.5 us
    pallas_call x1, Pallas kernels, spd_solve_t(): pl.pallas_call(_solve_body, out_shape=jax.ShapeDtypeStruct(rhs_t.shape, j...  50.4 us
    all_to_all x1, waiting for transfers between devices, on_device(): lax.all_to_all(spectrum[PSYM:], 'fh', split_axis=3, concat_axis=4, tiled=...  34.2 us
    all_to_all x1, blocking collectives, on_device(): return lax.all_to_all(result, 'fh', split_axis=0, concat_axis=3, tiled=True)  27.4 us
    all_to_all x1, starting transfers between devices, on_device(): lax.all_to_all(spectrum[:PSYM], 'fh', split_axis=3, concat_axis=4, tiled=...  11.3 us
    reshape x1, local copies, waits for them, and re-layouts, spectra(): shaped = samples.reshape(antennas_here, symbol_count, 2, FA, FB)  10.8 us
    another operation x1, local copies, waits for them, and re-layouts, spectra(): section_one = jnp.stack([real_part, imag_part], 1).astype(jnp.bfloat16)  9.14 us
    all_to_all x1, local copies, waits for them, and re-layouts, on_device(): lax.all_to_all(spectrum[:PSYM], 'fh', split_axis=3, concat_axis=4, tiled=...  9.04 us
  transfers between devices with their start and end apart: 2, of which 2 were waited for; matrix products, arithmetic and copies ran while one was open for 4% of the time, Pallas kernels for 0%

profile of v1, /device:TPU:0, one launch (start us, length us, event | category | flops | bytes accessed | tf_op | source)
XLA Modules:
  0.0 287.9 jit_solution(11965589932998758171)
XLA Ops:
  0.0 0.1 negate_convert_fusion.2
  0.1 0.1 fusion.56
  0.1 0.1 sine_multiply_fusion.1
  0.2 1.1 negate_convert_fusion
  1.3 1.0 fusion.33
  2.3 10.8 %reshape.353 = bf16[128,3,2,16,256,1]{4,3,2,1,0,5:T(8,128)(2,1)} reshape(bf16[128,3,2,4096]{3,2,1,0:T(2,128)(2,1)} %param.5) | data formatting | bytes 12582912 | tf_op jit(solution)/shard_map/reshape | solution.py:107
  13.2 4.7 %convolution_bitcast_fusion = f32[3,2,16,256,128]{3,2,0,4,1:T(8,128)S(1)} fusion(bf16[128,3,2,16,256,1]{4,3,2,1,0,5:T(8,128)(2,1)} %reshape.353, bf16[1,16,2,16]{1,3,0,2:T(8,128)(2,1)S(1)} %get-tuple-element.19, bf16[1,16,2,16]{1,3,0,2:T(8,128)(2,1)S(1)} %get-tuple-element.18), kind=kOutput, calls=%fused_computation.8 | convolution fusion | flops 201330688 | bytes 18876416 | tf_op jit(solution)/shard_map/ascnm,cndk->sdkma/dot_general | solution.py:108
  17.8 2.2 add_convert_fusion
  20.0 3.2 %pad_maximum_fusion = bf16[3,2,16,256,128]{3,2,0,4,1:T(8,128)(2,1)} fusion(bf16[3,1,16,256,128]{3,2,0,4,1:T(8,128)(2,1)S(1)} %get-tuple-element.8, bf16[3,1,16,256,128]{3,2,0,4,1:T(8,128)(2,1)S(1)} %get-tuple-element.7), kind=kLoop, calls=%fused_computation.3 | loop fusion | flops 3145728 | bytes 12582912 | tf_op jit(solution)/shard_map/stack | solution.py:116
  23.3 9.1 %copy.76 = bf16[3,2,16,256,128]{4,3,1,2,0:T(8,128)(2,1)} copy(bf16[3,2,16,256,128]{3,2,0,4,1:T(8,128)(2,1)} %pad_maximum_fusion) | data formatting | bytes 12582912 | tf_op jit(solution)/shard_map/stack | solution.py:116
  32.4 6.5 %fusion = bf16[3,2,16,256,128]{4,3,2,0,1:T(8,128)(2,1)S(1)} fusion(bf16[3,2,16,256,128]{4,3,1,2,0:T(8,128)(2,1)} %copy.76, bf16[1,256,2,256]{1,3,0,2:T(8,128)(2,1)S(1)} %get-tuple-element.13, bf16[1,256,2,256]{1,3,0,2:T(8,128)(2,1)S(1)} %get-tuple-element.12), kind=kOutput, calls=%fused_computation.2 | convolution fusion | flops 3225419776 | bytes 13107200 | tf_op jit(solution)/shard_map/sckma,cmdj->sdkja/dot_general | solution.py:117
  38.9 0.0 copy-start
  39.0 2.7 copy-done
  41.6 0.1 slice.57
  41.7 2.7 copy.84
  44.5 7.4 %all-to-all-start.1 = ((bf16[1,2,16,256,128]{4,2,0,1,3:T(8,128)(2,1)}), bf16[1,2,16,256,128]{4,2,0,1,3:T(8,128)(2,1)S(1)}, u32[]{:S(2)}, u32[]{:S(2)}) async-start(bf16[1,2,16,256,128]{4,2,0,1,3:T(8,128)(2,1)} %copy.84), calls=%async_computation.1 | async-start | bytes 4194304 | tf_op jit(solution)/shard_map/all_to_all | solution.py:191
  51.9 0.0 slice-start
  51.9 2.2 slice-done
  54.0 4.7 %copy.77 = bf16[2,2,16,256,128]{4,2,0,1,3:T(8,128)(2,1)} copy(bf16[2,2,16,256,128]{4,3,2,0,1:T(8,128)(2,1)S(1)} %slice-done) | data formatting | bytes 8388608 | tf_op jit(solution)/shard_map/slice | solution.py:190
  58.7 0.0 copy-start.4
  58.7 0.0 copy-start.2
  58.7 0.0 copy-start.1
  58.7 0.0 copy-start.3
  58.7 34.2 %all-to-all-done.1 = bf16[1,2,16,256,128]{4,2,0,1,3:T(8,128)(2,1)S(1)} async-done(((bf16[1,2,16,256,128]{4,2,0,1,3:T(8,128)(2,1)}), bf16[1,2,16,256,128]{4,2,0,1,3:T(8,128)(2,1)S(1)}, u32[]{:S(2)}, u32[]{:S(2)}) %all-to-all-start.1) | async-done | bytes 2097184 | tf_op jit(solution)/shard_map/all_to_all | solution.py:191
  93.0 11.3 %all-to-all-start = ((bf16[2,2,16,256,128]{4,2,0,1,3:T(8,128)(2,1)}), bf16[2,2,16,256,128]{4,2,0,1,3:T(8,128)(2,1)}, u32[]{:S(2)}, u32[]{:S(2)}) async-start(bf16[2,2,16,256,128]{4,2,0,1,3:T(8,128)(2,1)} %copy.77), calls=%async_computation | async-start | bytes 8388608 | tf_op jit(solution)/shard_map/all_to_all | solution.py:190
  104.2 0.0 copy-done.4
  104.3 0.1 iota_add_fusion
  104.3 0.1 broadcast_add_fusion
  104.4 0.0 copy-done.2
  104.4 0.2 fusion.40
  104.7 0.0 copy-done.1
  104.7 0.0 copy-done.3
  104.7 3.8 %copy.134 = bf16[1,2,16,16,16,128]{5,3,2,4,1,0:T(8,128)(2,1)} copy(bf16[1,2,16,16,16,128]{5,2,1,4,3,0:T(8,128)(2,1)S(1)} %bitcast.131) | data formatting | bytes 4194304 | tf_op jit(solution)/shard_map/all_to_all | solution.py:191
  108.5 2.8 reshape.349
  111.4 70.5 %all-to-all-done = bf16[2,2,16,256,128]{4,2,0,1,3:T(8,128)(2,1)} async-done(((bf16[2,2,16,256,128]{4,2,0,1,3:T(8,128)(2,1)}), bf16[2,2,16,256,128]{4,2,0,1,3:T(8,128)(2,1)}, u32[]{:S(2)}, u32[]{:S(2)}) %all-to-all-start) | async-done | bytes 4194336 | tf_op jit(solution)/shard_map/all_to_all | solution.py:190
  181.9 9.0 %copy.133 = bf16[2,2,16,16,16,128]{5,3,2,4,1,0:T(8,128)(2,1)} copy(bf16[2,2,16,16,16,128]{5,2,0,1,4,3:T(8,128)(2,1)} %bitcast.23) | data formatting | bytes 8388608 | tf_op jit(solution)/shard_map/all_to_all | solution.py:190
  190.9 7.3 %reshape.348 = bf16[2,2,16,8,2,2048]{5,2,4,3,1,0:T(8,128)(2,1)} reshape(bf16[2,2,16,16,16,128]{5,4,2,3,1,0:T(8,128)(2,1)} %bitcast.130) | data formatting | bytes 8388608 | tf_op jit(solution)/shard_map/reshape | solution.py:126
  198.2 3.5 %fusion.5 = bf16[2,64,8,2048,1,1,1]{3,1,6,5,2,0,4:T(8,128)(2,1)S(1)} fusion(bf16[1,64,2,2,16,2]{1,4,2,3,0,5:T(8,128)(2,1)S(1)} %get-tuple-element.15, bf16[1,64,2,2,16,2]{1,4,2,3,0,5:T(8,128)(2,1)S(1)} %get-tuple-element.14, bf16[2,2,16,8,2,2048]{5,2,4,3,1,0:T(8,128)(2,1)} %reshape.348), kind=kOutput, calls=%fused_computation.11 | convolution fusion | flops 536936448 | bytes 8421376 | tf_op jit(solution)/shard_map/tcarbm,dktcab->rdkm/dot_general | solution.py:147
  201.7 2.1 fusion.7
  203.8 2.1 fusion.14
  206.0 0.1 copy.87
  206.1 0.1 copy.88
  206.2 0.8 maximum_bitcast_fusion.4.b_ref
  206.9 0.2 fusion.60
  207.1 1.0 maximum_maximum_fusion.a_ref
  208.1 50.4 %shard_map.55 = f32[8,32,128]{2,1,0:T(8,128)} custom-call(f32[8,128,128]{2,1,0:T(8,128)} %maximum_maximum_fusion.a_ref, f32[8,32,128]{2,1,0:T(8,128)} %maximum_bitcast_fusion.4.b_ref), custom_call_target="tpu_custom_call" | custom-call | tf_op jit(solution)/shard_map/pallas_call | solution.py:74
  258.6 1.1 reshape.350
  259.7 0.1 copy.90
  259.8 27.4 %all_to_all.48 = f32[64,1,2,256]{3,2,1,0:T(2,128)S(1)} all-to-all(f32[64,1,2,256]{3,2,1,0:T(2,128)S(1)} %copy.90), channel_id=1, replica_groups=mesh['cells'=2,'fh'=16] {'fh'}, dimensions={0} | all-to-all | bytes 262144 | tf_op jit(solution)/shard_map/all_to_all | solution.py:196
  287.2 0.7 copy.109
  (11 shorter events, 0.2 us)
Async XLA Ops:
  38.9 2.7 copy-start
  44.5 48.5 %all-to-all-start.1 = ((bf16[1,2,16,256,128]{4,2,0,1,3:T(8,128)(2,1)}), bf16[1,2,16,256,128]{4,2,0,1,3:T(8,128)(2,1)S(1)}, u32[]{:S(2)}, u32[]{:S(2)}) async-start(bf16[1,2,16,256,128]{4,2,0,1,3:T(8,128)(2,1)} %copy.84), calls=%async_computation.1 | async-start | bytes 4194304 | tf_op jit(solution)/shard_map/all_to_all | solution.py:191
  51.9 2.2 slice-start
  58.7 45.5 %copy-start.4 = (s32[64]{0:T(128)S(1)}, s32[64]{0:T(128)}, u32[]{:S(2)}) copy-start(s32[64]{0:T(128)} %param.7) | copy-start | bytes 772
  58.7 45.7 %copy-start.2 = (s32[64]{0:T(128)S(1)}, s32[64]{0:T(128)}, u32[]{:S(2)}) copy-start(s32[64]{0:T(128)} %param.6) | copy-start | bytes 772
  58.7 45.9 %copy-start.1 = (s32[8,64]{1,0:T(8,128)S(1)}, s32[8,64]{1,0:T(8,128)}, u32[]{:S(2)}) copy-start(s32[8,64]{1,0:T(8,128)} %param.8) | copy-start | bytes 6148
  58.7 45.9 %copy-start.3 = (f32[64]{0:T(128)S(1)}, f32[64]{0:T(128)}, u32[]{:S(2)}) copy-start(f32[64]{0:T(128)} %param.9) | copy-start | bytes 772
  93.0 88.9 %all-to-all-start = ((bf16[2,2,16,256,128]{4,2,0,1,3:T(8,128)(2,1)}), bf16[2,2,16,256,128]{4,2,0,1,3:T(8,128)(2,1)}, u32[]{:S(2)}, u32[]{:S(2)}) async-start(bf16[2,2,16,256,128]{4,2,0,1,3:T(8,128)(2,1)} %copy.77), calls=%async_computation | async-start | bytes 8388608 | tf_op jit(solution)/shard_map/all_to_all | solution.py:190

commit v2 on v1

--- a/solution.py
+++ b/solution.py
@@ -1,3 +1,4 @@
+import functools
 import math
 
 import jax
@@ -184,13 +185,50 @@
     return solved.reshape(user_count, solved.shape[1], 2, -1)
 
 
-def on_device(received_time_rows, pilots, active_users, allocation, loading):
+def packed_terms(pilot_part, data_part, code_rows):
+    channel = jnp.einsum(
+        "tcarbm,dktcab->rdkm", pilot_part, code_rows, preferred_element_type=jnp.float32
+    ).astype(jnp.bfloat16)
+    gram = jnp.einsum("rdkm,relm->rdkel", channel, channel, preferred_element_type=jnp.float32)
+    gram_real = gram[:, 0, :, 0] + gram[:, 1, :, 1]
+    gram_imag = gram[:, 0, :, 1] - gram[:, 1, :, 0]
+    user_count = gram_real.shape[1]
+    row = lax.broadcasted_iota(jnp.int32, (user_count, user_count), 0)
+    col = lax.broadcasted_iota(jnp.int32, (user_count, user_count), 1)
+    packed = jnp.where(row <= col, gram_real, gram_imag)
+    matched = jnp.einsum(
+        "rdkm,tcarbm->rdktcab", channel, data_part, preferred_element_type=jnp.float32
+    )
+    matched_real = matched[:, 0, :, :, 0] + matched[:, 1, :, :, 1]
+    matched_imag = matched[:, 0, :, :, 1] - matched[:, 1, :, :, 0]
+    blocks = matched_real.shape[0]
+    matched_real = matched_real.reshape(blocks, user_count, -1)
+    matched_imag = matched_imag.reshape(blocks, user_count, -1)
+    return jnp.concatenate([packed, matched_real, matched_imag], 2)
+
+
+def unpack_terms(terms, user_count):
+    packed = terms[:, :, :user_count]
+    mirrored = jnp.swapaxes(packed, 1, 2)
+    row = lax.broadcasted_iota(jnp.int32, (user_count, user_count), 0)
+    col = lax.broadcasted_iota(jnp.int32, (user_count, user_count), 1)
+    gram_real = jnp.where(row <= col, packed, mirrored)
+    gram_imag = jnp.where(row > col, packed, jnp.where(row < col, -mirrored, 0.0))
+    width = (terms.shape[2] - user_count) // 2
+    matched_real = terms[:, :, user_count:user_count + width]
+    matched_imag = terms[:, :, user_count + width:]
+    left_half = jnp.stack([gram_real, gram_imag], 1)
+    right_half = jnp.stack([matched_real, matched_imag], 1)
+    return jnp.concatenate([left_half, right_half], 3)
+
+
+def on_device(received_time_rows, pilots, active_users, allocation, loading, fh_size):
     spectrum = spectra(received_time_rows)
     code_rows = code_table(pilots)
-    pilot_part = lax.all_to_all(spectrum[:PSYM], "fh", split_axis=3, concat_axis=4, tiled=True)
-    data_part = lax.all_to_all(spectrum[PSYM:], "fh", split_axis=3, concat_axis=4, tiled=True)
-    antenna_total = pilot_part.shape[4]
-    packed_layout = block_terms(split_blocks(pilot_part), split_blocks(data_part), code_rows)
+    terms = packed_terms(split_blocks(spectrum[:PSYM]), split_blocks(spectrum[PSYM:]), code_rows)
+    terms = lax.psum_scatter(terms, "fh", scatter_dimension=0, tiled=True)
+    antenna_total = received_time_rows.shape[0] * fh_size
+    packed_layout = unpack_terms(terms, pilots.shape[0])
     served_users = active_users.astype(jnp.float32)[None, :] * allocation.astype(jnp.float32)
     result = mmse_equalizer(packed_layout, served_users, loading, antenna_total)
     return lax.all_to_all(result, "fh", split_axis=0, concat_axis=3, tiled=True)
@@ -198,7 +236,7 @@
 
 def solution(mesh):
     return jax.shard_map(
-        on_device,
+        functools.partial(on_device, fh_size=mesh.shape["fh"]),
         mesh=mesh,
         in_specs=(
             P(("cells", "fh"), None, None, None),

time: 289 us -> 268 us (0.927)
  local copies, waits for them, and re-layouts: 57.4 us -> 30 us
  starting transfers between devices: 18.6 us -> 0.01 us
  blocking collectives: 27.4 us -> 12.2 us
  between operations: 0.25 us -> 13.6 us
  other arithmetic: 10.2 us -> 23.1 us
  matrix products: 18.9 us -> 31.4 us
    reduce_scatter x0 -> x1, waiting for transfers between devices: none -> 107 us  [on_device(): terms = lax.psum_scatter(terms, 'fh', scatter_dimension=0, tiled=True)]
    all_to_all x2 -> x0, waiting for transfers between devices: 105 us -> none  [the longest x1 70.5 us: on_device(): lax.all_to_all(spectrum[:PSYM], 'fh', split_axis=3, concat_axis=4, tiled=...]
    all_to_all x2 -> x0, starting transfers between devices: 18.6 us -> none  [the longest x1 11.3 us: on_device(): lax.all_to_all(spectrum[:PSYM], 'fh', split_axis=3, concat_axis=4, tiled=...]
    all_to_all x1, blocking collectives: 27.4 us -> 12.2 us  [on_device(): return lax.all_to_all(result, 'fh', split_axis=0, concat_axis=3, tiled=True)]
    all_to_all x2 -> x0, local copies, waits for them, and re-layouts: 12.9 us -> none  [the longest x1 9.04 us: on_device(): lax.all_to_all(spectrum[:PSYM], 'fh', split_axis=3, concat_axis=4, tiled=...]
    dot_general x3, matrix products: 7.72 us -> 20.1 us  [the longest x1 10.3 us: packed_terms(): jnp.einsum('rdkm,relm->rdkel', channel, channel, preferred_element_type=j...]
    select_n x0 -> x1, other arithmetic: none -> 7.89 us  [packed_terms(): packed = jnp.where(row <= col, gram_real, gram_imag)]
    reshape x1 -> x0, local copies, waits for them, and re-layouts: 7.27 us -> none  [split_blocks(): spectrum.reshape(shape_in[0], 2, FA, shape_in[3] // width_b, width_b, sha...]
  transfers between devices with their start and end apart: 2 -> 1, of which waited for: 2 -> 1; matrix products, arithmetic and copies ran while one was open for 4% -> 0% of each run, Pallas kernels for 0% -> 0%
where the time goes in v2:
time: 268 us; the launch traced here: 267 us
  waiting for transfers between devices  107 us (40%)
  Pallas kernels  50.4 us (19%)
  matrix products  31.4 us (12%)
  local copies, waits for them, and re-layouts  30 us (11%)
  other arithmetic  23.1 us (9%)
  between operations  13.6 us (5%)
  blocking collectives  12.2 us (5%)
    reduce_scatter x1, waiting for transfers between devices, on_device(): terms = lax.psum_scatter(terms, 'fh', scatter_dimension=0, tiled=True)  107 us
    pallas_call x1, Pallas kernels, spd_solve_t(): pl.pallas_call(_solve_body, out_shape=jax.ShapeDtypeStruct(rhs_t.shape, j...  50.4 us
    all_to_all x1, blocking collectives, on_device(): return lax.all_to_all(result, 'fh', split_axis=0, concat_axis=3, tiled=True)  12.2 us
    reshape x1, local copies, waits for them, and re-layouts, spectra(): shaped = samples.reshape(antennas_here, symbol_count, 2, FA, FB)  10.8 us
    dot_general x1, matrix products, packed_terms(): jnp.einsum('rdkm,relm->rdkel', channel, channel, preferred_element_type=j...  10.3 us
    another operation x1, local copies, waits for them, and re-layouts, spectra(): section_one = jnp.stack([real_part, imag_part], 1).astype(jnp.bfloat16)  9.14 us
    select_n x1, other arithmetic, packed_terms(): packed = jnp.where(row <= col, gram_real, gram_imag)  7.89 us
    dot_general x1, matrix products, spectra(): jnp.einsum('sckma,cmdj->sdkja', section_one, dft_table(FB), preferred_ele...  6.68 us
  transfers between devices with their start and end apart: 1, of which 1 were waited for; matrix products, arithmetic and copies ran while one was open for 0% of the time, Pallas kernels for 0%

profile of v2, /device:TPU:0, one launch (start us, length us, event | category | flops | bytes accessed | tf_op | source)
XLA Modules:
  0.0 267.4 jit_solution(706103352680459398)
XLA Ops:
  6.5 0.0 reduce-scatter.2.cloned.1.call-start
  6.5 0.1 negate_convert_fusion.2
  6.6 0.1 fusion.59
  6.7 0.1 sine_multiply_fusion.1
  6.8 1.1 negate_convert_fusion
  7.9 1.0 fusion.36
  8.9 10.8 %reshape.353 = bf16[128,3,2,16,256,1]{4,3,2,1,0,5:T(8,128)(2,1)} reshape(bf16[128,3,2,4096]{3,2,1,0:T(2,128)(2,1)} %param.5) | data formatting | bytes 12582912 | tf_op jit(solution)/shard_map/reshape | solution.py:108
  19.7 4.6 %convolution_bitcast_fusion = f32[3,2,16,256,128]{3,2,0,4,1:T(8,128)S(1)} fusion(bf16[128,3,2,16,256,1]{4,3,2,1,0,5:T(8,128)(2,1)} %reshape.353, bf16[1,16,2,16]{1,3,0,2:T(8,128)(2,1)S(1)} %get-tuple-element.19, bf16[1,16,2,16]{1,3,0,2:T(8,128)(2,1)S(1)} %get-tuple-element.18), kind=kOutput, calls=%fused_computation.9 | convolution fusion | flops 201330688 | bytes 18876416 | tf_op jit(solution)/shard_map/ascnm,cndk->sdkma/dot_general | solution.py:109
  24.3 2.2 add_convert_fusion
  26.5 3.2 %pad_maximum_fusion.1 = bf16[3,2,16,256,128]{3,2,0,4,1:T(8,128)(2,1)} fusion(bf16[3,1,16,256,128]{3,2,0,4,1:T(8,128)(2,1)S(1)} %get-tuple-element.8, bf16[3,1,16,256,128]{3,2,0,4,1:T(8,128)(2,1)S(1)} %get-tuple-element.7), kind=kLoop, calls=%fused_computation.4 | loop fusion | flops 3145728 | bytes 12582912 | tf_op jit(solution)/shard_map/stack | solution.py:117
  29.7 9.1 %copy.61 = bf16[3,2,16,256,128]{4,3,1,2,0:T(8,128)(2,1)} copy(bf16[3,2,16,256,128]{3,2,0,4,1:T(8,128)(2,1)} %pad_maximum_fusion.1) | data formatting | bytes 12582912 | tf_op jit(solution)/shard_map/stack | solution.py:117
  38.9 6.7 %fusion = bf16[3,2,16,256,128]{4,3,2,0,1:T(8,128)(2,1)S(1)} fusion(bf16[3,2,16,256,128]{4,3,1,2,0:T(8,128)(2,1)} %copy.61, bf16[1,256,2,256]{1,3,0,2:T(8,128)(2,1)S(1)} %get-tuple-element.15, bf16[1,256,2,256]{1,3,0,2:T(8,128)(2,1)S(1)} %get-tuple-element.14), kind=kOutput, calls=%fused_computation.3 | convolution fusion | flops 3225419776 | bytes 13107200 | tf_op jit(solution)/shard_map/sckma,cmdj->sdkja/dot_general | solution.py:118
  45.6 0.0 copy-start
  45.6 0.5 slice.64
  46.1 2.2 copy-done
  48.3 0.0 copy-start.3
  48.3 0.1 iota_add_fusion
  48.4 0.1 broadcast_add_fusion
  48.4 0.5 copy-done.3
  48.9 0.2 fusion.43
  49.2 5.7 %fusion.11 = bf16[2,64,128,128,1,1,1]{3,1,6,5,0,2,4:T(8,128)(2,1)S(1)} fusion(bf16[2,2,16,128,2,128,1]{5,4,3,2,0,1,6:T(2,128)(2,1)S(1)} %bitcast.122, bf16[1,64,2,2,16,2]{1,4,2,3,0,5:T(8,128)(2,1)S(1)} %get-tuple-element.17, bf16[1,64,2,2,16,2]{1,4,2,3,0,5:T(8,128)(2,1)S(1)} %get-tuple-element.16), kind=kOutput, calls=%fused_computation.20 | convolution fusion | flops 536936448 | bytes 8421376 | tf_op jit(solution)/shard_map/tcarbm,dktcab->rdkm/dot_general | solution.py:189
  54.9 0.0 slice-start
  54.9 10.3 %fusion.6 = f32[128,2,64,2,64]{2,4,0,3,1:T(8,128)} fusion(bf16[2,64,128,128,1,1,1]{3,1,6,5,0,2,4:T(8,128)(2,1)S(1)} %fusion.11), kind=kOutput, calls=%fused_computation.15 | convolution fusion | flops 536870912 | bytes 12582912 | tf_op jit(solution)/shard_map/rdkm,relm->rdkel/dot_general | solution.py:192
  65.1 0.0 slice-done
  65.1 4.1 %fusion.15 = f32[128,2,64,1,2,16,2]{2,5,6,4,1,0,3:T(8,128)S(1)} fusion(bf16[2,16,128,2,128,1]{4,3,2,1,0,5:T(2,128)(2,1)S(1)} %bitcast.123, bf16[2,64,128,128,1,1,1]{3,1,6,5,0,2,4:T(8,128)(2,1)S(1)} %fusion.11), kind=kOutput, calls=%fused_computation.22 | convolution fusion | flops 268435456 | bytes 10485760 | tf_op jit(solution)/shard_map/rdkm,tcarbm->rdktcab/dot_general | solution.py:199
  69.3 1.2 slice_add_fusion.1
  70.5 1.1 copy.71
  71.6 1.1 copy.72
  72.7 7.9 %fusion.4 = f32[128,64,64]{1,2,0:T(8,128)S(1)} fusion(f32[128,2,64,2,64]{2,4,0,3,1:T(8,128)} %fusion.6, pred[64,64]{0,1:T(8,128)(4,1)S(1)} %iota_compare_fusion.3), kind=kLoop, calls=%fused_computation.12 | loop fusion | flops 1572864 | bytes 10489856 | tf_op jit(solution)/shard_map/jit(_where)/select_n | solution.py:198
  80.6 3.6 %pad_maximum_fusion = f32[128,64,128]{1,2,0:T(8,128)} fusion(f32[128,64,32]{1,2,0:T(8,128)S(1)} %bitcast.125, f32[128,64,32]{1,2,0:T(8,128)S(1)} %bitcast.124, f32[128,64,64]{1,2,0:T(8,128)S(1)} %fusion.4), kind=kLoop, calls=%fused_computation.1 | loop fusion | flops 2097152 | bytes 8388608 | tf_op jit(solution)/shard_map/concatenate | solution.py:207
  84.2 0.0 copy-start.5
  84.2 0.0 copy-start.2
  84.2 0.0 copy-start.4
  84.2 0.0 reduce-scatter.2.cloned.1.call-update
  84.2 0.6 copy-done.5
  84.9 0.0 copy-done.2
  84.9 0.0 copy-done.4
  84.9 0.1 fusion.42
  85.0 106.7 %reduce-scatter.2.cloned.1.call-done = f32[8,64,128]{1,2,0:T(8,128)} async-done(((f32[128,64,128]{1,2,0:T(8,128)}), f32[8,64,128]{1,2,0:T(8,128)}) %reduce-scatter.2.cloned.1.call-update) | async-done | bytes 262160 | tf_op jit(solution)/shard_map/reduce_scatter | solution.py:229
  191.7 0.0 copy-start.1
  191.7 1.0 slice.74
  192.7 0.1 copy.73
  192.9 1.1 fusion.63
  194.0 0.2 maximum_maximum_fusion
  194.2 1.0 copy.74.a_ref
  195.2 0.0 copy-done.1
  195.2 0.8 maximum_bitcast_fusion.4.b_ref
  196.0 50.4 %shard_map.55 = f32[8,32,128]{2,1,0:T(8,128)} custom-call(f32[8,128,128]{2,1,0:T(8,128)} %copy.74.a_ref, f32[8,32,128]{2,1,0:T(8,128)} %maximum_bitcast_fusion.4.b_ref), custom_call_target="tpu_custom_call" | custom-call | tf_op jit(solution)/shard_map/pallas_call | solution.py:75
  246.4 1.1 reshape.350
  247.5 0.1 copy.76
  247.7 12.2 %all_to_all.18 = f32[64,1,2,256]{3,2,1,0:T(2,128)S(1)} all-to-all(f32[64,1,2,256]{3,2,1,0:T(2,128)S(1)} %copy.76), channel_id=1, replica_groups=mesh['cells'=2,'fh'=16] {'fh'}, dimensions={0} | all-to-all | bytes 262144 | tf_op jit(solution)/shard_map/all_to_all | solution.py:234
  259.9 0.7 copy.100
  (11 shorter events, 0.1 us)
Async XLA Ops:
  6.5 185.1 %reduce-scatter.2.cloned.1.call-start = ((), (), s32[]{:S(2)}) async-start(), calls=%async_computation.2 | async-start | bytes 8912896 | tf_op jit(solution)/shard_map/reduce_scatter | solution.py:229
  45.6 2.7 copy-start
  48.3 0.7 copy-start.3
  54.9 10.3 %slice-start = ((bf16[3,2,16,256,128]{4,3,2,0,1:T(8,128)(2,1)}), bf16[1,2,16,256,128]{4,3,2,0,1:T(8,128)(2,1)S(1)}, s32[]{:S(2)}) async-start(bf16[3,2,16,256,128]{4,3,2,0,1:T(8,128)(2,1)} %copy-done), calls=%async_computation.3 | async-start | bytes 4194304 | tf_op jit(solution)/shard_map/slice | solution.py:228
  84.2 0.7 copy-start.5
  84.2 0.7 copy-start.2
  84.2 0.7 copy-start.4
  191.7 3.5 %copy-start.1 = (f32[8,64,128]{1,2,0:T(8,128)S(1)}, f32[8,64,128]{1,2,0:T(8,128)}, u32[]{:S(2)}) copy-start(f32[8,64,128]{1,2,0:T(8,128)} %reduce-scatter.2.cloned.1.call-done) | copy-start | bytes 786436
Sparse Core Ops, SparseCore 0:
  84.3 107.2 reduce-scatter.1

commit v3 on v2

--- a/solution.py
+++ b/solution.py
@@ -222,11 +222,26 @@
     return jnp.concatenate([left_half, right_half], 3)
 
 
+def halving_reduce_scatter(terms, fh_size):
+    position = lax.axis_index("fh")
+    parts = terms.reshape(fh_size, -1, *terms.shape[1:])
+    bit = 0
+    while (1 << bit) < fh_size:
+        paired = parts.reshape(parts.shape[0] // 2, 2, *parts.shape[1:])
+        mine = (position >> bit) & 1
+        keep = lax.dynamic_index_in_dim(paired, mine, axis=1, keepdims=False)
+        send = lax.dynamic_index_in_dim(paired, 1 - mine, axis=1, keepdims=False)
+        pairs = [(i, i ^ (1 << bit)) for i in range(fh_size)]
+        parts = keep + lax.ppermute(send, "fh", perm=pairs)
+        bit += 1
+    return parts.reshape(-1, *terms.shape[1:])
+
+
 def on_device(received_time_rows, pilots, active_users, allocation, loading, fh_size):
     spectrum = spectra(received_time_rows)
     code_rows = code_table(pilots)
     terms = packed_terms(split_blocks(spectrum[:PSYM]), split_blocks(spectrum[PSYM:]), code_rows)
-    terms = lax.psum_scatter(terms, "fh", scatter_dimension=0, tiled=True)
+    terms = halving_reduce_scatter(terms, fh_size)
     antenna_total = received_time_rows.shape[0] * fh_size
     packed_layout = unpack_terms(terms, pilots.shape[0])
     served_users = active_users.astype(jnp.float32)[None, :] * allocation.astype(jnp.float32)

time: 268 us -> 245 us (0.914)
  waiting for transfers between devices: 107 us -> 60.9 us
  between operations: 13.6 us -> 0.35 us
  local copies, waits for them, and re-layouts: 30 us -> 41.9 us
  other arithmetic: 23.1 us -> 34.8 us
  starting transfers between devices: 0.01 us -> 7.88 us
  matrix products: 31.4 us -> 34.8 us
    reduce_scatter x1 -> x0, waiting for transfers between devices: 107 us -> none  [on_device(): terms = lax.psum_scatter(terms, 'fh', scatter_dimension=0, tiled=True)]
    ppermute x0 -> x4, waiting for transfers between devices: none -> 60.9 us  [halving_reduce_scatter(): parts = keep + lax.ppermute(send, 'fh', perm=pairs)]
    sub x0 -> x1, other arithmetic: none -> 12.1 us  [packed_terms(): gram_imag = gram[:, 0, :, 1] - gram[:, 1, :, 0]]
    ppermute x0 -> x4, starting transfers between devices: none -> 7.88 us  [halving_reduce_scatter(): parts = keep + lax.ppermute(send, 'fh', perm=pairs)]
    add x1 -> x2, local copies, waits for them, and re-layouts: 1.08 us -> 5.65 us  [packed_terms(): matched_real = matched[:, 0, :, :, 0] + matched[:, 1, :, :, 1]]
    add x0 -> x3, other arithmetic: none -> 4.1 us  [halving_reduce_scatter(): parts = keep + lax.ppermute(send, 'fh', perm=pairs)]
    dot_general x1, matrix products: 10.3 us -> 13.8 us  [packed_terms(): jnp.einsum('rdkm,relm->rdkel', channel, channel, preferred_element_type=j...]
    select_n x1, other arithmetic: 7.89 us -> 4.59 us  [packed_terms(): packed = jnp.where(row <= col, gram_real, gram_imag)]
  transfers between devices with their start and end apart: 1 -> 4, of which waited for: 1 -> 4; matrix products, arithmetic and copies ran while one was open for 0% -> 0% of each run, Pallas kernels for 0% -> 0%
where the time goes in v3:
time: 245 us; the launch traced here: 244 us
  waiting for transfers between devices  60.9 us (25%)
  Pallas kernels  50.4 us (21%)
  local copies, waits for them, and re-layouts  41.9 us (17%)
  other arithmetic  34.8 us (14%)
  matrix products  34.8 us (14%)
  blocking collectives  13.1 us (5%)
  starting transfers between devices  7.88 us (3%)
    ppermute x4, waiting for transfers between devices, halving_reduce_scatter(): parts = keep + lax.ppermute(send, 'fh', perm=pairs)  60.9 us
    pallas_call x1, Pallas kernels, spd_solve_t(): pl.pallas_call(_solve_body, out_shape=jax.ShapeDtypeStruct(rhs_t.shape, j...  50.4 us
    dot_general x1, matrix products, packed_terms(): jnp.einsum('rdkm,relm->rdkel', channel, channel, preferred_element_type=j...  13.8 us
    all_to_all x1, blocking collectives, on_device(): return lax.all_to_all(result, 'fh', split_axis=0, concat_axis=3, tiled=True)  13.1 us
    sub x1, other arithmetic, packed_terms(): gram_imag = gram[:, 0, :, 1] - gram[:, 1, :, 0]  12.1 us
    reshape x1, local copies, waits for them, and re-layouts, spectra(): shaped = samples.reshape(antennas_here, symbol_count, 2, FA, FB)  10.9 us
    another operation x1, local copies, waits for them, and re-layouts, spectra(): section_one = jnp.stack([real_part, imag_part], 1).astype(jnp.bfloat16)  9.11 us
    ppermute x4, starting transfers between devices, halving_reduce_scatter(): parts = keep + lax.ppermute(send, 'fh', perm=pairs)  7.88 us
  transfers between devices with their start and end apart: 4, of which 4 were waited for; matrix products, arithmetic and copies ran while one was open for 0% of the time, Pallas kernels for 0%

profile of v3, /device:TPU:0, one launch (start us, length us, event | category | flops | bytes accessed | tf_op | source)
XLA Modules:
  0.0 244.2 jit_solution(18429641957044498812)
XLA Ops:
  0.0 0.1 negate_convert_fusion.2
  0.1 0.1 fusion.57
  0.1 0.1 sine_multiply_fusion.1
  0.2 1.1 negate_convert_fusion
  1.3 1.0 fusion.34
  2.3 10.9 %reshape.381 = bf16[128,3,2,16,256,1]{4,3,2,1,0,5:T(8,128)(2,1)} reshape(bf16[128,3,2,4096]{3,2,1,0:T(2,128)(2,1)} %param.5) | data formatting | bytes 12582912 | tf_op jit(solution)/shard_map/reshape | solution.py:108
  13.2 4.6 %convolution_bitcast_fusion = f32[3,2,16,256,128]{3,2,0,4,1:T(8,128)S(1)} fusion(bf16[128,3,2,16,256,1]{4,3,2,1,0,5:T(8,128)(2,1)} %reshape.381, bf16[1,16,2,16]{1,3,0,2:T(8,128)(2,1)S(1)} %get-tuple-element.25, bf16[1,16,2,16]{1,3,0,2:T(8,128)(2,1)S(1)} %get-tuple-element.24), kind=kOutput, calls=%fused_computation.8 | convolution fusion | flops 201330688 | bytes 18876416 | tf_op jit(solution)/shard_map/ascnm,cndk->sdkma/dot_general | solution.py:109
  17.8 2.2 add_convert_fusion
  20.0 3.2 %pad_maximum_fusion = bf16[3,2,16,256,128]{3,2,0,4,1:T(8,128)(2,1)} fusion(bf16[3,1,16,256,128]{3,2,0,4,1:T(8,128)(2,1)S(1)} %get-tuple-element.10, bf16[3,1,16,256,128]{3,2,0,4,1:T(8,128)(2,1)S(1)} %get-tuple-element.9), kind=kLoop, calls=%fused_computation.3 | loop fusion | flops 3145728 | bytes 12582912 | tf_op jit(solution)/shard_map/stack | solution.py:117
  23.2 9.1 %copy.59 = bf16[3,2,16,256,128]{4,3,1,2,0:T(8,128)(2,1)} copy(bf16[3,2,16,256,128]{3,2,0,4,1:T(8,128)(2,1)} %pad_maximum_fusion) | data formatting | bytes 12582912 | tf_op jit(solution)/shard_map/stack | solution.py:117
  32.4 6.6 %fusion = bf16[3,2,16,256,128]{4,3,2,0,1:T(8,128)(2,1)S(1)} fusion(bf16[3,2,16,256,128]{4,3,1,2,0:T(8,128)(2,1)} %copy.59, bf16[1,256,2,256]{1,3,0,2:T(8,128)(2,1)S(1)} %get-tuple-element.21, bf16[1,256,2,256]{1,3,0,2:T(8,128)(2,1)S(1)} %get-tuple-element.20), kind=kOutput, calls=%fused_computation.2 | convolution fusion | flops 3225419776 | bytes 13107200 | tf_op jit(solution)/shard_map/sckma,cmdj->sdkja/dot_general | solution.py:118
  39.0 0.3 slice.64
  39.3 2.4 copy-done.4
  41.7 0.1 iota_add_fusion
  41.7 0.1 broadcast_add_fusion
  41.8 0.5 copy-done.6
  42.3 0.2 fusion.41
  42.5 5.7 %fusion.8 = bf16[2,64,128,128,1,1,1]{3,1,6,5,0,2,4:T(8,128)(2,1)S(1)} fusion(bf16[2,2,16,128,2,128,1]{5,4,3,2,0,1,6:T(2,128)(2,1)S(1)} %bitcast.124, bf16[1,64,2,2,16,2]{1,4,2,3,0,5:T(8,128)(2,1)S(1)} %get-tuple-element.23, bf16[1,64,2,2,16,2]{1,4,2,3,0,5:T(8,128)(2,1)S(1)} %get-tuple-element.22), kind=kOutput, calls=%fused_computation.17 | convolution fusion | flops 536936448 | bytes 8421376 | tf_op jit(solution)/shard_map/tcarbm,dktcab->rdkm/dot_general | solution.py:189
  48.2 1.2 copy.116
  49.4 0.4 slice-done
  49.8 4.1 %fusion.12 = f32[128,2,64,1,2,16,2]{2,5,6,4,1,0,3:T(8,128)S(1)} fusion(bf16[128,2,64,128,1,1]{3,2,0,1,5,4:T(8,128)(2,1)S(1)} %bitcast.122, bf16[2,16,128,2,128,1]{4,3,2,1,0,5:T(2,128)(2,1)S(1)} %bitcast.129), kind=kOutput, calls=%fused_computation.19 | convolution fusion | flops 268435456 | bytes 10485760 | tf_op jit(solution)/shard_map/rdkm,tcarbm->rdktcab/dot_general | solution.py:199
  53.9 2.4 slice_add_fusion.1
  56.3 1.2 copy.66
  57.5 2.7 %copy.68 = f32[8,2,8,64,32]{4,3,2,1,0:T(8,128)} copy(f32[8,2,8,64,32]{3,2,1,0,4:T(8,128)S(1)} %bitcast.130) | data formatting | bytes 2097152 | tf_op jit(solution)/shard_map/sub | solution.py:203
  60.3 2.8 %copy.65 = f32[128,1,64,1,1,16,2]{2,0,6,5,4,3,1:T(8,128)S(1)} copy(f32[128,1,64,1,1,16,2]{2,5,6,4,1,0,3:T(8,128)} %get-tuple-element.11) | data formatting | bytes 2097152 | tf_op jit(solution)/shard_map/add | solution.py:202
  63.1 2.8 %copy.67 = f32[8,2,8,64,32]{4,3,2,1,0:T(8,128)} copy(f32[8,2,8,64,32]{3,2,1,0,4:T(8,128)S(1)} %bitcast.131) | data formatting | bytes 2097152 | tf_op jit(solution)/shard_map/add | solution.py:202
  65.9 13.8 %fusion.5 = f32[128,2,64,2,64]{4,2,3,1,0:T(8,128)} fusion(bf16[128,2,64,128,1]{3,2,0,1,4:T(8,128)(2,1)} %bitcast.123), kind=kOutput, calls=%fused_computation.14 | convolution fusion | flops 536870912 | bytes 12582912 | tf_op jit(solution)/shard_map/rdkm,relm->rdkel/dot_general | solution.py:192
  79.7 12.1 %slice_subtract_fusion = (f32[128,1,64,1,64]{4,2,3,1,0:T(8,128)}, f32[128,1,64,1,64]{4,2,3,1,0:T(8,128)}) fusion(f32[128,2,64,2,64]{4,2,3,1,0:T(8,128)} %fusion.5), kind=kLoop, calls=%fused_computation.9 | loop fusion | flops 1048576 | bytes 12582912 | tf_op jit(solution)/shard_map/sub | solution.py:194
  91.8 0.1 copy.55
  91.9 4.6 %broadcast_select_fusion = f32[8,2,8,64,64]{4,3,2,1,0:T(8,128)S(1)} fusion(f32[8,2,8,64,64]{4,3,2,1,0:T(8,128)} %bitcast.126, f32[8,2,8,64,64]{4,3,2,1,0:T(8,128)} %bitcast.125, pred[64,64]{1,0:T(8,128)(4,1)S(1)} %copy.55), kind=kLoop, calls=%fused_computation.25 | loop fusion | flops 524288 | bytes 6295552 | tf_op jit(solution)/shard_map/jit(_where)/select_n | solution.py:198
  96.5 0.0 copy-done.2
  96.5 1.3 copy-done.3
  97.8 2.2 pad_maximum_fusion.1
  100.1 1.9 copy-done.1
  102.0 0.2 dynamic-slice_bitcast_fusion
  102.2 0.5 collective-permute-start
  102.8 3.9 %collective-permute-done = f32[8,8,64,128]{3,2,1,0:T(8,128)} collective-permute-done((f32[8,8,64,128]{3,2,1,0:T(8,128)S(1)}, f32[8,8,64,128]{3,2,1,0:T(8,128)}, u32[]{:S(2)}, u32[]{:S(2)}) %collective-permute-start) | collective-permute-done | bytes 2097184 | tf_op jit(solution)/shard_map/ppermute | solution.py:235
  106.7 2.6 %bitcast_add_fusion = f32[8,8,64,128]{3,2,1,0:T(8,128)S(1)} fusion(f32[8,8,64,128]{3,2,1,0:T(8,128)} %collective-permute-done, f32[8,2,8,64,128]{4,3,2,1,0:T(8,128)} %copy-done.1, s32[]{:T(128)S(6)} %select_n.144), kind=kLoop, calls=%fused_computation.22 | loop fusion | flops 524288 | bytes 6291460 | tf_op jit(solution)/shard_map/add | solution.py:235
  109.3 0.0 copy-start.8
  109.3 0.1 dynamic-slice_bitcast_fusion.1
  109.4 3.0 %collective-permute-start.1 = (f32[4,8,64,128]{3,2,1,0:T(8,128)S(1)}, f32[4,8,64,128]{3,2,1,0:T(8,128)}, u32[]{:S(2)}, u32[]{:S(2)}) collective-permute-start(f32[4,8,64,128]{3,2,1,0:T(8,128)S(1)} %dynamic-slice_bitcast_fusion.1), channel_id=1, source_target_pairs={{0,2},{1,3},{2,0},{3,1},{4,6},{5,7},{6,4},{7,5},{8,10},{9,11},{10,... | collective-permute-start | bytes 3145736 | tf_op jit(solution)/shard_map/ppermute | solution.py:235
  112.4 23.6 %collective-permute-done.1 = f32[4,8,64,128]{3,2,1,0:T(8,128)} collective-permute-done((f32[4,8,64,128]{3,2,1,0:T(8,128)S(1)}, f32[4,8,64,128]{3,2,1,0:T(8,128)}, u32[]{:S(2)}, u32[]{:S(2)}) %collective-permute-start.1) | collective-permute-done | bytes 1048608 | tf_op jit(solution)/shard_map/ppermute | solution.py:235
  136.0 1.4 bitcast_add_fusion.2
  137.3 0.1 constant_dynamic-slice_fusion.1
  137.4 0.0 copy-start.7
  137.5 1.9 collective-permute-start.2
  139.3 0.3 copy.69
  139.7 11.3 %collective-permute-done.2 = f32[2,8,64,128]{3,2,1,0:T(8,128)S(1)} collective-permute-done((f32[2,8,64,128]{3,2,1,0:T(8,128)S(1)}, f32[2,8,64,128]{3,2,1,0:T(8,128)S(1)}, u32[]{:S(2)}, u32[]{:S(2)}) %collective-permute-start.2) | collective-permute-done | bytes 524320 | tf_op jit(solution)/shard_map/ppermute | solution.py:235
  151.0 0.3 copy.70
  151.3 0.1 bitcast_add_fusion.1
  151.5 2.6 %collective-permute-start.3 = (f32[1,8,64,128]{2,3,1,0:T(8,128)S(1)}, f32[1,8,64,128]{2,3,1,0:T(8,128)S(1)}, u32[]{:S(2)}, u32[]{:S(2)}) collective-permute-start(f32[1,8,64,128]{2,3,1,0:T(8,128)S(1)} %constant_dynamic-slice_fusion), channel_id=1, source_target_pairs={{0,8},{1,9},{2,10},{3,11},{4,12},{5,13},{6,14},{7,15},{8,0},{9,1},... | collective-permute-start | bytes 786440 | tf_op jit(solution)/shard_map/ppermute | solution.py:235
  154.1 0.1 fusion.40
  154.2 22.1 %collective-permute-done.3 = f32[1,8,64,128]{2,3,1,0:T(8,128)S(1)} collective-permute-done((f32[1,8,64,128]{2,3,1,0:T(8,128)S(1)}, f32[1,8,64,128]{2,3,1,0:T(8,128)S(1)}, u32[]{:S(2)}, u32[]{:S(2)}) %collective-permute-start.3) | collective-permute-done | bytes 262176 | tf_op jit(solution)/shard_map/ppermute | solution.py:235
  176.3 0.1 add_bitcast_fusion
  176.4 0.1 copy.71
  176.5 0.2 fusion.61
  176.7 0.2 maximum_maximum_fusion
  176.9 1.0 copy.72.a_ref
  177.9 0.8 maximum_bitcast_fusion.4.b_ref
  178.7 50.4 %shard_map.55 = f32[8,32,128]{2,1,0:T(8,128)} custom-call(f32[8,128,128]{2,1,0:T(8,128)} %copy.72.a_ref, f32[8,32,128]{2,1,0:T(8,128)} %maximum_bitcast_fusion.4.b_ref), custom_call_target="tpu_custom_call" | custom-call | tf_op jit(solution)/shard_map/pallas_call | solution.py:75
  229.1 1.1 reshape.378
  230.2 0.1 copy.74
  230.4 13.1 %all_to_all.18 = f32[64,1,2,256]{3,2,1,0:T(2,128)S(1)} all-to-all(f32[64,1,2,256]{3,2,1,0:T(2,128)S(1)} %copy.74), channel_id=1, replica_groups=mesh['cells'=2,'fh'=16] {'fh'}, dimensions={0} | all-to-all | bytes 262144 | tf_op jit(solution)/shard_map/all_to_all | solution.py:249
  243.5 0.7 copy.98
  (25 shorter events, 0.2 us)
Async XLA Ops:
  39.0 2.6 %copy-start.4 = (bf16[3,2,16,256,128]{4,3,2,0,1:T(8,128)(2,1)}, bf16[3,2,16,256,128]{4,3,2,0,1:T(8,128)(2,1)S(1)}, u32[]{:S(2)}) copy-start(bf16[3,2,16,256,128]{4,3,2,0,1:T(8,128)(2,1)S(1)} %fusion) | copy-start | bytes 18874372
  41.6 0.7 copy-start.6
  48.2 1.6 slice-start
  49.4 4.5 %copy-start = (bf16[2,64,128,128,1,1,1]{3,1,2,0,4,5,6:T(8,128)(2,1)}, bf16[2,64,128,128,1,1,1]{3,1,2,0,4,5,6:T(8,128)(2,1)S(1)}, u32[]{:S(2)}) copy-start(bf16[2,64,128,128,1,1,1]{3,1,2,0,4,5,6:T(8,128)(2,1)S(1)} %copy.116) | copy-start | bytes 12582916
  91.9 4.6 %copy-start.2 = (f32[8,2,8,64,32]{4,3,2,1,0:T(8,128)S(1)}, f32[8,2,8,64,32]{4,3,2,1,0:T(8,128)}, u32[]{:S(2)}) copy-start(f32[8,2,8,64,32]{4,3,2,1,0:T(8,128)} %copy.68) | copy-start | bytes 3145732
  91.9 5.9 %copy-start.3 = (f32[8,2,8,64,32]{4,3,2,1,0:T(8,128)S(1)}, f32[8,2,8,64,32]{4,3,2,1,0:T(8,128)}, u32[]{:S(2)}) copy-start(f32[8,2,8,64,32]{4,3,2,1,0:T(8,128)} %copy.67) | copy-start | bytes 3145732
  100.1 1.9 copy-start.1
  102.2 4.4 %collective-permute-start = (f32[8,8,64,128]{3,2,1,0:T(8,128)S(1)}, f32[8,8,64,128]{3,2,1,0:T(8,128)}, u32[]{:S(2)}, u32[]{:S(2)}) collective-permute-start(f32[8,8,64,128]{3,2,1,0:T(8,128)S(1)} %dynamic-slice_bitcast_fusion), channel_id=1, source_target_pairs={{0,1},{1,0},{2,3},{3,2},{4,5},{5,4},{6,7},{7,6},{8,9},{9,8},{10,11... | collective-permute-start | bytes 6291464 | tf_op jit(solution)/shard_map/ppermute | solution.py:235
  109.3 30.0 %copy-start.8 = (s32[64]{0:T(128)S(1)}, s32[64]{0:T(128)}, u32[]{:S(2)}) copy-start(s32[64]{0:T(128)} %param.7) | copy-start | bytes 772
  109.3 30.0 %copy-start.5 = (s32[8,64]{1,0:T(8,128)S(1)}, s32[8,64]{1,0:T(8,128)}, u32[]{:S(2)}) copy-start(s32[8,64]{1,0:T(8,128)} %param.8) | copy-start | bytes 6148
  109.4 26.5 %collective-permute-start.1 = (f32[4,8,64,128]{3,2,1,0:T(8,128)S(1)}, f32[4,8,64,128]{3,2,1,0:T(8,128)}, u32[]{:S(2)}, u32[]{:S(2)}) collective-permute-start(f32[4,8,64,128]{3,2,1,0:T(8,128)S(1)} %dynamic-slice_bitcast_fusion.1), channel_id=1, source_target_pairs={{0,2},{1,3},{2,0},{3,1},{4,6},{5,7},{6,4},{7,5},{8,10},{9,11},{10,... | collective-permute-start | bytes 3145736 | tf_op jit(solution)/shard_map/ppermute | solution.py:235
  137.4 16.6 %copy-start.7 = (f32[64]{0:T(128)S(1)}, f32[64]{0:T(128)}, u32[]{:S(2)}) copy-start(f32[64]{0:T(128)} %param.9) | copy-start | bytes 772
  137.5 13.5 %collective-permute-start.2 = (f32[2,8,64,128]{3,2,1,0:T(8,128)S(1)}, f32[2,8,64,128]{3,2,1,0:T(8,128)S(1)}, u32[]{:S(2)}, u32[]{:S(2)}) collective-permute-start(f32[2,8,64,128]{3,2,1,0:T(8,128)S(1)} %get-tuple-element.16), channel_id=1, source_target_pairs={{0,4},{1,5},{2,6},{3,7},{4,0},{5,1},{6,2},{7,3},{8,12},{9,13},{10,... | collective-permute-start | bytes 1572872 | tf_op jit(solution)/shard_map/ppermute | solution.py:235
  151.5 24.8 %collective-permute-start.3 = (f32[1,8,64,128]{2,3,1,0:T(8,128)S(1)}, f32[1,8,64,128]{2,3,1,0:T(8,128)S(1)}, u32[]{:S(2)}, u32[]{:S(2)}) collective-permute-start(f32[1,8,64,128]{2,3,1,0:T(8,128)S(1)} %constant_dynamic-slice_fusion), channel_id=1, source_target_pairs={{0,8},{1,9},{2,10},{3,11},{4,12},{5,13},{6,14},{7,15},{8,0},{9,1},... | collective-permute-start | bytes 786440 | tf_op jit(solution)/shard_map/ppermute | solution.py:235

commit v4 on v3

--- a/solution.py
+++ b/solution.py
@@ -185,26 +185,33 @@
     return solved.reshape(user_count, solved.shape[1], 2, -1)
 
 
-def packed_terms(pilot_part, data_part, code_rows):
-    channel = jnp.einsum(
+def channel_estimate(pilot_part, code_rows):
+    return jnp.einsum(
         "tcarbm,dktcab->rdkm", pilot_part, code_rows, preferred_element_type=jnp.float32
     ).astype(jnp.bfloat16)
+
+
+def gram_terms(channel):
     gram = jnp.einsum("rdkm,relm->rdkel", channel, channel, preferred_element_type=jnp.float32)
     gram_real = gram[:, 0, :, 0] + gram[:, 1, :, 1]
     gram_imag = gram[:, 0, :, 1] - gram[:, 1, :, 0]
     user_count = gram_real.shape[1]
     row = lax.broadcasted_iota(jnp.int32, (user_count, user_count), 0)
     col = lax.broadcasted_iota(jnp.int32, (user_count, user_count), 1)
-    packed = jnp.where(row <= col, gram_real, gram_imag)
+    return jnp.where(row <= col, gram_real, gram_imag)
+
+
+def matched_terms(channel, data_part):
     matched = jnp.einsum(
         "rdkm,tcarbm->rdktcab", channel, data_part, preferred_element_type=jnp.float32
     )
     matched_real = matched[:, 0, :, :, 0] + matched[:, 1, :, :, 1]
     matched_imag = matched[:, 0, :, :, 1] - matched[:, 1, :, :, 0]
     blocks = matched_real.shape[0]
+    user_count = matched_real.shape[1]
     matched_real = matched_real.reshape(blocks, user_count, -1)
     matched_imag = matched_imag.reshape(blocks, user_count, -1)
-    return jnp.concatenate([packed, matched_real, matched_imag], 2)
+    return jnp.concatenate([matched_real, matched_imag], 2)
 
 
 def unpack_terms(terms, user_count):
@@ -238,10 +245,12 @@
 
 
 def on_device(received_time_rows, pilots, active_users, allocation, loading, fh_size):
-    spectrum = spectra(received_time_rows)
     code_rows = code_table(pilots)
-    terms = packed_terms(split_blocks(spectrum[:PSYM]), split_blocks(spectrum[PSYM:]), code_rows)
-    terms = halving_reduce_scatter(terms, fh_size)
+    channel = channel_estimate(split_blocks(spectra(received_time_rows[:, :PSYM])), code_rows)
+    gram = halving_reduce_scatter(gram_terms(channel), fh_size)
+    matched = matched_terms(channel, split_blocks(spectra(received_time_rows[:, PSYM:])))
+    matched = halving_reduce_scatter(matched, fh_size)
+    terms = jnp.concatenate([gram, matched], 2)
     antenna_total = received_time_rows.shape[0] * fh_size
     packed_layout = unpack_terms(terms, pilots.shape[0])
     served_users = active_users.astype(jnp.float32)[None, :] * allocation.astype(jnp.float32)

time: 245 us -> 285 us (1.16)
  local copies, waits for them, and re-layouts: 41.9 us -> 61.2 us
  other arithmetic: 34.8 us -> 51.4 us
  starting transfers between devices: 7.88 us -> 11.8 us
  matrix products: 34.8 us -> 31.8 us
    slice x5 -> x2, local copies, waits for them, and re-layouts: 0.81 us -> 16.9 us  [the longest x1 11.9 us: on_device(): received_time_rows[:, :PSYM]]
    sub x1 -> x2, other arithmetic: 12.1 us -> 23.7 us  [the longest x1 22.7 us: gram_terms(): gram_imag = gram[:, 0, :, 1] - gram[:, 1, :, 0]]
    add x3 -> x6, other arithmetic: 4.1 us -> 9.68 us  [halving_reduce_scatter(): parts = keep + lax.ppermute(send, 'fh', perm=pairs)]
    dynamic_slice x0 -> x2, local copies, waits for them, and re-layouts: none -> 4.38 us  [halving_reduce_scatter(): send = lax.dynamic_index_in_dim(paired, 1 - mine, axis=1, keepdims=False)]
    ppermute x4 -> x8, starting transfers between devices: 7.88 us -> 11.8 us  [halving_reduce_scatter(): parts = keep + lax.ppermute(send, 'fh', perm=pairs)]
    dot_general x3, matrix products: 23.5 us -> 20.1 us  [the longest x1 10.3 us: gram_terms(): jnp.einsum('rdkm,relm->rdkel', channel, channel, preferred_element_type=j...]
    reshape x1, local copies, waits for them, and re-layouts: 10.9 us -> 7.66 us  [spectra(): shaped = samples.reshape(antennas_here, symbol_count, 2, FA, FB)]
    another operation x0 -> x1, local copies, waits for them, and re-layouts: none -> 3.15 us
  transfers between devices with their start and end apart: 4 -> 8, of which waited for: 4 -> 4; matrix products, arithmetic and copies ran while one was open for 0% -> 17% of each run, Pallas kernels for 0% -> 0%
where the time goes in v4:
time: 285 us; the launch traced here: 282 us
  waiting for transfers between devices  62.8 us (22%)
  local copies, waits for them, and re-layouts  61.2 us (21%)
  other arithmetic  51.4 us (18%)
  Pallas kernels  50.4 us (18%)
  matrix products  31.8 us (11%)
  blocking collectives  12.2 us (4%)
  starting transfers between devices  11.8 us (4%)
    ppermute x8, waiting for transfers between devices, halving_reduce_scatter(): parts = keep + lax.ppermute(send, 'fh', perm=pairs)  62.8 us
    pallas_call x1, Pallas kernels, spd_solve_t(): pl.pallas_call(_solve_body, out_shape=jax.ShapeDtypeStruct(rhs_t.shape, j...  50.4 us
    sub x1, other arithmetic, gram_terms(): gram_imag = gram[:, 0, :, 1] - gram[:, 1, :, 0]  22.7 us
    all_to_all x1, blocking collectives, on_device(): return lax.all_to_all(result, 'fh', split_axis=0, concat_axis=3, tiled=True)  12.2 us
    slice x1, local copies, waits for them, and re-layouts, on_device(): received_time_rows[:, :PSYM]  11.9 us
    ppermute x8, starting transfers between devices, halving_reduce_scatter(): parts = keep + lax.ppermute(send, 'fh', perm=pairs)  11.8 us
    another operation x2, local copies, waits for them, and re-layouts, spectra(): section_one = jnp.stack([real_part, imag_part], 1).astype(jnp.bfloat16)  11.2 us
    dot_general x1, matrix products, gram_terms(): jnp.einsum('rdkm,relm->rdkel', channel, channel, preferred_element_type=j...  10.3 us
  transfers between devices with their start and end apart: 8, of which 4 were waited for; matrix products, arithmetic and copies ran while one was open for 17% of the time, Pallas kernels for 0%

profile of v4, /device:TPU:0, one launch (start us, length us, event | category | flops | bytes accessed | tf_op | source)
XLA Modules:
  0.0 282.4 jit_solution(2305608279161234808)
XLA Ops:
  0.1 0.1 sine_multiply_fusion.1
  0.2 1.1 negate_convert_fusion
  1.3 1.0 fusion.36
  2.4 11.9 %slice.52 = bf16[128,2,2,4096]{3,2,1,0:T(2,128)(2,1)} slice(bf16[128,3,2,4096]{3,2,1,0:T(2,128)(2,1)} %param.5), slice={[0:128], [0:2], [0:2], [0:4096]} | slice | bytes 8388608 | tf_op jit(solution)/shard_map/slice | solution.py:249
  14.3 7.7 %reshape.416 = bf16[128,2,2,16,256,1]{4,3,2,1,0,5:T(8,128)(2,1)} reshape(bf16[128,2,2,4096]{3,2,1,0:T(2,128)(2,1)} %slice.52) | data formatting | bytes 8388608 | tf_op jit(solution)/shard_map/reshape | solution.py:108
  22.0 3.5 %convolution_bitcast_fusion = f32[2,2,16,256,128]{3,2,0,4,1:T(8,128)S(1)} fusion(bf16[128,2,2,16,256,1]{4,3,2,1,0,5:T(8,128)(2,1)} %reshape.416, bf16[1,16,2,16]{1,3,0,2:T(8,128)(2,1)S(1)} %get-tuple-element.27, bf16[1,16,2,16]{1,3,0,2:T(8,128)(2,1)S(1)} %get-tuple-element.26), kind=kOutput, calls=%fused_computation.22 | convolution fusion | flops 134221824 | bytes 12584960 | tf_op jit(solution)/shard_map/ascnm,cndk->sdkma/dot_general | solution.py:109
  25.5 1.4 add_convert_fusion
  26.9 2.3 pad_maximum_fusion
  29.2 8.2 %copy.72 = bf16[2,2,16,256,128]{4,3,1,2,0:T(8,128)(2,1)} copy(bf16[2,2,16,256,128]{3,2,0,4,1:T(8,128)(2,1)} %pad_maximum_fusion) | data formatting | bytes 8388608 | tf_op jit(solution)/shard_map/stack | solution.py:117
  37.5 0.1 broadcast_add_fusion
  37.6 0.2 fusion.43
  37.8 4.5 %bitcast_convert_fusion.1 = bf16[2,256,2,16,128]{4,1,3,2,0:T(8,128)(2,1)S(1)} fusion(bf16[2,2,16,256,128]{4,3,1,2,0:T(8,128)(2,1)} %copy.72, bf16[1,256,2,256]{1,3,0,2:T(8,128)(2,1)S(1)} %get-tuple-element.23, bf16[1,256,2,256]{1,3,0,2:T(8,128)(2,1)S(1)} %get-tuple-element.22), kind=kOutput, calls=%fused_computation.1 | convolution fusion | flops 2150629376 | bytes 8912896 | tf_op jit(solution)/shard_map/sckma,cmdj->sdkja/dot_general | solution.py:118
  42.4 5.7 %fusion.5 = bf16[2,64,128,128,1,1,1]{3,1,6,5,2,0,4:T(8,128)(2,1)S(1)} fusion(bf16[2,2,16,128,2,128,1]{5,4,3,2,0,1,6:T(2,128)(2,1)S(1)} %bitcast.180, bf16[1,64,2,2,16,2]{1,4,2,3,0,5:T(8,128)(2,1)S(1)} %get-tuple-element.25, bf16[1,64,2,2,16,2]{1,4,2,3,0,5:T(8,128)(2,1)S(1)} %get-tuple-element.24), kind=kOutput, calls=%fused_computation.15 | convolution fusion | flops 536936448 | bytes 8421376 | tf_op jit(solution)/shard_map/tcarbm,dktcab->rdkm/dot_general | solution.py:189
  48.1 1.9 copy-done
  50.0 10.3 %fusion.2 = f32[128,2,64,2,64]{4,2,3,1,0:T(8,128)} fusion(bf16[2,64,128,128,1,1,1]{3,1,6,5,2,0,4:T(8,128)(2,1)S(1)} %fusion.5), kind=kOutput, calls=%fused_computation.11 | convolution fusion | flops 536870912 | bytes 12582912 | tf_op jit(solution)/shard_map/rdkm,relm->rdkel/dot_general | solution.py:195
  60.3 22.7 %slice_subtract_fusion = (f32[128,1,64,1,64]{4,2,3,1,0:T(8,128)}, f32[128,1,64,1,64]{4,2,3,1,0:T(8,128)}) fusion(f32[128,2,64,2,64]{4,2,3,1,0:T(8,128)} %fusion.2), kind=kLoop, calls=%fused_computation.6 | loop fusion | flops 1048576 | bytes 12582912 | tf_op jit(solution)/shard_map/sub | solution.py:197
  83.0 4.4 %broadcast_select_fusion = f32[8,2,8,64,64]{4,3,2,1,0:T(8,128)S(1)} fusion(f32[8,2,8,64,64]{4,3,2,1,0:T(8,128)} %bitcast.179, f32[8,2,8,64,64]{4,3,2,1,0:T(8,128)} %bitcast.178, pred[64,64]{1,0:T(8,128)(4,1)S(1)} %iota_compare_fusion.3), kind=kLoop, calls=%fused_computation.36 | loop fusion | flops 524288 | bytes 6295552 | tf_op jit(solution)/shard_map/jit(_where)/select_n | solution.py:201
  87.4 1.9 copy-done.2
  89.4 1.5 dynamic-slice_bitcast_fusion
  90.9 0.4 collective-permute-start
  91.4 5.0 %slice.59 = bf16[128,1,2,4096]{3,2,1,0:T(2,128)(2,1)} slice(bf16[128,3,2,4096]{3,2,1,0:T(2,128)(2,1)} %param.5), slice={[0:128], [2:3], [0:2], [0:4096]} | slice | bytes 4194304 | tf_op jit(solution)/shard_map/slice | solution.py:251
  96.3 3.1 %reshape.426 = bf16[128,2,16,256,1]{3,2,1,0,4:T(8,128)(2,1)S(1)} reshape(bf16[128,1,2,4096]{3,2,1,0:T(2,128)(2,1)} %slice.59) | data formatting | bytes 4194304 | tf_op jit(solution)/shard_map/reshape.6
  99.5 0.7 convolution_bitcast_fusion.1
  100.2 0.7 fusion.18
  100.9 0.2 pad_maximum_fusion.1
  101.1 3.0 %copy.75 = bf16[2,16,256,128]{3,2,0,1:T(8,128)(2,1)} copy(bf16[2,16,256,128]{2,1,3,0:T(8,128)(2,1)S(1)} %pad_maximum_fusion.1) | data formatting | bytes 4194304 | tf_op jit(solution)/shard_map/stack | solution.py:117
  104.1 3.0 %bitcast_convert_fusion.2 = bf16[2,256,16,128]{3,1,2,0:T(8,128)(2,1)S(1)} fusion(bf16[2,16,256,128]{3,2,0,1:T(8,128)(2,1)} %copy.75, bf16[1,256,2,256]{1,3,0,2:T(8,128)(2,1)S(1)} %get-tuple-element.23, bf16[1,256,2,256]{1,3,0,2:T(8,128)(2,1)S(1)} %get-tuple-element.22), kind=kOutput, calls=%fused_computation.14 | convolution fusion | flops 1075838976 | bytes 4718592 | tf_op jit(solution)/shard_map/sckma,cmdj->sdkja/dot_general | solution.py:118
  107.1 4.1 %fusion.9 = f32[128,2,64,1,2,16,2]{2,5,6,4,1,0,3:T(8,128)S(1)} fusion(bf16[2,16,128,2,128,1]{4,3,2,1,0,5:T(2,128)(2,1)S(1)} %bitcast.190, bf16[2,64,128,128,1,1,1]{3,1,6,5,2,0,4:T(8,128)(2,1)S(1)} %copy-done.1), kind=kOutput, calls=%fused_computation.21 | convolution fusion | flops 268435456 | bytes 10485760 | tf_op jit(solution)/shard_map/rdkm,tcarbm->rdktcab/dot_general | solution.py:205
  111.2 1.0 slice_subtract_fusion.1
  112.3 2.6 copy.77
  114.8 2.5 copy.78
  117.4 4.2 %fusion.15 = (f32[8,1,8,64,64]{3,2,1,0,4:T(8,128)S(1)}, f32[8,1,8,64,64]{3,2,1,0,4:T(8,128)}) fusion(s32[]{:T(128)S(6)} %select_n.163, f32[8,2,8,64,32]{3,2,1,0,4:T(8,128)} %bitcast.185, f32[8,2,8,64,32]{3,2,1,0,4:T(8,128)} %bitcast.186, s32[]{:T(128)S(6)} %select_n.164), kind=kLoop, calls=%fused_computation.25 | loop fusion | flops 524288 | bytes 4194312 | tf_op jit(solution)/shard_map/concatenate | solution.py:214
  121.5 3.4 %copy.80 = f32[8,1,8,64,64]{4,3,2,0,1:T(8,128)} copy(f32[8,1,8,64,64]{3,2,1,0,4:T(8,128)} %get-tuple-element.16) | data formatting | bytes 2097152 | tf_op jit(solution)/shard_map/jit(dynamic_index_in_dim)/dynamic_slice | solution.py:240
  125.0 2.4 copy.79
  127.5 2.8 bitcast_add_fusion.1
  130.3 0.1 dynamic-slice_bitcast_fusion.2
  130.4 3.0 %collective-permute-start.1 = (f32[4,8,64,64]{3,2,1,0:T(8,128)S(1)}, f32[4,8,64,64]{3,2,1,0:T(8,128)}, u32[]{:S(2)}, u32[]{:S(2)}) collective-permute-start(f32[4,8,64,64]{3,2,1,0:T(8,128)S(1)} %dynamic-slice_bitcast_fusion.2), channel_id=1, source_target_pairs={{0,2},{1,3},{2,0},{3,1},{4,6},{5,7},{6,4},{7,5},{8,10},{9,11},{10,... | collective-permute-start | bytes 1572872 | tf_op jit(solution)/shard_map/ppermute | solution.py:242
  133.4 2.0 bitcast_add_fusion
  135.4 1.3 copy-done.3
  136.8 1.1 dynamic-slice_bitcast_fusion.1
  137.9 19.6 %collective-permute-done.1 = f32[4,8,64,64]{3,2,1,0:T(8,128)} collective-permute-done((f32[4,8,64,64]{3,2,1,0:T(8,128)S(1)}, f32[4,8,64,64]{3,2,1,0:T(8,128)}, u32[]{:S(2)}, u32[]{:S(2)}) %collective-permute-start.1) | collective-permute-done | bytes 524320 | tf_op jit(solution)/shard_map/ppermute | solution.py:242
  157.5 1.4 bitcast_add_fusion.3
  158.9 2.2 collective-permute-start.2
  161.1 18.2 %collective-permute-done.5 = f32[4,8,64,64]{3,2,1,0:T(8,128)} collective-permute-done((f32[4,8,64,64]{3,2,1,0:T(8,128)}, f32[4,8,64,64]{3,2,1,0:T(8,128)}, u32[]{:S(2)}, u32[]{:S(2)}) %collective-permute-start.5) | collective-permute-done | bytes 524320 | tf_op jit(solution)/shard_map/ppermute | solution.py:242
  179.3 1.4 bitcast_add_fusion.2
  180.7 0.1 constant_dynamic-slice_fusion.2
  180.8 1.0 copy.82
  181.8 1.8 collective-permute-start.6
  183.6 0.2 copy.81
  183.8 1.1 bitcast_add_fusion.5
  184.9 2.6 collective-permute-start.3
  187.6 13.5 %collective-permute-done.6 = f32[2,8,64,64]{2,3,1,0:T(8,128)} collective-permute-done((f32[2,8,64,64]{2,3,1,0:T(8,128)}, f32[2,8,64,64]{2,3,1,0:T(8,128)}, u32[]{:S(2)}, u32[]{:S(2)}) %collective-permute-start.6) | collective-permute-done | bytes 262176 | tf_op jit(solution)/shard_map/ppermute | solution.py:242
  201.1 1.1 bitcast_add_fusion.4
  202.2 1.6 collective-permute-start.7
  203.8 0.1 copy.74
  204.0 11.6 %collective-permute-done.7 = f32[1,8,64,64]{2,3,1,0:T(8,128)S(1)} collective-permute-done((f32[1,8,64,64]{2,3,1,0:T(8,128)S(1)}, f32[1,8,64,64]{2,3,1,0:T(8,128)S(1)}, u32[]{:S(2)}, u32[]{:S(2)}) %collective-permute-start.7) | collective-permute-done | bytes 131104 | tf_op jit(solution)/shard_map/ppermute | solution.py:242
  215.6 0.8 maximum_bitcast_fusion.2.b_ref
  216.4 0.2 fusion.65
  216.6 1.0 maximum_maximum_fusion.a_ref
  217.6 50.4 %shard_map.55 = f32[8,32,128]{2,1,0:T(8,128)} custom-call(f32[8,128,128]{2,1,0:T(8,128)} %maximum_maximum_fusion.a_ref, f32[8,32,128]{2,1,0:T(8,128)} %maximum_bitcast_fusion.2.b_ref), custom_call_target="tpu_custom_call" | custom-call | tf_op jit(solution)/shard_map/pallas_call | solution.py:75
  268.0 1.1 reshape.413
  269.1 0.1 copy.84
  269.2 12.2 %all_to_all.18 = f32[64,1,2,256]{3,2,1,0:T(2,128)S(1)} all-to-all(f32[64,1,2,256]{3,2,1,0:T(2,128)S(1)} %copy.84), channel_id=1, replica_groups=mesh['cells'=2,'fh'=16] {'fh'}, dimensions={0} | all-to-all | bytes 262144 | tf_op jit(solution)/shard_map/all_to_all | solution.py:258
  281.5 0.7 copy.106
  (43 shorter events, 0.7 us)
Async XLA Ops:
  29.2 8.3 %copy-start.7 = (s32[64]{0:T(128)S(1)}, s32[64]{0:T(128)}, u32[]{:S(2)}) copy-start(s32[64]{0:T(128)} %param.6) | copy-start | bytes 772
  48.1 2.0 copy-start
  87.4 2.0 copy-start.2
  90.9 36.5 %collective-permute-start = (f32[8,8,64,64]{3,2,1,0:T(8,128)}, f32[8,8,64,64]{3,2,1,0:T(8,128)}, u32[]{:S(2)}, u32[]{:S(2)}) collective-permute-start(f32[8,8,64,64]{3,2,1,0:T(8,128)} %dynamic-slice_bitcast_fusion), channel_id=1, source_target_pairs={{0,1},{1,0},{2,3},{3,2},{4,5},{5,4},{6,7},{7,6},{8,9},{9,8},{10,11... | collective-permute-start | bytes 3145736 | tf_op jit(solution)/shard_map/ppermute | solution.py:242
  104.1 3.0 %copy-start.1 = (bf16[2,64,128,128,1,1,1]{3,1,6,5,2,0,4:T(8,128)(2,1)S(1)}, bf16[2,64,128,128,1,1,1]{3,1,6,5,2,0,4:T(8,128)(2,1)}, u32[]{:S(2)}) copy-start(bf16[2,64,128,128,1,1,1]{3,1,6,5,2,0,4:T(8,128)(2,1)} %copy-done) | copy-start | bytes 12582916
  121.5 5.9 %copy-start.9 = (s32[64]{0:T(128)S(1)}, s32[64]{0:T(128)}, u32[]{:S(2)}) copy-start(s32[64]{0:T(128)} %param.7) | copy-start | bytes 772
  121.5 5.9 %copy-start.8 = (f32[64]{0:T(128)S(1)}, f32[64]{0:T(128)}, u32[]{:S(2)}) copy-start(f32[64]{0:T(128)} %param.9) | copy-start | bytes 772
  124.9 8.5 %collective-permute-start.4 = (f32[8,8,64,64]{3,2,1,0:T(8,128)}, f32[8,8,64,64]{3,2,1,0:T(8,128)}, u32[]{:S(2)}, u32[]{:S(2)}) collective-permute-start(f32[8,8,64,64]{3,2,1,0:T(8,128)} %bitcast.191), channel_id=1, source_target_pairs={{0,1},{1,0},{2,3},{3,2},{4,5},{5,4},{6,7},{7,6},{8,9},{9,8},{10,11... | collective-permute-start | bytes 3145736 | tf_op jit(solution)/shard_map/ppermute | solution.py:242
  127.5 6.0 %copy-start.5 = (f32[8,1,8,64,64]{4,3,2,0,1:T(8,128)S(1)}, f32[8,1,8,64,64]{4,3,2,0,1:T(8,128)}, u32[]{:S(2)}) copy-start(f32[8,1,8,64,64]{4,3,2,0,1:T(8,128)} %copy.79) | copy-start | bytes 3145732
  130.4 7.5 %copy-start.6 = (s32[8,64]{1,0:T(8,128)S(1)}, s32[8,64]{1,0:T(8,128)}, u32[]{:S(2)}) copy-start(s32[8,64]{1,0:T(8,128)} %param.8) | copy-start | bytes 6148
  130.4 27.1 %collective-permute-start.1 = (f32[4,8,64,64]{3,2,1,0:T(8,128)S(1)}, f32[4,8,64,64]{3,2,1,0:T(8,128)}, u32[]{:S(2)}, u32[]{:S(2)}) collective-permute-start(f32[4,8,64,64]{3,2,1,0:T(8,128)S(1)} %dynamic-slice_bitcast_fusion.2), channel_id=1, source_target_pairs={{0,2},{1,3},{2,0},{3,1},{4,6},{5,7},{6,4},{7,5},{8,10},{9,11},{10,... | collective-permute-start | bytes 1572872 | tf_op jit(solution)/shard_map/ppermute | solution.py:242
  135.4 1.4 copy-start.3
  137.9 41.5 %collective-permute-start.5 = (f32[4,8,64,64]{3,2,1,0:T(8,128)}, f32[4,8,64,64]{3,2,1,0:T(8,128)}, u32[]{:S(2)}, u32[]{:S(2)}) collective-permute-start(f32[4,8,64,64]{3,2,1,0:T(8,128)} %dynamic-slice_bitcast_fusion.1), channel_id=1, source_target_pairs={{0,2},{1,3},{2,0},{3,1},{4,6},{5,7},{6,4},{7,5},{8,10},{9,11},{10,... | collective-permute-start | bytes 1572872 | tf_op jit(solution)/shard_map/ppermute | solution.py:242
  137.9 41.4 %copy-start.4 = (f32[8,8,64,64]{3,2,1,0:T(8,128)S(1)}, f32[8,8,64,64]{3,2,1,0:T(8,128)}, u32[]{:S(2)}) copy-start(f32[8,8,64,64]{3,2,1,0:T(8,128)} %copy-done.3) | copy-start | bytes 3145732
  158.9 24.9 %collective-permute-start.2 = (f32[2,8,64,64]{3,2,1,0:T(8,128)S(1)}, f32[2,8,64,64]{3,2,1,0:T(8,128)}, u32[]{:S(2)}, u32[]{:S(2)}) collective-permute-start(f32[2,8,64,64]{3,2,1,0:T(8,128)S(1)} %dynamic-slice_bitcast_fusion.3), channel_id=1, source_target_pairs={{0,4},{1,5},{2,6},{3,7},{4,0},{5,1},{6,2},{7,3},{8,12},{9,13},{10,... | collective-permute-start | bytes 786440 | tf_op jit(solution)/shard_map/ppermute | solution.py:242
  181.8 19.2 %collective-permute-start.6 = (f32[2,8,64,64]{2,3,1,0:T(8,128)}, f32[2,8,64,64]{2,3,1,0:T(8,128)}, u32[]{:S(2)}, u32[]{:S(2)}) collective-permute-start(f32[2,8,64,64]{2,3,1,0:T(8,128)} %bitcast.73), channel_id=1, source_target_pairs={{0,4},{1,5},{2,6},{3,7},{4,0},{5,1},{6,2},{7,3},{8,12},{9,13},{10,... | collective-permute-start | bytes 786440 | tf_op jit(solution)/shard_map/ppermute | solution.py:242
  184.9 18.9 %collective-permute-start.3 = (f32[1,8,64,64]{3,2,1,0:T(8,128)S(1)}, f32[1,8,64,64]{3,2,1,0:T(8,128)S(1)}, u32[]{:S(2)}, u32[]{:S(2)}) collective-permute-start(f32[1,8,64,64]{3,2,1,0:T(8,128)S(1)} %constant_dynamic-slice_fusion.3), channel_id=1, source_target_pairs={{0,8},{1,9},{2,10},{3,11},{4,12},{5,13},{6,14},{7,15},{8,0},{9,1},... | collective-permute-start | bytes 393224 | tf_op jit(solution)/shard_map/ppermute | solution.py:242
  202.2 13.4 %collective-permute-start.7 = (f32[1,8,64,64]{2,3,1,0:T(8,128)S(1)}, f32[1,8,64,64]{2,3,1,0:T(8,128)S(1)}, u32[]{:S(2)}, u32[]{:S(2)}) collective-permute-start(f32[1,8,64,64]{2,3,1,0:T(8,128)S(1)} %constant_dynamic-slice_fusion), channel_id=1, source_target_pairs={{0,8},{1,9},{2,10},{3,11},{4,12},{5,13},{6,14},{7,15},{8,0},{9,1},... | collective-permute-start | bytes 393224 | tf_op jit(solution)/shard_map/ppermute | solution.py:242

commit v5 on v3

--- a/solution.py
+++ b/solution.py
@@ -15,72 +15,92 @@
 FB = 256
 
 PANEL = 8
-PREC = lax.Precision.HIGHEST
-
-
-def _solve_body(a_ref, b_ref, x_ref, s_ref, lt_ref, l_ref):
+PREC = lax.Precision.HIGH
+
+
+def _solve_body(a_ref, b_ref, x_ref, s_ref, r_ref, lt_ref, y_ref):
     nb, n, _ = a_ref.shape
+    panels = n // PANEL
     s_ref[...] = a_ref[...]
-    x_ref[...] = b_ref[...]
+    r_ref[...] = b_ref[...]
     lane = lax.broadcasted_iota(jnp.int32, (1, n), 1)
-
-    def panel(p, carry):
+    sub = lax.broadcasted_iota(jnp.int32, (PANEL, 1), 0)
+
+    def forward(p, carry):
         j0 = pl.multiple_of(p * PANEL, PANEL)
         rows = [s_ref[b, pl.ds(j0, PANEL), :] for b in range(nb)]
-        xts = [x_ref[b] for b in range(nb)]
-        factors = [[] for b in range(nb)]
+        sides = [r_ref[b, pl.ds(j0, PANEL), :] for b in range(nb)]
+        factors = [[] for _ in range(nb)]
+        solved = [[] for _ in range(nb)]
         for t in range(PANEL):
             j = j0 + t
             hit = lane == j
             keep = lane >= j
-            after = lane > j
             for b in range(nb):
-                d = jnp.sum(jnp.where(hit, rows[b][t:t + 1, :], 0.0), axis=1, keepdims=True)
+                pivot_row = rows[b][t:t + 1, :]
+                d = jnp.sum(jnp.where(hit, pivot_row, 0.0), axis=1, keepdims=True)
                 inv = 1.0 / jnp.sqrt(d)
-                l = jnp.where(keep, rows[b][t:t + 1, :], 0.0) * inv
+                l = jnp.where(keep, pivot_row, 0.0) * inv
                 col = jnp.sum(jnp.where(hit, rows[b], 0.0), axis=1, keepdims=True) * inv
                 rows[b] = rows[b] - col * l
-                y = jnp.sum(jnp.where(hit, xts[b], 0.0), axis=1, keepdims=True) * inv
-                xts[b] = jnp.where(hit, y, xts[b] - y * jnp.where(after, l, 0.0))
+                y = sides[b][t:t + 1, :] * inv
+                sides[b] = sides[b] - col * y
                 factors[b].append(l)
+                solved[b].append(y)
         for b in range(nb):
             block = jnp.concatenate(factors[b], axis=0)
+            ys = jnp.concatenate(solved[b], axis=0)
             lt_ref[b, pl.ds(j0, PANEL), :] = block
-            x_ref[b] = xts[b]
+            y_ref[b, pl.ds(j0, PANEL), :] = ys
             update = lax.dot_general(
-                block, block, (((0,), (0,)), ((), ())),
+                block, jnp.concatenate([block, ys], axis=1), (((0,), (0,)), ((), ())),
                 precision=PREC, preferred_element_type=jnp.float32)
-            s_ref[b] = s_ref[b] - update
+            s_ref[b] = s_ref[b] - update[:, :n]
+            r_ref[b] = r_ref[b] - update[:, n:]
         return carry
 
-    lax.fori_loop(0, n // PANEL, panel, 0)
-    for b in range(nb):
-        l_ref[b] = jnp.transpose(lt_ref[b])
-
-    def backward(t, carry):
-        i = n - 1 - t
+    lax.fori_loop(0, panels, forward, 0)
+    x_ref[...] = jnp.zeros(x_ref.shape, jnp.float32)
+
+    def backward(q, carry):
+        j0 = pl.multiple_of((panels - 1 - q) * PANEL, PANEL)
+        blocks = []
+        rests = []
+        diags = []
         for b in range(nb):
-            lrow = l_ref[b, pl.ds(i, 1), :]
-            lii = jnp.sum(jnp.where(lane == i, lrow, 0.0), axis=1, keepdims=True)
-            yt = x_ref[b]
-            xi = jnp.sum(jnp.where(lane == i, yt, 0.0), axis=1, keepdims=True) / lii
-            x_ref[b] = jnp.where(lane == i, xi, yt - xi * jnp.where(lane < i, lrow, 0.0))
+            block = lt_ref[b, pl.ds(j0, PANEL), :]
+            rest = y_ref[b, pl.ds(j0, PANEL), :] - jnp.dot(
+                block, x_ref[b], precision=PREC, preferred_element_type=jnp.float32)
+            blocks.append(block)
+            rests.append(rest)
+            diags.append(jnp.sum(jnp.where(lane == j0 + sub, block, 0.0), axis=1, keepdims=True))
+        outs = [[None] * PANEL for _ in range(nb)]
+        for t in reversed(range(PANEL)):
+            hit = lane == j0 + t
+            for b in range(nb):
+                xt = rests[b][t:t + 1, :] / diags[b][t:t + 1, :]
+                col = jnp.sum(jnp.where(hit, blocks[b], 0.0), axis=1, keepdims=True)
+                rests[b] = rests[b] - col * xt
+                outs[b][t] = xt
+        for b in range(nb):
+            x_ref[b, pl.ds(j0, PANEL), :] = jnp.concatenate(outs[b], axis=0)
         return carry
 
-    lax.fori_loop(0, n, backward, 0)
-
-
-def spd_solve_t(matrix, rhs_t):
+    lax.fori_loop(0, panels, backward, 0)
+
+
+def spd_solve(matrix, rhs):
     nb, n, _ = matrix.shape
     return pl.pallas_call(
         _solve_body,
-        out_shape=jax.ShapeDtypeStruct(rhs_t.shape, jnp.float32),
+        out_shape=jax.ShapeDtypeStruct(rhs.shape, jnp.float32),
         scratch_shapes=[
             pltpu.VMEM((nb, n, n), jnp.float32),
+            pltpu.VMEM(rhs.shape, jnp.float32),
             pltpu.VMEM((nb, n, n), jnp.float32),
-            pltpu.VMEM((nb, n, n), jnp.float32),
+            pltpu.VMEM(rhs.shape, jnp.float32),
         ],
-    )(matrix, rhs_t)
+    )(matrix, rhs)
 
 
 def dft_table(length):
@@ -178,7 +198,7 @@
         [jnp.concatenate([sys_real, -sys_imag], 2), jnp.concatenate([sys_imag, sys_real], 2)], 1
     )
     right_side = jnp.concatenate([side_real, side_imag], 1)
-    solved = jnp.swapaxes(spd_solve_t(matrix, jnp.swapaxes(right_side, 1, 2)), 1, 2)
+    solved = spd_solve(matrix, right_side)
     blocks = solved.shape[0]
     solved = solved.reshape(blocks, 2, user_count, -1, FA, B // FA)
     solved = jnp.transpose(solved, (2, 3, 1, 0, 5, 4))

time: 245 us -> 215 us (0.88)
  Pallas kernels: 50.4 us -> 37 us
  waiting for transfers between devices: 60.9 us -> 50.1 us
  local copies, waits for them, and re-layouts: 41.9 us -> 38.2 us
  matrix products: 34.8 us -> 31.3 us
    pallas_call x1, Pallas kernels: 50.4 us -> 37 us  [spd_solve(): pl.pallas_call(_solve_body, out_shape=jax.ShapeDtypeStruct(rhs.shape, jnp...]
    ppermute x4, waiting for transfers between devices: 60.9 us -> 50.1 us  [halving_reduce_scatter(): parts = keep + lax.ppermute(send, 'fh', perm=pairs)]
    dot_general x1, matrix products: 13.8 us -> 10.3 us  [packed_terms(): jnp.einsum('rdkm,relm->rdkel', channel, channel, preferred_element_type=j...]
    unnamed x18 -> x16, local copies, waits for them, and re-layouts: 6.12 us -> 5.64 us
where the time goes in v5:
time: 215 us; the launch traced here: 214 us
  waiting for transfers between devices  50.1 us (23%)
  local copies, waits for them, and re-layouts  38.2 us (18%)
  Pallas kernels  37 us (17%)
  other arithmetic  36.1 us (17%)
  matrix products  31.3 us (15%)
  blocking collectives  13.1 us (6%)
  starting transfers between devices  7.83 us (4%)
    ppermute x4, waiting for transfers between devices, halving_reduce_scatter(): parts = keep + lax.ppermute(send, 'fh', perm=pairs)  50.1 us
    pallas_call x1, Pallas kernels, spd_solve(): pl.pallas_call(_solve_body, out_shape=jax.ShapeDtypeStruct(rhs.shape, jnp...  37 us
    all_to_all x1, blocking collectives, on_device(): return lax.all_to_all(result, 'fh', split_axis=0, concat_axis=3, tiled=True)  13.1 us
    sub x1, other arithmetic, packed_terms(): gram_imag = gram[:, 0, :, 1] - gram[:, 1, :, 0]  12.1 us
    reshape x1, local copies, waits for them, and re-layouts, spectra(): shaped = samples.reshape(antennas_here, symbol_count, 2, FA, FB)  10.8 us
    dot_general x1, matrix products, packed_terms(): jnp.einsum('rdkm,relm->rdkel', channel, channel, preferred_element_type=j...  10.3 us
    another operation x1, local copies, waits for them, and re-layouts, spectra(): section_one = jnp.stack([real_part, imag_part], 1).astype(jnp.bfloat16)  9.13 us
    ppermute x4, starting transfers between devices, halving_reduce_scatter(): parts = keep + lax.ppermute(send, 'fh', perm=pairs)  7.83 us
  transfers between devices with their start and end apart: 4, of which 4 were waited for; matrix products, arithmetic and copies ran while one was open for 0% of the time, Pallas kernels for 0%

profile of v5, /device:TPU:0, one launch (start us, length us, event | category | flops | bytes accessed | tf_op | source)
XLA Modules:
  0.0 213.9 jit_solution(7687229301071222526)
XLA Ops:
  0.0 0.1 negate_convert_fusion.2
  0.1 0.1 fusion.55
  0.1 0.1 sine_multiply_fusion.1
  0.2 1.1 negate_convert_fusion
  1.3 1.0 fusion.32
  2.3 10.8 %reshape.381 = bf16[128,3,2,16,256,1]{4,3,2,1,0,5:T(8,128)(2,1)} reshape(bf16[128,3,2,4096]{3,2,1,0:T(2,128)(2,1)} %param.5) | data formatting | bytes 12582912 | tf_op jit(solution)/shard_map/reshape | solution.py:128
  13.1 4.7 %convolution_bitcast_fusion = f32[3,2,16,256,128]{3,2,0,4,1:T(8,128)S(1)} fusion(bf16[128,3,2,16,256,1]{4,3,2,1,0,5:T(8,128)(2,1)} %reshape.381, bf16[1,16,2,16]{1,3,0,2:T(8,128)(2,1)S(1)} %get-tuple-element.21, bf16[1,16,2,16]{1,3,0,2:T(8,128)(2,1)S(1)} %get-tuple-element.20), kind=kOutput, calls=%fused_computation.8 | convolution fusion | flops 201330688 | bytes 18876416 | tf_op jit(solution)/shard_map/ascnm,cndk->sdkma/dot_general | solution.py:129
  17.8 2.2 %add_convert_fusion = (bf16[3,1,16,256,128]{3,2,0,4,1:T(8,128)(2,1)S(1)}, bf16[3,1,16,256,128]{3,2,0,4,1:T(8,128)(2,1)S(1)}) fusion(f32[3,2,16,256,128]{3,2,0,4,1:T(8,128)S(1)} %convolution_bitcast_fusion, f32[16,256]{1,0:T(8,128)S(1)} %get-tuple-element.27, f32[16,256]{1,0:T(8,128)S(1)} %get-tuple-element.28), kind=kLoop, calls=%fused_computation.7 | loop fusion | flops 12582912 | bytes 18907136 | tf_op jit(solution)/shard_map/convert
  20.0 3.2 %pad_maximum_fusion = bf16[3,2,16,256,128]{3,2,0,4,1:T(8,128)(2,1)} fusion(bf16[3,1,16,256,128]{3,2,0,4,1:T(8,128)(2,1)S(1)} %get-tuple-element.10, bf16[3,1,16,256,128]{3,2,0,4,1:T(8,128)(2,1)S(1)} %get-tuple-element.9), kind=kLoop, calls=%fused_computation.3 | loop fusion | flops 3145728 | bytes 12582912 | tf_op jit(solution)/shard_map/stack | solution.py:137
  23.2 9.1 %copy.72 = bf16[3,2,16,256,128]{4,3,1,2,0:T(8,128)(2,1)} copy(bf16[3,2,16,256,128]{3,2,0,4,1:T(8,128)(2,1)} %pad_maximum_fusion) | data formatting | bytes 12582912 | tf_op jit(solution)/shard_map/stack | solution.py:137
  32.4 6.6 %fusion = bf16[3,2,16,256,128]{4,3,2,0,1:T(8,128)(2,1)S(1)} fusion(bf16[3,2,16,256,128]{4,3,1,2,0:T(8,128)(2,1)} %copy.72, bf16[1,256,2,256]{1,3,0,2:T(8,128)(2,1)S(1)} %get-tuple-element.17, bf16[1,256,2,256]{1,3,0,2:T(8,128)(2,1)S(1)} %get-tuple-element.16), kind=kOutput, calls=%fused_computation.2 | convolution fusion | flops 3225419776 | bytes 13107200 | tf_op jit(solution)/shard_map/sckma,cmdj->sdkja/dot_general | solution.py:138
  39.0 0.0 copy-start.3
  39.0 0.0 copy-start.5
  39.0 0.3 slice.64
  39.3 2.4 %copy-done.3 = bf16[3,2,16,256,128]{4,3,2,0,1:T(8,128)(2,1)} copy-done((bf16[3,2,16,256,128]{4,3,2,0,1:T(8,128)(2,1)}, bf16[3,2,16,256,128]{4,3,2,0,1:T(8,128)(2,1)S(1)}, u32[]{:S(2)}) %copy-start.3) | copy-done | bytes 6291480
  41.7 0.1 iota_add_fusion
  41.8 0.1 broadcast_add_fusion
  41.8 0.0 copy-done.5
  41.8 0.2 fusion.39
  42.1 5.7 %fusion.8 = bf16[2,64,128,128,1,1,1]{3,1,6,5,2,0,4:T(8,128)(2,1)S(1)} fusion(bf16[2,2,16,128,2,128,1]{5,4,3,2,0,1,6:T(2,128)(2,1)S(1)} %bitcast.132, bf16[1,64,2,2,16,2]{1,4,2,3,0,5:T(8,128)(2,1)S(1)} %get-tuple-element.19, bf16[1,64,2,2,16,2]{1,4,2,3,0,5:T(8,128)(2,1)S(1)} %get-tuple-element.18), kind=kOutput, calls=%fused_computation.17 | convolution fusion | flops 536936448 | bytes 8421376 | tf_op jit(solution)/shard_map/tcarbm,dktcab->rdkm/dot_general | solution.py:209
  47.8 0.0 slice-start
  47.8 10.3 %fusion.5 = f32[128,2,64,2,64]{4,2,3,1,0:T(8,128)} fusion(bf16[2,64,128,128,1,1,1]{3,1,6,5,2,0,4:T(8,128)(2,1)S(1)} %fusion.8), kind=kOutput, calls=%fused_computation.14 | convolution fusion | flops 536870912 | bytes 12582912 | tf_op jit(solution)/shard_map/rdkm,relm->rdkel/dot_general | solution.py:212
  58.0 0.0 slice-done
  58.0 4.1 %fusion.12 = f32[128,2,64,1,2,16,2]{2,5,6,4,1,0,3:T(8,128)S(1)} fusion(bf16[2,16,128,2,128,1]{4,3,2,1,0,5:T(2,128)(2,1)S(1)} %bitcast.135, bf16[2,64,128,128,1,1,1]{3,1,6,5,2,0,4:T(8,128)(2,1)S(1)} %fusion.8), kind=kOutput, calls=%fused_computation.19 | convolution fusion | flops 268435456 | bytes 10485760 | tf_op jit(solution)/shard_map/rdkm,tcarbm->rdktcab/dot_general | solution.py:219
  62.1 2.6 %slice_add_fusion.1 = (f32[128,1,64,1,1,16,2]{2,5,6,4,1,0,3:T(8,128)}, f32[128,1,64,1,1,16,2]{2,5,6,4,1,0,3:T(8,128)S(1)}) fusion(f32[128,2,64,1,2,16,2]{2,5,6,4,1,0,3:T(8,128)S(1)} %fusion.12), kind=kLoop, calls=%fused_computation.21 | loop fusion | flops 524288 | bytes 6291456 | tf_op jit(solution)/shard_map/add | solution.py:222
  64.7 1.2 copy.76
  66.0 2.7 %copy.78 = f32[8,2,8,64,32]{4,3,2,1,0:T(8,128)} copy(f32[8,2,8,64,32]{3,2,1,0,4:T(8,128)S(1)} %bitcast.138) | data formatting | bytes 2097152 | tf_op jit(solution)/shard_map/sub | solution.py:223
  68.7 2.8 %copy.75 = f32[128,1,64,1,1,16,2]{2,0,6,5,4,3,1:T(8,128)S(1)} copy(f32[128,1,64,1,1,16,2]{2,5,6,4,1,0,3:T(8,128)} %get-tuple-element.11) | data formatting | bytes 2097152 | tf_op jit(solution)/shard_map/add | solution.py:222
  71.5 2.8 %copy.77 = f32[8,2,8,64,32]{4,3,2,1,0:T(8,128)} copy(f32[8,2,8,64,32]{3,2,1,0,4:T(8,128)S(1)} %bitcast.139) | data formatting | bytes 2097152 | tf_op jit(solution)/shard_map/add | solution.py:222
  74.3 12.1 %slice_subtract_fusion = (f32[128,1,64,1,64]{4,2,3,1,0:T(8,128)}, f32[128,1,64,1,64]{4,2,3,1,0:T(8,128)}) fusion(f32[128,2,64,2,64]{4,2,3,1,0:T(8,128)} %fusion.5), kind=kLoop, calls=%fused_computation.9 | loop fusion | flops 1048576 | bytes 12582912 | tf_op jit(solution)/shard_map/sub | solution.py:214
  86.5 4.6 %broadcast_select_fusion = f32[8,2,8,64,64]{4,3,2,1,0:T(8,128)S(1)} fusion(f32[8,2,8,64,64]{4,3,2,1,0:T(8,128)} %bitcast.134, f32[8,2,8,64,64]{4,3,2,1,0:T(8,128)} %bitcast.133, pred[64,64]{1,0:T(8,128)(4,1)S(1)} %iota_compare_fusion.3), kind=kLoop, calls=%fused_computation.25 | loop fusion | flops 524288 | bytes 6295552 | tf_op jit(solution)/shard_map/jit(_where)/select_n | solution.py:218
  91.1 0.0 copy-done.1
  91.1 1.3 copy-done.2
  92.4 2.2 %pad_maximum_fusion.1 = f32[8,2,8,64,128]{4,3,2,1,0:T(8,128)S(1)} fusion(f32[8,2,8,64,32]{4,3,2,1,0:T(8,128)S(1)} %copy-done.1, f32[8,2,8,64,32]{4,3,2,1,0:T(8,128)S(1)} %copy-done.2, f32[8,2,8,64,64]{4,3,2,1,0:T(8,128)S(1)} %broadcast_select_fusion), kind=kLoop, calls=%fused_computation.11 | loop fusion | flops 2097152 | bytes 8388608 | tf_op jit(solution)/shard_map/concatenate | solution.py:227
  94.6 0.0 copy-start
  94.6 1.9 copy-done
  96.6 0.2 dynamic-slice_bitcast_fusion
  96.8 0.5 collective-permute-start
  97.3 3.9 %collective-permute-done = f32[8,8,64,128]{3,2,1,0:T(8,128)} collective-permute-done((f32[8,8,64,128]{3,2,1,0:T(8,128)S(1)}, f32[8,8,64,128]{3,2,1,0:T(8,128)}, u32[]{:S(2)}, u32[]{:S(2)}) %collective-permute-start) | collective-permute-done | bytes 2097184 | tf_op jit(solution)/shard_map/ppermute | solution.py:255
  101.2 2.6 %bitcast_add_fusion = f32[8,8,64,128]{3,2,1,0:T(8,128)S(1)} fusion(f32[8,8,64,128]{3,2,1,0:T(8,128)} %collective-permute-done, f32[8,2,8,64,128]{4,3,2,1,0:T(8,128)} %copy-done, s32[]{:T(128)S(6)} %select_n.144), kind=kLoop, calls=%fused_computation.22 | loop fusion | flops 524288 | bytes 6291460 | tf_op jit(solution)/shard_map/add | solution.py:255
  103.8 0.0 copy-start.7
  103.8 0.0 copy-start.4
  103.8 0.0 copy-start.6
  103.9 0.1 dynamic-slice_bitcast_fusion.1
  104.0 3.0 %collective-permute-start.1 = (f32[4,8,64,128]{3,2,1,0:T(8,128)S(1)}, f32[4,8,64,128]{3,2,1,0:T(8,128)}, u32[]{:S(2)}, u32[]{:S(2)}) collective-permute-start(f32[4,8,64,128]{3,2,1,0:T(8,128)S(1)} %dynamic-slice_bitcast_fusion.1), channel_id=1, source_target_pairs={{0,2},{1,3},{2,0},{3,1},{4,6},{5,7},{6,4},{7,5},{8,10},{9,11},{10,... | collective-permute-start | bytes 3145736 | tf_op jit(solution)/shard_map/ppermute | solution.py:255
  107.0 23.6 %collective-permute-done.1 = f32[4,8,64,128]{3,2,1,0:T(8,128)} collective-permute-done((f32[4,8,64,128]{3,2,1,0:T(8,128)S(1)}, f32[4,8,64,128]{3,2,1,0:T(8,128)}, u32[]{:S(2)}, u32[]{:S(2)}) %collective-permute-start.1) | collective-permute-done | bytes 1048608 | tf_op jit(solution)/shard_map/ppermute | solution.py:255
  130.5 1.4 bitcast_add_fusion.1
  131.9 0.1 dynamic-slice_bitcast_fusion.2
  131.9 1.8 collective-permute-start.2
  133.8 11.7 %collective-permute-done.2 = f32[2,8,64,128]{3,2,1,0:T(8,128)S(1)} collective-permute-done((f32[2,8,64,128]{3,2,1,0:T(8,128)S(1)}, f32[2,8,64,128]{3,2,1,0:T(8,128)S(1)}, u32[]{:S(2)}, u32[]{:S(2)}) %collective-permute-start.2) | collective-permute-done | bytes 524320 | tf_op jit(solution)/shard_map/ppermute | solution.py:255
  145.5 0.1 bitcast_add_fusion.2
  145.6 2.5 %collective-permute-start.3 = (f32[1,8,64,128]{3,2,1,0:T(8,128)S(1)}, f32[1,8,64,128]{3,2,1,0:T(8,128)S(1)}, u32[]{:S(2)}, u32[]{:S(2)}) collective-permute-start(f32[1,8,64,128]{3,2,1,0:T(8,128)S(1)} %constant_dynamic-slice_fusion), channel_id=1, source_target_pairs={{0,8},{1,9},{2,10},{3,11},{4,12},{5,13},{6,14},{7,15},{8,0},{9,1},... | collective-permute-start | bytes 786440 | tf_op jit(solution)/shard_map/ppermute | solution.py:255
  148.1 11.0 %collective-permute-done.3 = f32[1,8,64,128]{3,2,1,0:T(8,128)S(1)} collective-permute-done((f32[1,8,64,128]{3,2,1,0:T(8,128)S(1)}, f32[1,8,64,128]{3,2,1,0:T(8,128)S(1)}, u32[]{:S(2)}, u32[]{:S(2)}) %collective-permute-start.3) | collective-permute-done | bytes 262176 | tf_op jit(solution)/shard_map/ppermute | solution.py:255
  159.1 0.1 copy.79
  159.3 0.3 fusion.25
  159.5 0.8 pad_maximum_fusion.2.b_ref
  160.4 0.2 fusion.59
  160.6 1.0 maximum_maximum_fusion.a_ref
  161.6 37.0 %shard_map.55 = f32[8,128,32]{2,1,0:T(8,128)} custom-call(f32[8,128,128]{2,1,0:T(8,128)} %maximum_maximum_fusion.a_ref, f32[8,128,32]{2,1,0:T(8,128)} %pad_maximum_fusion.2.b_ref), custom_call_target="tpu_custom_call" | custom-call | tf_op jit(solution)/shard_map/pallas_call | solution.py:94
  198.6 1.2 copy.80
  199.8 0.2 reshape.378
  200.0 0.1 copy.82
  200.1 13.1 %all_to_all.18 = f32[64,1,2,256]{3,2,1,0:T(2,128)S(1)} all-to-all(f32[64,1,2,256]{3,2,1,0:T(2,128)S(1)} %copy.82), channel_id=1, replica_groups=mesh['cells'=2,'fh'=16] {'fh'}, dimensions={0} | all-to-all | bytes 262144 | tf_op jit(solution)/shard_map/all_to_all | solution.py:269
  213.2 0.7 copy.100
  (18 shorter events, 0.2 us)
Async XLA Ops:
  39.0 2.7 %copy-start.3 = (bf16[3,2,16,256,128]{4,3,2,0,1:T(8,128)(2,1)}, bf16[3,2,16,256,128]{4,3,2,0,1:T(8,128)(2,1)S(1)}, u32[]{:S(2)}) copy-start(bf16[3,2,16,256,128]{4,3,2,0,1:T(8,128)(2,1)S(1)} %fusion) | copy-start | bytes 18874372
  39.0 2.8 %copy-start.5 = (s32[64]{0:T(128)S(1)}, s32[64]{0:T(128)}, u32[]{:S(2)}) copy-start(s32[64]{0:T(128)} %param.6) | copy-start | bytes 772
  47.8 10.3 %slice-start = ((bf16[3,2,16,256,128]{4,3,2,0,1:T(8,128)(2,1)}), bf16[1,2,16,256,128]{4,3,2,0,1:T(8,128)(2,1)S(1)}, s32[]{:S(2)}) async-start(bf16[3,2,16,256,128]{4,3,2,0,1:T(8,128)(2,1)} %copy-done.3), calls=%async_computation.1 | async-start | bytes 4194304 | tf_op jit(solution)/shard_map/slice | solution.py:263
  86.5 4.6 %copy-start.1 = (f32[8,2,8,64,32]{4,3,2,1,0:T(8,128)S(1)}, f32[8,2,8,64,32]{4,3,2,1,0:T(8,128)}, u32[]{:S(2)}) copy-start(f32[8,2,8,64,32]{4,3,2,1,0:T(8,128)} %copy.78) | copy-start | bytes 3145732
  86.5 5.9 %copy-start.2 = (f32[8,2,8,64,32]{4,3,2,1,0:T(8,128)S(1)}, f32[8,2,8,64,32]{4,3,2,1,0:T(8,128)}, u32[]{:S(2)}) copy-start(f32[8,2,8,64,32]{4,3,2,1,0:T(8,128)} %copy.77) | copy-start | bytes 3145732
  94.6 1.9 copy-start
  96.8 4.4 %collective-permute-start = (f32[8,8,64,128]{3,2,1,0:T(8,128)S(1)}, f32[8,8,64,128]{3,2,1,0:T(8,128)}, u32[]{:S(2)}, u32[]{:S(2)}) collective-permute-start(f32[8,8,64,128]{3,2,1,0:T(8,128)S(1)} %dynamic-slice_bitcast_fusion), channel_id=1, source_target_pairs={{0,1},{1,0},{2,3},{3,2},{4,5},{5,4},{6,7},{7,6},{8,9},{9,8},{10,11... | collective-permute-start | bytes 6291464 | tf_op jit(solution)/shard_map/ppermute | solution.py:255
  103.8 30.0 %copy-start.7 = (s32[64]{0:T(128)S(1)}, s32[64]{0:T(128)}, u32[]{:S(2)}) copy-start(s32[64]{0:T(128)} %param.7) | copy-start | bytes 772
  103.8 30.0 %copy-start.4 = (s32[8,64]{1,0:T(8,128)S(1)}, s32[8,64]{1,0:T(8,128)}, u32[]{:S(2)}) copy-start(s32[8,64]{1,0:T(8,128)} %param.8) | copy-start | bytes 6148
  103.8 44.3 %copy-start.6 = (f32[64]{0:T(128)S(1)}, f32[64]{0:T(128)}, u32[]{:S(2)}) copy-start(f32[64]{0:T(128)} %param.9) | copy-start | bytes 772
  104.0 26.5 %collective-permute-start.1 = (f32[4,8,64,128]{3,2,1,0:T(8,128)S(1)}, f32[4,8,64,128]{3,2,1,0:T(8,128)}, u32[]{:S(2)}, u32[]{:S(2)}) collective-permute-start(f32[4,8,64,128]{3,2,1,0:T(8,128)S(1)} %dynamic-slice_bitcast_fusion.1), channel_id=1, source_target_pairs={{0,2},{1,3},{2,0},{3,1},{4,6},{5,7},{6,4},{7,5},{8,10},{9,11},{10,... | collective-permute-start | bytes 3145736 | tf_op jit(solution)/shard_map/ppermute | solution.py:255
  131.9 13.5 %collective-permute-start.2 = (f32[2,8,64,128]{3,2,1,0:T(8,128)S(1)}, f32[2,8,64,128]{3,2,1,0:T(8,128)S(1)}, u32[]{:S(2)}, u32[]{:S(2)}) collective-permute-start(f32[2,8,64,128]{3,2,1,0:T(8,128)S(1)} %dynamic-slice_bitcast_fusion.2), channel_id=1, source_target_pairs={{0,4},{1,5},{2,6},{3,7},{4,0},{5,1},{6,2},{7,3},{8,12},{9,13},{10,... | collective-permute-start | bytes 1572872 | tf_op jit(solution)/shard_map/ppermute | solution.py:255
  145.6 13.5 %collective-permute-start.3 = (f32[1,8,64,128]{3,2,1,0:T(8,128)S(1)}, f32[1,8,64,128]{3,2,1,0:T(8,128)S(1)}, u32[]{:S(2)}, u32[]{:S(2)}) collective-permute-start(f32[1,8,64,128]{3,2,1,0:T(8,128)S(1)} %constant_dynamic-slice_fusion), channel_id=1, source_target_pairs={{0,8},{1,9},{2,10},{3,11},{4,12},{5,13},{6,14},{7,15},{8,0},{9,1},... | collective-permute-start | bytes 786440 | tf_op jit(solution)/shard_map/ppermute | solution.py:255

commit v6 on v5

--- a/solution.py
+++ b/solution.py
@@ -38,10 +38,10 @@
             keep = lane >= j
             for b in range(nb):
                 pivot_row = rows[b][t:t + 1, :]
-                d = jnp.sum(jnp.where(hit, pivot_row, 0.0), axis=1, keepdims=True)
-                inv = 1.0 / jnp.sqrt(d)
+                column = jnp.sum(jnp.where(hit, rows[b], 0.0), axis=1, keepdims=True)
+                inv = 1.0 / jnp.sqrt(column[t:t + 1, :])
                 l = jnp.where(keep, pivot_row, 0.0) * inv
-                col = jnp.sum(jnp.where(hit, rows[b], 0.0), axis=1, keepdims=True) * inv
+                col = column * inv
                 rows[b] = rows[b] - col * l
                 y = sides[b][t:t + 1, :] * inv
                 sides[b] = sides[b] - col * y
@@ -73,12 +73,12 @@
                 block, x_ref[b], precision=PREC, preferred_element_type=jnp.float32)
             blocks.append(block)
             rests.append(rest)
-            diags.append(jnp.sum(jnp.where(lane == j0 + sub, block, 0.0), axis=1, keepdims=True))
+            diags.append(1.0 / jnp.sum(jnp.where(lane == j0 + sub, block, 0.0), axis=1, keepdims=True))
         outs = [[None] * PANEL for _ in range(nb)]
         for t in reversed(range(PANEL)):
             hit = lane == j0 + t
             for b in range(nb):
-                xt = rests[b][t:t + 1, :] / diags[b][t:t + 1, :]
+                xt = rests[b][t:t + 1, :] * diags[b][t:t + 1, :]
                 col = jnp.sum(jnp.where(hit, blocks[b], 0.0), axis=1, keepdims=True)
                 rests[b] = rests[b] - col * xt
                 outs[b][t] = xt

time: 215 us -> 212 us (0.986)
  Pallas kernels: 37 us -> 33.9 us
    pallas_call x1, Pallas kernels: 37 us -> 33.9 us  [spd_solve(): pl.pallas_call(_solve_body, out_shape=jax.ShapeDtypeStruct(rhs.shape, jnp...]
where the time goes in v6:
time: 212 us; the launch traced here: 211 us
  waiting for transfers between devices  50.1 us (24%)
  local copies, waits for them, and re-layouts  38.2 us (18%)
  other arithmetic  36.1 us (17%)
  Pallas kernels  33.9 us (16%)
  matrix products  31.3 us (15%)
  blocking collectives  13.1 us (6%)
  starting transfers between devices  7.83 us (4%)
    ppermute x4, waiting for transfers between devices, halving_reduce_scatter(): parts = keep + lax.ppermute(send, 'fh', perm=pairs)  50.1 us
    pallas_call x1, Pallas kernels, spd_solve(): pl.pallas_call(_solve_body, out_shape=jax.ShapeDtypeStruct(rhs.shape, jnp...  33.9 us
    all_to_all x1, blocking collectives, on_device(): return lax.all_to_all(result, 'fh', split_axis=0, concat_axis=3, tiled=True)  13.1 us
    sub x1, other arithmetic, packed_terms(): gram_imag = gram[:, 0, :, 1] - gram[:, 1, :, 0]  12.1 us
    reshape x1, local copies, waits for them, and re-layouts, spectra(): shaped = samples.reshape(antennas_here, symbol_count, 2, FA, FB)  10.8 us
    dot_general x1, matrix products, packed_terms(): jnp.einsum('rdkm,relm->rdkel', channel, channel, preferred_element_type=j...  10.3 us
    another operation x1, local copies, waits for them, and re-layouts, spectra(): section_one = jnp.stack([real_part, imag_part], 1).astype(jnp.bfloat16)  9.13 us
    ppermute x4, starting transfers between devices, halving_reduce_scatter(): parts = keep + lax.ppermute(send, 'fh', perm=pairs)  7.83 us
  transfers between devices with their start and end apart: 4, of which 4 were waited for; matrix products, arithmetic and copies ran while one was open for 0% of the time, Pallas kernels for 0%

profile of v6, /device:TPU:0, one launch (start us, length us, event | category | flops | bytes accessed | tf_op | source)
XLA Modules:
  0.0 210.9 jit_solution(5903164692260749690)
XLA Ops:
  0.0 0.1 negate_convert_fusion.2
  0.1 0.1 fusion.55
  0.1 0.1 sine_multiply_fusion.1
  0.2 1.1 negate_convert_fusion
  1.3 1.0 fusion.32
  2.3 10.8 %reshape.381 = bf16[128,3,2,16,256,1]{4,3,2,1,0,5:T(8,128)(2,1)} reshape(bf16[128,3,2,4096]{3,2,1,0:T(2,128)(2,1)} %param.5) | data formatting | bytes 12582912 | tf_op jit(solution)/shard_map/reshape | solution.py:128
  13.1 4.7 %convolution_bitcast_fusion = f32[3,2,16,256,128]{3,2,0,4,1:T(8,128)S(1)} fusion(bf16[128,3,2,16,256,1]{4,3,2,1,0,5:T(8,128)(2,1)} %reshape.381, bf16[1,16,2,16]{1,3,0,2:T(8,128)(2,1)S(1)} %get-tuple-element.21, bf16[1,16,2,16]{1,3,0,2:T(8,128)(2,1)S(1)} %get-tuple-element.20), kind=kOutput, calls=%fused_computation.8 | convolution fusion | flops 201330688 | bytes 18876416 | tf_op jit(solution)/shard_map/ascnm,cndk->sdkma/dot_general | solution.py:129
  17.8 2.2 %add_convert_fusion = (bf16[3,1,16,256,128]{3,2,0,4,1:T(8,128)(2,1)S(1)}, bf16[3,1,16,256,128]{3,2,0,4,1:T(8,128)(2,1)S(1)}) fusion(f32[3,2,16,256,128]{3,2,0,4,1:T(8,128)S(1)} %convolution_bitcast_fusion, f32[16,256]{1,0:T(8,128)S(1)} %get-tuple-element.27, f32[16,256]{1,0:T(8,128)S(1)} %get-tuple-element.28), kind=kLoop, calls=%fused_computation.7 | loop fusion | flops 12582912 | bytes 18907136 | tf_op jit(solution)/shard_map/convert
  20.0 3.2 %pad_maximum_fusion = bf16[3,2,16,256,128]{3,2,0,4,1:T(8,128)(2,1)} fusion(bf16[3,1,16,256,128]{3,2,0,4,1:T(8,128)(2,1)S(1)} %get-tuple-element.10, bf16[3,1,16,256,128]{3,2,0,4,1:T(8,128)(2,1)S(1)} %get-tuple-element.9), kind=kLoop, calls=%fused_computation.3 | loop fusion | flops 3145728 | bytes 12582912 | tf_op jit(solution)/shard_map/stack | solution.py:137
  23.2 9.1 %copy.72 = bf16[3,2,16,256,128]{4,3,1,2,0:T(8,128)(2,1)} copy(bf16[3,2,16,256,128]{3,2,0,4,1:T(8,128)(2,1)} %pad_maximum_fusion) | data formatting | bytes 12582912 | tf_op jit(solution)/shard_map/stack | solution.py:137
  32.4 6.6 %fusion = bf16[3,2,16,256,128]{4,3,2,0,1:T(8,128)(2,1)S(1)} fusion(bf16[3,2,16,256,128]{4,3,1,2,0:T(8,128)(2,1)} %copy.72, bf16[1,256,2,256]{1,3,0,2:T(8,128)(2,1)S(1)} %get-tuple-element.17, bf16[1,256,2,256]{1,3,0,2:T(8,128)(2,1)S(1)} %get-tuple-element.16), kind=kOutput, calls=%fused_computation.2 | convolution fusion | flops 3225419776 | bytes 13107200 | tf_op jit(solution)/shard_map/sckma,cmdj->sdkja/dot_general | solution.py:138
  39.0 0.0 copy-start.3
  39.0 0.0 copy-start.5
  39.0 0.3 slice.64
  39.3 2.4 %copy-done.3 = bf16[3,2,16,256,128]{4,3,2,0,1:T(8,128)(2,1)} copy-done((bf16[3,2,16,256,128]{4,3,2,0,1:T(8,128)(2,1)}, bf16[3,2,16,256,128]{4,3,2,0,1:T(8,128)(2,1)S(1)}, u32[]{:S(2)}) %copy-start.3) | copy-done | bytes 6291480
  41.7 0.1 iota_add_fusion
  41.8 0.1 broadcast_add_fusion
  41.8 0.0 copy-done.5
  41.8 0.2 fusion.39
  42.1 5.7 %fusion.8 = bf16[2,64,128,128,1,1,1]{3,1,6,5,2,0,4:T(8,128)(2,1)S(1)} fusion(bf16[2,2,16,128,2,128,1]{5,4,3,2,0,1,6:T(2,128)(2,1)S(1)} %bitcast.132, bf16[1,64,2,2,16,2]{1,4,2,3,0,5:T(8,128)(2,1)S(1)} %get-tuple-element.19, bf16[1,64,2,2,16,2]{1,4,2,3,0,5:T(8,128)(2,1)S(1)} %get-tuple-element.18), kind=kOutput, calls=%fused_computation.17 | convolution fusion | flops 536936448 | bytes 8421376 | tf_op jit(solution)/shard_map/tcarbm,dktcab->rdkm/dot_general | solution.py:209
  47.8 0.0 slice-start
  47.8 10.3 %fusion.5 = f32[128,2,64,2,64]{4,2,3,1,0:T(8,128)} fusion(bf16[2,64,128,128,1,1,1]{3,1,6,5,2,0,4:T(8,128)(2,1)S(1)} %fusion.8), kind=kOutput, calls=%fused_computation.14 | convolution fusion | flops 536870912 | bytes 12582912 | tf_op jit(solution)/shard_map/rdkm,relm->rdkel/dot_general | solution.py:212
  58.0 0.0 slice-done
  58.0 4.1 %fusion.12 = f32[128,2,64,1,2,16,2]{2,5,6,4,1,0,3:T(8,128)S(1)} fusion(bf16[2,16,128,2,128,1]{4,3,2,1,0,5:T(2,128)(2,1)S(1)} %bitcast.135, bf16[2,64,128,128,1,1,1]{3,1,6,5,2,0,4:T(8,128)(2,1)S(1)} %fusion.8), kind=kOutput, calls=%fused_computation.19 | convolution fusion | flops 268435456 | bytes 10485760 | tf_op jit(solution)/shard_map/rdkm,tcarbm->rdktcab/dot_general | solution.py:219
  62.1 2.6 %slice_add_fusion.1 = (f32[128,1,64,1,1,16,2]{2,5,6,4,1,0,3:T(8,128)}, f32[128,1,64,1,1,16,2]{2,5,6,4,1,0,3:T(8,128)S(1)}) fusion(f32[128,2,64,1,2,16,2]{2,5,6,4,1,0,3:T(8,128)S(1)} %fusion.12), kind=kLoop, calls=%fused_computation.21 | loop fusion | flops 524288 | bytes 6291456 | tf_op jit(solution)/shard_map/add | solution.py:222
  64.7 1.2 copy.76
  66.0 2.7 %copy.78 = f32[8,2,8,64,32]{4,3,2,1,0:T(8,128)} copy(f32[8,2,8,64,32]{3,2,1,0,4:T(8,128)S(1)} %bitcast.138) | data formatting | bytes 2097152 | tf_op jit(solution)/shard_map/sub | solution.py:223
  68.7 2.8 %copy.75 = f32[128,1,64,1,1,16,2]{2,0,6,5,4,3,1:T(8,128)S(1)} copy(f32[128,1,64,1,1,16,2]{2,5,6,4,1,0,3:T(8,128)} %get-tuple-element.11) | data formatting | bytes 2097152 | tf_op jit(solution)/shard_map/add | solution.py:222
  71.5 2.8 %copy.77 = f32[8,2,8,64,32]{4,3,2,1,0:T(8,128)} copy(f32[8,2,8,64,32]{3,2,1,0,4:T(8,128)S(1)} %bitcast.139) | data formatting | bytes 2097152 | tf_op jit(solution)/shard_map/add | solution.py:222
  74.3 12.1 %slice_subtract_fusion = (f32[128,1,64,1,64]{4,2,3,1,0:T(8,128)}, f32[128,1,64,1,64]{4,2,3,1,0:T(8,128)}) fusion(f32[128,2,64,2,64]{4,2,3,1,0:T(8,128)} %fusion.5), kind=kLoop, calls=%fused_computation.9 | loop fusion | flops 1048576 | bytes 12582912 | tf_op jit(solution)/shard_map/sub | solution.py:214
  86.5 4.6 %broadcast_select_fusion = f32[8,2,8,64,64]{4,3,2,1,0:T(8,128)S(1)} fusion(f32[8,2,8,64,64]{4,3,2,1,0:T(8,128)} %bitcast.134, f32[8,2,8,64,64]{4,3,2,1,0:T(8,128)} %bitcast.133, pred[64,64]{1,0:T(8,128)(4,1)S(1)} %iota_compare_fusion.3), kind=kLoop, calls=%fused_computation.25 | loop fusion | flops 524288 | bytes 6295552 | tf_op jit(solution)/shard_map/jit(_where)/select_n | solution.py:218
  91.1 0.0 copy-done.1
  91.1 1.3 copy-done.2
  92.4 2.2 %pad_maximum_fusion.1 = f32[8,2,8,64,128]{4,3,2,1,0:T(8,128)S(1)} fusion(f32[8,2,8,64,32]{4,3,2,1,0:T(8,128)S(1)} %copy-done.1, f32[8,2,8,64,32]{4,3,2,1,0:T(8,128)S(1)} %copy-done.2, f32[8,2,8,64,64]{4,3,2,1,0:T(8,128)S(1)} %broadcast_select_fusion), kind=kLoop, calls=%fused_computation.11 | loop fusion | flops 2097152 | bytes 8388608 | tf_op jit(solution)/shard_map/concatenate | solution.py:227
  94.6 0.0 copy-start
  94.6 1.9 copy-done
  96.6 0.2 dynamic-slice_bitcast_fusion
  96.8 0.5 collective-permute-start
  97.3 3.9 %collective-permute-done = f32[8,8,64,128]{3,2,1,0:T(8,128)} collective-permute-done((f32[8,8,64,128]{3,2,1,0:T(8,128)S(1)}, f32[8,8,64,128]{3,2,1,0:T(8,128)}, u32[]{:S(2)}, u32[]{:S(2)}) %collective-permute-start) | collective-permute-done | bytes 2097184 | tf_op jit(solution)/shard_map/ppermute | solution.py:255
  101.2 2.6 %bitcast_add_fusion = f32[8,8,64,128]{3,2,1,0:T(8,128)S(1)} fusion(f32[8,8,64,128]{3,2,1,0:T(8,128)} %collective-permute-done, f32[8,2,8,64,128]{4,3,2,1,0:T(8,128)} %copy-done, s32[]{:T(128)S(6)} %select_n.144), kind=kLoop, calls=%fused_computation.22 | loop fusion | flops 524288 | bytes 6291460 | tf_op jit(solution)/shard_map/add | solution.py:255
  103.8 0.0 copy-start.7
  103.8 0.0 copy-start.4
  103.8 0.0 copy-start.6
  103.9 0.1 dynamic-slice_bitcast_fusion.1
  104.0 3.0 %collective-permute-start.1 = (f32[4,8,64,128]{3,2,1,0:T(8,128)S(1)}, f32[4,8,64,128]{3,2,1,0:T(8,128)}, u32[]{:S(2)}, u32[]{:S(2)}) collective-permute-start(f32[4,8,64,128]{3,2,1,0:T(8,128)S(1)} %dynamic-slice_bitcast_fusion.1), channel_id=1, source_target_pairs={{0,2},{1,3},{2,0},{3,1},{4,6},{5,7},{6,4},{7,5},{8,10},{9,11},{10,... | collective-permute-start | bytes 3145736 | tf_op jit(solution)/shard_map/ppermute | solution.py:255
  107.0 23.6 %collective-permute-done.1 = f32[4,8,64,128]{3,2,1,0:T(8,128)} collective-permute-done((f32[4,8,64,128]{3,2,1,0:T(8,128)S(1)}, f32[4,8,64,128]{3,2,1,0:T(8,128)}, u32[]{:S(2)}, u32[]{:S(2)}) %collective-permute-start.1) | collective-permute-done | bytes 1048608 | tf_op jit(solution)/shard_map/ppermute | solution.py:255
  130.5 1.4 bitcast_add_fusion.1
  131.9 0.1 dynamic-slice_bitcast_fusion.2
  131.9 1.8 collective-permute-start.2
  133.8 11.7 %collective-permute-done.2 = f32[2,8,64,128]{3,2,1,0:T(8,128)S(1)} collective-permute-done((f32[2,8,64,128]{3,2,1,0:T(8,128)S(1)}, f32[2,8,64,128]{3,2,1,0:T(8,128)S(1)}, u32[]{:S(2)}, u32[]{:S(2)}) %collective-permute-start.2) | collective-permute-done | bytes 524320 | tf_op jit(solution)/shard_map/ppermute | solution.py:255
  145.5 0.1 bitcast_add_fusion.2
  145.6 2.5 %collective-permute-start.3 = (f32[1,8,64,128]{3,2,1,0:T(8,128)S(1)}, f32[1,8,64,128]{3,2,1,0:T(8,128)S(1)}, u32[]{:S(2)}, u32[]{:S(2)}) collective-permute-start(f32[1,8,64,128]{3,2,1,0:T(8,128)S(1)} %constant_dynamic-slice_fusion), channel_id=1, source_target_pairs={{0,8},{1,9},{2,10},{3,11},{4,12},{5,13},{6,14},{7,15},{8,0},{9,1},... | collective-permute-start | bytes 786440 | tf_op jit(solution)/shard_map/ppermute | solution.py:255
  148.1 11.0 %collective-permute-done.3 = f32[1,8,64,128]{3,2,1,0:T(8,128)S(1)} collective-permute-done((f32[1,8,64,128]{3,2,1,0:T(8,128)S(1)}, f32[1,8,64,128]{3,2,1,0:T(8,128)S(1)}, u32[]{:S(2)}, u32[]{:S(2)}) %collective-permute-start.3) | collective-permute-done | bytes 262176 | tf_op jit(solution)/shard_map/ppermute | solution.py:255
  159.1 0.1 copy.79
  159.3 0.3 fusion.25
  159.5 0.8 pad_maximum_fusion.2.b_ref
  160.4 0.2 fusion.59
  160.6 1.0 maximum_maximum_fusion.a_ref
  161.6 33.9 %shard_map.55 = f32[8,128,32]{2,1,0:T(8,128)} custom-call(f32[8,128,128]{2,1,0:T(8,128)} %maximum_maximum_fusion.a_ref, f32[8,128,32]{2,1,0:T(8,128)} %pad_maximum_fusion.2.b_ref), custom_call_target="tpu_custom_call" | custom-call | tf_op jit(solution)/shard_map/pallas_call | solution.py:94
  195.5 1.2 copy.80
  196.7 0.2 reshape.378
  197.0 0.1 copy.82
  197.1 13.1 %all_to_all.18 = f32[64,1,2,256]{3,2,1,0:T(2,128)S(1)} all-to-all(f32[64,1,2,256]{3,2,1,0:T(2,128)S(1)} %copy.82), channel_id=1, replica_groups=mesh['cells'=2,'fh'=16] {'fh'}, dimensions={0} | all-to-all | bytes 262144 | tf_op jit(solution)/shard_map/all_to_all | solution.py:269
  210.2 0.7 copy.100
  (18 shorter events, 0.2 us)
Async XLA Ops:
  39.0 2.7 %copy-start.3 = (bf16[3,2,16,256,128]{4,3,2,0,1:T(8,128)(2,1)}, bf16[3,2,16,256,128]{4,3,2,0,1:T(8,128)(2,1)S(1)}, u32[]{:S(2)}) copy-start(bf16[3,2,16,256,128]{4,3,2,0,1:T(8,128)(2,1)S(1)} %fusion) | copy-start | bytes 18874372
  39.0 2.8 %copy-start.5 = (s32[64]{0:T(128)S(1)}, s32[64]{0:T(128)}, u32[]{:S(2)}) copy-start(s32[64]{0:T(128)} %param.6) | copy-start | bytes 772
  47.8 10.3 %slice-start = ((bf16[3,2,16,256,128]{4,3,2,0,1:T(8,128)(2,1)}), bf16[1,2,16,256,128]{4,3,2,0,1:T(8,128)(2,1)S(1)}, s32[]{:S(2)}) async-start(bf16[3,2,16,256,128]{4,3,2,0,1:T(8,128)(2,1)} %copy-done.3), calls=%async_computation.1 | async-start | bytes 4194304 | tf_op jit(solution)/shard_map/slice | solution.py:263
  86.5 4.6 %copy-start.1 = (f32[8,2,8,64,32]{4,3,2,1,0:T(8,128)S(1)}, f32[8,2,8,64,32]{4,3,2,1,0:T(8,128)}, u32[]{:S(2)}) copy-start(f32[8,2,8,64,32]{4,3,2,1,0:T(8,128)} %copy.78) | copy-start | bytes 3145732
  86.5 5.9 %copy-start.2 = (f32[8,2,8,64,32]{4,3,2,1,0:T(8,128)S(1)}, f32[8,2,8,64,32]{4,3,2,1,0:T(8,128)}, u32[]{:S(2)}) copy-start(f32[8,2,8,64,32]{4,3,2,1,0:T(8,128)} %copy.77) | copy-start | bytes 3145732
  94.6 1.9 copy-start
  96.8 4.4 %collective-permute-start = (f32[8,8,64,128]{3,2,1,0:T(8,128)S(1)}, f32[8,8,64,128]{3,2,1,0:T(8,128)}, u32[]{:S(2)}, u32[]{:S(2)}) collective-permute-start(f32[8,8,64,128]{3,2,1,0:T(8,128)S(1)} %dynamic-slice_bitcast_fusion), channel_id=1, source_target_pairs={{0,1},{1,0},{2,3},{3,2},{4,5},{5,4},{6,7},{7,6},{8,9},{9,8},{10,11... | collective-permute-start | bytes 6291464 | tf_op jit(solution)/shard_map/ppermute | solution.py:255
  103.8 30.0 %copy-start.7 = (s32[64]{0:T(128)S(1)}, s32[64]{0:T(128)}, u32[]{:S(2)}) copy-start(s32[64]{0:T(128)} %param.7) | copy-start | bytes 772
  103.8 30.0 %copy-start.4 = (s32[8,64]{1,0:T(8,128)S(1)}, s32[8,64]{1,0:T(8,128)}, u32[]{:S(2)}) copy-start(s32[8,64]{1,0:T(8,128)} %param.8) | copy-start | bytes 6148
  103.8 44.3 %copy-start.6 = (f32[64]{0:T(128)S(1)}, f32[64]{0:T(128)}, u32[]{:S(2)}) copy-start(f32[64]{0:T(128)} %param.9) | copy-start | bytes 772
  104.0 26.5 %collective-permute-start.1 = (f32[4,8,64,128]{3,2,1,0:T(8,128)S(1)}, f32[4,8,64,128]{3,2,1,0:T(8,128)}, u32[]{:S(2)}, u32[]{:S(2)}) collective-permute-start(f32[4,8,64,128]{3,2,1,0:T(8,128)S(1)} %dynamic-slice_bitcast_fusion.1), channel_id=1, source_target_pairs={{0,2},{1,3},{2,0},{3,1},{4,6},{5,7},{6,4},{7,5},{8,10},{9,11},{10,... | collective-permute-start | bytes 3145736 | tf_op jit(solution)/shard_map/ppermute | solution.py:255
  131.9 13.5 %collective-permute-start.2 = (f32[2,8,64,128]{3,2,1,0:T(8,128)S(1)}, f32[2,8,64,128]{3,2,1,0:T(8,128)S(1)}, u32[]{:S(2)}, u32[]{:S(2)}) collective-permute-start(f32[2,8,64,128]{3,2,1,0:T(8,128)S(1)} %dynamic-slice_bitcast_fusion.2), channel_id=1, source_target_pairs={{0,4},{1,5},{2,6},{3,7},{4,0},{5,1},{6,2},{7,3},{8,12},{9,13},{10,... | collective-permute-start | bytes 1572872 | tf_op jit(solution)/shard_map/ppermute | solution.py:255
  145.6 13.5 %collective-permute-start.3 = (f32[1,8,64,128]{3,2,1,0:T(8,128)S(1)}, f32[1,8,64,128]{3,2,1,0:T(8,128)S(1)}, u32[]{:S(2)}, u32[]{:S(2)}) collective-permute-start(f32[1,8,64,128]{3,2,1,0:T(8,128)S(1)} %constant_dynamic-slice_fusion), channel_id=1, source_target_pairs={{0,8},{1,9},{2,10},{3,11},{4,12},{5,13},{6,14},{7,15},{8,0},{9,1},... | collective-permute-start | bytes 786440 | tf_op jit(solution)/shard_map/ppermute | solution.py:255

commit v7 on v6

--- a/solution.py
+++ b/solution.py
@@ -242,19 +242,35 @@
     return jnp.concatenate([left_half, right_half], 3)
 
 
+def halve(parts, bits, bit, position, fh_size):
+    axis = bits.index(bit)
+    mine = (position >> bit) & 1
+    keep = lax.dynamic_index_in_dim(parts, mine, axis=axis, keepdims=False)
+    send = lax.dynamic_index_in_dim(parts, 1 - mine, axis=axis, keepdims=False)
+    pairs = [(i, i ^ (1 << bit)) for i in range(fh_size)]
+    return keep + lax.ppermute(send, "fh", perm=pairs), bits[:axis] + bits[axis + 1:]
+
+
 def halving_reduce_scatter(terms, fh_size):
     position = lax.axis_index("fh")
-    parts = terms.reshape(fh_size, -1, *terms.shape[1:])
-    bit = 0
-    while (1 << bit) < fh_size:
-        paired = parts.reshape(parts.shape[0] // 2, 2, *parts.shape[1:])
-        mine = (position >> bit) & 1
-        keep = lax.dynamic_index_in_dim(paired, mine, axis=1, keepdims=False)
-        send = lax.dynamic_index_in_dim(paired, 1 - mine, axis=1, keepdims=False)
-        pairs = [(i, i ^ (1 << bit)) for i in range(fh_size)]
-        parts = keep + lax.ppermute(send, "fh", perm=pairs)
-        bit += 1
-    return parts.reshape(-1, *terms.shape[1:])
+    count = fh_size.bit_length() - 1
+    bits = list(reversed(range(count)))
+    parts = terms.reshape(*([2] * count), -1, *terms.shape[1:])
+    share = parts.shape[count]
+    if count < 3 or share % 2:
+        for bit in range(count):
+            parts, bits = halve(parts, bits, bit, position, fh_size)
+        return parts.reshape(-1, *terms.shape[1:])
+    parts, bits = halve(parts, bits, 0, position, fh_size)
+    first = lax.slice_in_dim(parts, 0, share // 2, axis=count - 1)
+    second = lax.slice_in_dim(parts, share // 2, share, axis=count - 1)
+    bits_first = bits_second = bits
+    order_first = list(range(1, count))
+    order_second = [2, 1] + list(range(3, count))
+    for bit_first, bit_second in zip(order_first, order_second):
+        first, bits_first = halve(first, bits_first, bit_first, position, fh_size)
+        second, bits_second = halve(second, bits_second, bit_second, position, fh_size)
+    return jnp.concatenate([first, second], axis=0).reshape(-1, *terms.shape[1:])
 
 
 def on_device(received_time_rows, pilots, active_users, allocation, loading, fh_size):

time: 212 us -> 194 us (0.915)
  waiting for transfers between devices: 50.1 us -> 28.2 us
  starting transfers between devices: 7.83 us -> 12.5 us
    ppermute x4 -> x7, waiting for transfers between devices: 50.1 us -> 28.2 us  [halve(): lax.ppermute(send, 'fh', perm=pairs)]
    ppermute x4 -> x7, starting transfers between devices: 7.83 us -> 12.5 us  [halve(): lax.ppermute(send, 'fh', perm=pairs)]
  transfers between devices with their start and end apart: 4 -> 7, of which waited for: 4 -> 5; matrix products, arithmetic and copies ran while one was open for 0% -> 0% of each run, Pallas kernels for 0% -> 0%
where the time goes in v7:
time: 194 us; the launch traced here: 193 us
  local copies, waits for them, and re-layouts  39.9 us (21%)
  other arithmetic  34.2 us (18%)
  Pallas kernels  33.9 us (17%)
  matrix products  31.3 us (16%)
  waiting for transfers between devices  28.2 us (15%)
  blocking collectives  13.1 us (7%)
  starting transfers between devices  12.5 us (6%)
    pallas_call x1, Pallas kernels, spd_solve(): pl.pallas_call(_solve_body, out_shape=jax.ShapeDtypeStruct(rhs.shape, jnp...  33.9 us
    ppermute x7, waiting for transfers between devices, halve(): lax.ppermute(send, 'fh', perm=pairs)  28.2 us
    all_to_all x1, blocking collectives, on_device(): return lax.all_to_all(result, 'fh', split_axis=0, concat_axis=3, tiled=True)  13.1 us
    ppermute x7, starting transfers between devices, halve(): lax.ppermute(send, 'fh', perm=pairs)  12.5 us
    sub x1, other arithmetic, packed_terms(): gram_imag = gram[:, 0, :, 1] - gram[:, 1, :, 0]  12.1 us
    reshape x1, local copies, waits for them, and re-layouts, spectra(): shaped = samples.reshape(antennas_here, symbol_count, 2, FA, FB)  10.8 us
    dot_general x1, matrix products, packed_terms(): jnp.einsum('rdkm,relm->rdkel', channel, channel, preferred_element_type=j...  10.3 us
    another operation x1, local copies, waits for them, and re-layouts, spectra(): section_one = jnp.stack([real_part, imag_part], 1).astype(jnp.bfloat16)  9.19 us
  transfers between devices with their start and end apart: 7, of which 5 were waited for; matrix products, arithmetic and copies ran while one was open for 0% of the time, Pallas kernels for 0%

profile of v7, /device:TPU:0, one launch (start us, length us, event | category | flops | bytes accessed | tf_op | source)
XLA Modules:
  0.0 193.5 jit_solution(1778834978766369081)
XLA Ops:
  0.0 0.1 negate_convert_fusion.2
  0.1 0.1 fusion.59
  0.1 0.1 sine_multiply_fusion.1
  0.2 1.1 negate_convert_fusion
  1.3 1.0 fusion.36
  2.3 10.8 %reshape.365 = bf16[128,3,2,16,256,1]{4,3,2,1,0,5:T(8,128)(2,1)} reshape(bf16[128,3,2,4096]{3,2,1,0:T(2,128)(2,1)} %param.5) | data formatting | bytes 12582912 | tf_op jit(solution)/shard_map/reshape | solution.py:128
  13.2 4.6 %convolution_bitcast_fusion = f32[3,2,16,256,128]{3,2,0,4,1:T(8,128)S(1)} fusion(bf16[128,3,2,16,256,1]{4,3,2,1,0,5:T(8,128)(2,1)} %reshape.365, bf16[1,16,2,16]{1,3,0,2:T(8,128)(2,1)S(1)} %get-tuple-element.27, bf16[1,16,2,16]{1,3,0,2:T(8,128)(2,1)S(1)} %get-tuple-element.26), kind=kOutput, calls=%fused_computation.8 | convolution fusion | flops 201330688 | bytes 18876416 | tf_op jit(solution)/shard_map/ascnm,cndk->sdkma/dot_general | solution.py:129
  17.8 2.2 %add_convert_fusion = (bf16[3,1,16,256,128]{3,2,0,4,1:T(8,128)(2,1)S(1)}, bf16[3,1,16,256,128]{3,2,0,4,1:T(8,128)(2,1)S(1)}) fusion(f32[3,2,16,256,128]{3,2,0,4,1:T(8,128)S(1)} %convolution_bitcast_fusion, f32[16,256]{1,0:T(8,128)S(1)} %get-tuple-element.33, f32[16,256]{1,0:T(8,128)S(1)} %get-tuple-element.34), kind=kLoop, calls=%fused_computation.7 | loop fusion | flops 12582912 | bytes 18907136 | tf_op jit(solution)/shard_map/convert
  20.0 3.2 %pad_maximum_fusion = bf16[3,2,16,256,128]{3,2,0,4,1:T(8,128)(2,1)} fusion(bf16[3,1,16,256,128]{3,2,0,4,1:T(8,128)(2,1)S(1)} %get-tuple-element.10, bf16[3,1,16,256,128]{3,2,0,4,1:T(8,128)(2,1)S(1)} %get-tuple-element.9), kind=kLoop, calls=%fused_computation.3 | loop fusion | flops 3145728 | bytes 12582912 | tf_op jit(solution)/shard_map/stack | solution.py:137
  23.2 9.2 %copy.88 = bf16[3,2,16,256,128]{4,3,1,2,0:T(8,128)(2,1)} copy(bf16[3,2,16,256,128]{3,2,0,4,1:T(8,128)(2,1)} %pad_maximum_fusion) | data formatting | bytes 12582912 | tf_op jit(solution)/shard_map/stack | solution.py:137
  32.4 6.6 %fusion = bf16[3,2,16,256,128]{4,3,2,0,1:T(8,128)(2,1)S(1)} fusion(bf16[3,2,16,256,128]{4,3,1,2,0:T(8,128)(2,1)} %copy.88, bf16[1,256,2,256]{1,3,0,2:T(8,128)(2,1)S(1)} %get-tuple-element.23, bf16[1,256,2,256]{1,3,0,2:T(8,128)(2,1)S(1)} %get-tuple-element.22), kind=kOutput, calls=%fused_computation.2 | convolution fusion | flops 3225419776 | bytes 13107200 | tf_op jit(solution)/shard_map/sckma,cmdj->sdkja/dot_general | solution.py:138
  39.0 0.0 copy-start.5
  39.0 0.3 slice.72
  39.3 2.3 %copy-done.3 = bf16[3,2,16,256,128]{4,3,2,0,1:T(8,128)(2,1)} copy-done((bf16[3,2,16,256,128]{4,3,2,0,1:T(8,128)(2,1)}, bf16[3,2,16,256,128]{4,3,2,0,1:T(8,128)(2,1)S(1)}, u32[]{:S(2)}) %copy-start.3) | copy-done | bytes 6291480
  41.7 0.1 iota_add_fusion
  41.7 0.1 broadcast_add_fusion
  41.8 0.2 fusion.43
  42.1 5.7 %fusion.8 = bf16[2,64,128,128,1,1,1]{3,1,6,5,2,0,4:T(8,128)(2,1)S(1)} fusion(bf16[2,2,16,128,2,128,1]{5,4,3,2,0,1,6:T(2,128)(2,1)S(1)} %bitcast.145, bf16[1,64,2,2,16,2]{1,4,2,3,0,5:T(8,128)(2,1)S(1)} %get-tuple-element.25, bf16[1,64,2,2,16,2]{1,4,2,3,0,5:T(8,128)(2,1)S(1)} %get-tuple-element.24), kind=kOutput, calls=%fused_computation.17 | convolution fusion | flops 536936448 | bytes 8421376 | tf_op jit(solution)/shard_map/tcarbm,dktcab->rdkm/dot_general | solution.py:209
  47.7 10.3 %fusion.5 = f32[128,2,64,2,64]{4,2,3,1,0:T(8,128)} fusion(bf16[2,64,128,128,1,1,1]{3,1,6,5,2,0,4:T(8,128)(2,1)S(1)} %fusion.8), kind=kOutput, calls=%fused_computation.14 | convolution fusion | flops 536870912 | bytes 12582912 | tf_op jit(solution)/shard_map/rdkm,relm->rdkel/dot_general | solution.py:212
  58.0 4.1 %fusion.12 = f32[128,2,64,1,2,16,2]{2,5,6,4,1,0,3:T(8,128)S(1)} fusion(bf16[2,16,128,2,128,1]{4,3,2,1,0,5:T(2,128)(2,1)S(1)} %bitcast.148, bf16[2,64,128,128,1,1,1]{3,1,6,5,2,0,4:T(8,128)(2,1)S(1)} %fusion.8), kind=kOutput, calls=%fused_computation.19 | convolution fusion | flops 268435456 | bytes 10485760 | tf_op jit(solution)/shard_map/rdkm,tcarbm->rdktcab/dot_general | solution.py:219
  62.1 2.6 %slice_add_fusion.1 = (f32[128,1,64,1,1,16,2]{2,5,6,4,1,0,3:T(8,128)}, f32[128,1,64,1,1,16,2]{2,5,6,4,1,0,3:T(8,128)S(1)}) fusion(f32[128,2,64,1,2,16,2]{2,5,6,4,1,0,3:T(8,128)S(1)} %fusion.12), kind=kLoop, calls=%fused_computation.21 | loop fusion | flops 524288 | bytes 6291456 | tf_op jit(solution)/shard_map/add | solution.py:222
  64.7 1.2 copy.92
  66.0 2.8 %copy.94 = f32[2,2,2,2,8,64,32]{6,5,4,3,2,1,0:T(8,128)} copy(f32[2,2,2,2,8,64,32]{5,4,3,2,1,0,6:T(8,128)S(1)} %bitcast.149) | data formatting | bytes 2097152 | tf_op jit(solution)/shard_map/sub | solution.py:223
  68.7 2.8 %copy.91 = f32[128,1,64,1,1,16,2]{2,0,6,5,4,3,1:T(8,128)S(1)} copy(f32[128,1,64,1,1,16,2]{2,5,6,4,1,0,3:T(8,128)} %get-tuple-element.11) | data formatting | bytes 2097152 | tf_op jit(solution)/shard_map/add | solution.py:222
  71.5 2.8 %copy.93 = f32[2,2,2,2,8,64,32]{6,5,4,3,2,1,0:T(8,128)} copy(f32[2,2,2,2,8,64,32]{5,4,3,2,1,0,6:T(8,128)S(1)} %bitcast.150) | data formatting | bytes 2097152 | tf_op jit(solution)/shard_map/add | solution.py:222
  74.4 12.1 %slice_subtract_fusion = (f32[128,1,64,1,64]{4,2,3,1,0:T(8,128)}, f32[128,1,64,1,64]{4,2,3,1,0:T(8,128)}) fusion(f32[128,2,64,2,64]{4,2,3,1,0:T(8,128)} %fusion.5), kind=kLoop, calls=%fused_computation.9 | loop fusion | flops 1048576 | bytes 12582912 | tf_op jit(solution)/shard_map/sub | solution.py:214
  86.5 4.6 %broadcast_select_fusion = f32[2,2,2,2,8,64,64]{6,5,4,3,2,1,0:T(8,128)S(1)} fusion(f32[2,2,2,2,8,64,64]{6,5,4,3,2,1,0:T(8,128)} %bitcast.147, f32[2,2,2,2,8,64,64]{6,5,4,3,2,1,0:T(8,128)} %bitcast.146, pred[64,64]{1,0:T(8,128)(4,1)S(1)} %iota_compare_fusion.3), kind=kLoop, calls=%fused_computation.25 | loop fusion | flops 524288 | bytes 6295552 | tf_op jit(solution)/shard_map/jit(_where)/select_n | solution.py:218
  91.1 0.0 copy-done.1
  91.1 1.3 copy-done.2
  92.4 2.2 %pad_maximum_fusion.1 = f32[2,2,2,2,8,64,128]{6,5,4,3,2,1,0:T(8,128)S(1)} fusion(f32[2,2,2,2,8,64,32]{6,5,4,3,2,1,0:T(8,128)S(1)} %copy-done.1, f32[2,2,2,2,8,64,32]{6,5,4,3,2,1,0:T(8,128)S(1)} %copy-done.2, f32[2,2,2,2,8,64,64]{6,5,4,3,2,1,0:T(8,128)S(1)} %broadcast_select_fusion), kind=kLoop, calls=%fused_computation.11 | loop fusion | flops 2097152 | bytes 8388608 | tf_op jit(solution)/shard_map/concatenate | solution.py:227
  94.6 2.0 %copy-done = f32[2,2,2,2,8,64,128]{6,5,4,3,2,1,0:T(8,128)} copy-done((f32[2,2,2,2,8,64,128]{6,5,4,3,2,1,0:T(8,128)}, f32[2,2,2,2,8,64,128]{6,5,4,3,2,1,0:T(8,128)S(1)}, u32[]{:S(2)}) %copy-start) | copy-done | bytes 4194328
  96.6 1.5 dynamic-slice_bitcast_fusion
  98.1 0.5 collective-permute-start
  98.6 4.0 %collective-permute-done = f32[2,2,2,8,64,128]{5,4,3,2,1,0:T(8,128)S(1)} collective-permute-done((f32[2,2,2,8,64,128]{5,4,3,2,1,0:T(8,128)}, f32[2,2,2,8,64,128]{5,4,3,2,1,0:T(8,128)S(1)}, u32[]{:S(2)}, u32[]{:S(2)}) %collective-permute-start) | collective-permute-done | bytes 2097184 | tf_op jit(solution)/shard_map/ppermute | solution.py:251
  102.6 2.0 %bitcast_add_fusion = f32[2,2,2,8,64,128]{5,4,3,2,1,0:T(8,128)S(1)} fusion(f32[2,2,2,8,64,128]{5,4,3,2,1,0:T(8,128)S(1)} %collective-permute-done, f32[2,2,2,2,8,64,128]{6,5,4,3,2,1,0:T(8,128)} %copy-done, s32[]{:T(128)S(6)} %select_n.151), kind=kLoop, calls=%fused_computation.22 | loop fusion | flops 524288 | bytes 6291460 | tf_op jit(solution)/shard_map/add | solution.py:251
  104.6 0.0 copy-start.6
  104.6 0.0 copy-start.7
  104.6 0.2 fusion.65
  104.8 0.0 copy-start.4
  104.8 0.1 constant_dynamic-slice_fusion.3
  104.9 2.9 %collective-permute-start.1 = (f32[2,2,4,64,128]{4,3,2,0,1:T(8,128)S(1)}, f32[2,2,4,64,128]{4,3,2,0,1:T(8,128)S(1)}, u32[]{:S(2)}, u32[]{:S(2)}) collective-permute-start(f32[2,2,4,64,128]{4,3,2,0,1:T(8,128)S(1)} %bitcast.153), channel_id=1, source_target_pairs={{0,2},{1,3},{2,0},{3,1},{4,6},{5,7},{6,4},{7,5},{8,10},{9,11},{10,... | collective-permute-start | bytes 1572872 | tf_op jit(solution)/shard_map/ppermute | solution.py:251
  107.9 0.1 constant_dynamic-slice_fusion.1
  108.0 1.6 collective-permute-start.4
  109.7 10.4 %collective-permute-done.1 = f32[2,2,4,64,128]{4,3,2,0,1:T(8,128)S(1)} collective-permute-done((f32[2,2,4,64,128]{4,3,2,0,1:T(8,128)S(1)}, f32[2,2,4,64,128]{4,3,2,0,1:T(8,128)S(1)}, u32[]{:S(2)}, u32[]{:S(2)}) %collective-permute-start.1) | collective-permute-done | bytes 524320 | tf_op jit(solution)/shard_map/ppermute | solution.py:251
  120.1 0.1 bitcast_add_fusion.2
  120.2 1.9 collective-permute-start.2
  122.0 0.1 bitcast_add_fusion.1
  122.1 1.6 collective-permute-start.5
  123.7 4.3 %collective-permute-done.2 = f32[2,4,64,128]{3,2,1,0:T(8,128)S(1)} collective-permute-done((f32[2,4,64,128]{3,2,1,0:T(8,128)S(1)}, f32[2,4,64,128]{3,2,1,0:T(8,128)S(1)}, u32[]{:S(2)}, u32[]{:S(2)}) %collective-permute-start.2) | collective-permute-done | bytes 262176 | tf_op jit(solution)/shard_map/ppermute | solution.py:251
  128.1 2.6 %collective-permute-start.3 = (f32[4,64,128]{2,1,0:T(8,128)S(1)}, f32[4,64,128]{2,1,0:T(8,128)S(1)}, u32[]{:S(2)}, u32[]{:S(2)}) collective-permute-start(f32[4,64,128]{2,1,0:T(8,128)S(1)} %dynamic-slice_bitcast_fusion.4), channel_id=1, source_target_pairs={{0,8},{1,9},{2,10},{3,11},{4,12},{5,13},{6,14},{7,15},{8,0},{9,1},... | collective-permute-start | bytes 393224 | tf_op jit(solution)/shard_map/ppermute | solution.py:251
  130.8 1.4 collective-permute-start.6
  132.2 7.6 %collective-permute-done.3 = f32[4,64,128]{2,1,0:T(8,128)S(1)} collective-permute-done((f32[4,64,128]{2,1,0:T(8,128)S(1)}, f32[4,64,128]{2,1,0:T(8,128)S(1)}, u32[]{:S(2)}, u32[]{:S(2)}) %collective-permute-start.3) | collective-permute-done | bytes 131104 | tf_op jit(solution)/shard_map/ppermute | solution.py:251
  139.8 1.9 collective-permute-done.6
  141.7 0.1 copy.99
  141.8 0.3 fusion.20
  142.1 0.9 pad_maximum_fusion.2.b_ref
  143.0 0.2 fusion.63
  143.2 1.0 maximum_maximum_fusion.a_ref
  144.2 33.9 %shard_map.55 = f32[8,128,32]{2,1,0:T(8,128)} custom-call(f32[8,128,128]{2,1,0:T(8,128)} %maximum_maximum_fusion.a_ref, f32[8,128,32]{2,1,0:T(8,128)} %pad_maximum_fusion.2.b_ref), custom_call_target="tpu_custom_call" | custom-call | tf_op jit(solution)/shard_map/pallas_call | solution.py:94
  178.1 1.2 copy.100
  179.3 0.2 reshape.362
  179.5 0.1 copy.102
  179.7 13.1 %all_to_all.18 = f32[64,1,2,256]{3,2,1,0:T(2,128)S(1)} all-to-all(f32[64,1,2,256]{3,2,1,0:T(2,128)S(1)} %copy.102), channel_id=1, replica_groups=mesh['cells'=2,'fh'=16] {'fh'}, dimensions={0} | all-to-all | bytes 262144 | tf_op jit(solution)/shard_map/all_to_all | solution.py:285
  192.8 0.7 copy.120
  (34 shorter events, 0.4 us)
Async XLA Ops:
  39.0 2.6 %copy-start.3 = (bf16[3,2,16,256,128]{4,3,2,0,1:T(8,128)(2,1)}, bf16[3,2,16,256,128]{4,3,2,0,1:T(8,128)(2,1)S(1)}, u32[]{:S(2)}) copy-start(bf16[3,2,16,256,128]{4,3,2,0,1:T(8,128)(2,1)S(1)} %fusion) | copy-start | bytes 18874372
  39.0 2.8 %copy-start.5 = (s32[64]{0:T(128)S(1)}, s32[64]{0:T(128)}, u32[]{:S(2)}) copy-start(s32[64]{0:T(128)} %param.6) | copy-start | bytes 772
  47.7 10.3 %slice-start = ((bf16[3,2,16,256,128]{4,3,2,0,1:T(8,128)(2,1)}), bf16[1,2,16,256,128]{4,3,2,0,1:T(8,128)(2,1)S(1)}, s32[]{:S(2)}) async-start(bf16[3,2,16,256,128]{4,3,2,0,1:T(8,128)(2,1)} %copy-done.3), calls=%async_computation.1 | async-start | bytes 4194304 | tf_op jit(solution)/shard_map/slice | solution.py:279
  86.5 4.6 %copy-start.1 = (f32[2,2,2,2,8,64,32]{6,5,4,3,2,1,0:T(8,128)S(1)}, f32[2,2,2,2,8,64,32]{6,5,4,3,2,1,0:T(8,128)}, u32[]{:S(2)}) copy-start(f32[2,2,2,2,8,64,32]{6,5,4,3,2,1,0:T(8,128)} %copy.94) | copy-start | bytes 3145732
  86.5 5.9 %copy-start.2 = (f32[2,2,2,2,8,64,32]{6,5,4,3,2,1,0:T(8,128)S(1)}, f32[2,2,2,2,8,64,32]{6,5,4,3,2,1,0:T(8,128)}, u32[]{:S(2)}) copy-start(f32[2,2,2,2,8,64,32]{6,5,4,3,2,1,0:T(8,128)} %copy.93) | copy-start | bytes 3145732
  94.6 2.0 %copy-start = (f32[2,2,2,2,8,64,128]{6,5,4,3,2,1,0:T(8,128)}, f32[2,2,2,2,8,64,128]{6,5,4,3,2,1,0:T(8,128)S(1)}, u32[]{:S(2)}) copy-start(f32[2,2,2,2,8,64,128]{6,5,4,3,2,1,0:T(8,128)S(1)} %pad_maximum_fusion.1) | copy-start | bytes 12582916
  98.1 4.5 %collective-permute-start = (f32[2,2,2,8,64,128]{5,4,3,2,1,0:T(8,128)}, f32[2,2,2,8,64,128]{5,4,3,2,1,0:T(8,128)S(1)}, u32[]{:S(2)}, u32[]{:S(2)}) collective-permute-start(f32[2,2,2,8,64,128]{5,4,3,2,1,0:T(8,128)} %dynamic-slice_bitcast_fusion), channel_id=1, source_target_pairs={{0,1},{1,0},{2,3},{3,2},{4,5},{5,4},{6,7},{7,6},{8,9},{9,8},{10,11... | collective-permute-start | bytes 6291464 | tf_op jit(solution)/shard_map/ppermute | solution.py:251
  104.6 3.3 %copy-start.6 = (f32[64]{0:T(128)S(1)}, f32[64]{0:T(128)}, u32[]{:S(2)}) copy-start(f32[64]{0:T(128)} %param.9) | copy-start | bytes 772
  104.6 3.3 %copy-start.7 = (s32[64]{0:T(128)S(1)}, s32[64]{0:T(128)}, u32[]{:S(2)}) copy-start(s32[64]{0:T(128)} %param.7) | copy-start | bytes 772
  104.8 4.9 %copy-start.4 = (s32[8,64]{1,0:T(8,128)S(1)}, s32[8,64]{1,0:T(8,128)}, u32[]{:S(2)}) copy-start(s32[8,64]{1,0:T(8,128)} %param.8) | copy-start | bytes 6148
  104.9 15.1 %collective-permute-start.1 = (f32[2,2,4,64,128]{4,3,2,0,1:T(8,128)S(1)}, f32[2,2,4,64,128]{4,3,2,0,1:T(8,128)S(1)}, u32[]{:S(2)}, u32[]{:S(2)}) collective-permute-start(f32[2,2,4,64,128]{4,3,2,0,1:T(8,128)S(1)} %bitcast.153), channel_id=1, source_target_pairs={{0,2},{1,3},{2,0},{3,1},{4,6},{5,7},{6,4},{7,5},{8,10},{9,11},{10,... | collective-permute-start | bytes 1572872 | tf_op jit(solution)/shard_map/ppermute | solution.py:251
  108.0 14.0 %collective-permute-start.4 = (f32[2,2,4,64,128]{4,3,2,0,1:T(8,128)S(1)}, f32[2,2,4,64,128]{4,3,2,0,1:T(8,128)S(1)}, u32[]{:S(2)}, u32[]{:S(2)}) collective-permute-start(f32[2,2,4,64,128]{4,3,2,0,1:T(8,128)S(1)} %bitcast.154), channel_id=1, source_target_pairs={{0,4},{1,5},{2,6},{3,7},{4,0},{5,1},{6,2},{7,3},{8,12},{9,13},{10,... | collective-permute-start | bytes 1572872 | tf_op jit(solution)/shard_map/ppermute | solution.py:251
  120.2 7.9 %collective-permute-start.2 = (f32[2,4,64,128]{3,2,1,0:T(8,128)S(1)}, f32[2,4,64,128]{3,2,1,0:T(8,128)S(1)}, u32[]{:S(2)}, u32[]{:S(2)}) collective-permute-start(f32[2,4,64,128]{3,2,1,0:T(8,128)S(1)} %dynamic-slice_bitcast_fusion.2), channel_id=1, source_target_pairs={{0,4},{1,5},{2,6},{3,7},{4,0},{5,1},{6,2},{7,3},{8,12},{9,13},{10,... | collective-permute-start | bytes 786440 | tf_op jit(solution)/shard_map/ppermute | solution.py:251
  122.1 8.5 %collective-permute-start.5 = (f32[2,4,64,128]{3,2,1,0:T(8,128)S(1)}, f32[2,4,64,128]{3,2,1,0:T(8,128)S(1)}, u32[]{:S(2)}, u32[]{:S(2)}) collective-permute-start(f32[2,4,64,128]{3,2,1,0:T(8,128)S(1)} %dynamic-slice_bitcast_fusion.1), channel_id=1, source_target_pairs={{0,2},{1,3},{2,0},{3,1},{4,6},{5,7},{6,4},{7,5},{8,10},{9,11},{10,... | collective-permute-start | bytes 786440 | tf_op jit(solution)/shard_map/ppermute | solution.py:251
  128.1 11.6 %collective-permute-start.3 = (f32[4,64,128]{2,1,0:T(8,128)S(1)}, f32[4,64,128]{2,1,0:T(8,128)S(1)}, u32[]{:S(2)}, u32[]{:S(2)}) collective-permute-start(f32[4,64,128]{2,1,0:T(8,128)S(1)} %dynamic-slice_bitcast_fusion.4), channel_id=1, source_target_pairs={{0,8},{1,9},{2,10},{3,11},{4,12},{5,13},{6,14},{7,15},{8,0},{9,1},... | collective-permute-start | bytes 393224 | tf_op jit(solution)/shard_map/ppermute | solution.py:251
  130.8 10.9 %collective-permute-start.6 = (f32[4,64,128]{2,1,0:T(8,128)S(1)}, f32[4,64,128]{2,1,0:T(8,128)S(1)}, u32[]{:S(2)}, u32[]{:S(2)}) collective-permute-start(f32[4,64,128]{2,1,0:T(8,128)S(1)} %dynamic-slice_bitcast_fusion.3), channel_id=1, source_target_pairs={{0,8},{1,9},{2,10},{3,11},{4,12},{5,13},{6,14},{7,15},{8,0},{9,1},... | collective-permute-start | bytes 393224 | tf_op jit(solution)/shard_map/ppermute | solution.py:251

commit v8 on v7

--- a/solution.py
+++ b/solution.py
@@ -209,18 +209,17 @@
     channel = jnp.einsum(
         "tcarbm,dktcab->rdkm", pilot_part, code_rows, preferred_element_type=jnp.float32
     ).astype(jnp.bfloat16)
-    gram = jnp.einsum("rdkm,relm->rdkel", channel, channel, preferred_element_type=jnp.float32)
-    gram_real = gram[:, 0, :, 0] + gram[:, 1, :, 1]
-    gram_imag = gram[:, 0, :, 1] - gram[:, 1, :, 0]
+    turned = jnp.stack([-channel[:, 1], channel[:, 0]], 1)
+    gram_real = jnp.einsum("rckm,rclm->rkl", channel, channel, preferred_element_type=jnp.float32)
+    gram_imag = jnp.einsum("rckm,rclm->rkl", turned, channel, preferred_element_type=jnp.float32)
     user_count = gram_real.shape[1]
     row = lax.broadcasted_iota(jnp.int32, (user_count, user_count), 0)
     col = lax.broadcasted_iota(jnp.int32, (user_count, user_count), 1)
     packed = jnp.where(row <= col, gram_real, gram_imag)
-    matched = jnp.einsum(
-        "rdkm,tcarbm->rdktcab", channel, data_part, preferred_element_type=jnp.float32
-    )
-    matched_real = matched[:, 0, :, :, 0] + matched[:, 1, :, :, 1]
-    matched_imag = matched[:, 0, :, :, 1] - matched[:, 1, :, :, 0]
+    matched_real = jnp.einsum(
+        "rckm,tcarbm->rktab", channel, data_part, preferred_element_type=jnp.float32)
+    matched_imag = jnp.einsum(
+        "rckm,tcarbm->rktab", turned, data_part, preferred_element_type=jnp.float32)
     blocks = matched_real.shape[0]
     matched_real = matched_real.reshape(blocks, user_count, -1)
     matched_imag = matched_imag.reshape(blocks, user_count, -1)

time: 194 us -> 177 us (0.912)
  other arithmetic: 34.2 us -> 15.3 us
    sub x1 -> x0, other arithmetic: 12.1 us -> none  [packed_terms(): gram_imag = gram[:, 0, :, 1] - gram[:, 1, :, 0]]
    dot_general x0 -> x3, local copies, waits for them, and re-layouts: none -> 6.84 us  [the longest x1 3.02 us: packed_terms(): jnp.einsum('rckm,tcarbm->rktab', channel, data_part, preferred_element_ty...]
    add x2 -> x0, local copies, waits for them, and re-layouts: 5.63 us -> none  [packed_terms(): matched_real = matched[:, 0, :, :, 0] + matched[:, 1, :, :, 1]]
    concatenate x0 -> x2, local copies, waits for them, and re-layouts: none -> 5.54 us  [packed_terms(): return jnp.concatenate([packed, matched_real, matched_imag], 2)]
    select_n x1 -> x0, other arithmetic: 4.58 us -> none  [packed_terms(): packed = jnp.where(row <= col, gram_real, gram_imag)]
    sub x2 -> x0, local copies, waits for them, and re-layouts: 3.98 us -> none  [packed_terms(): matched_imag = matched[:, 0, :, :, 1] - matched[:, 1, :, :, 0]]
    unnamed x16, local copies, waits for them, and re-layouts: 5.63 us -> 2.99 us
    add x1 -> x0, other arithmetic: 2.6 us -> none  [packed_terms(): matched_real = matched[:, 0, :, :, 0] + matched[:, 1, :, :, 1]]
where the time goes in v8:
time: 177 us; the launch traced here: 176 us
  local copies, waits for them, and re-layouts  40.4 us (23%)
  Pallas kernels  33.9 us (19%)
  matrix products  32.4 us (18%)
  waiting for transfers between devices  28.1 us (16%)
  other arithmetic  15.3 us (9%)
  blocking collectives  13.1 us (7%)
  starting transfers between devices  12.6 us (7%)
    pallas_call x1, Pallas kernels, spd_solve(): pl.pallas_call(_solve_body, out_shape=jax.ShapeDtypeStruct(rhs.shape, jnp...  33.9 us
    ppermute x7, waiting for transfers between devices, halve(): lax.ppermute(send, 'fh', perm=pairs)  28.1 us
    all_to_all x1, blocking collectives, on_device(): return lax.all_to_all(result, 'fh', split_axis=0, concat_axis=3, tiled=True)  13.1 us
    ppermute x7, starting transfers between devices, halve(): lax.ppermute(send, 'fh', perm=pairs)  12.6 us
    reshape x1, local copies, waits for them, and re-layouts, spectra(): shaped = samples.reshape(antennas_here, symbol_count, 2, FA, FB)  10.8 us
    another operation x1, local copies, waits for them, and re-layouts, spectra(): section_one = jnp.stack([real_part, imag_part], 1).astype(jnp.bfloat16)  9.14 us
    dot_general x1, matrix products, spectra(): jnp.einsum('sckma,cmdj->sdkja', section_one, dft_table(FB), preferred_ele...  6.68 us
    dot_general x1, matrix products, packed_terms(): jnp.einsum('rckm,rclm->rkl', channel, channel, preferred_element_type=jnp...  6.1 us
  transfers between devices with their start and end apart: 7, of which 5 were waited for; matrix products, arithmetic and copies ran while one was open for 0% of the time, Pallas kernels for 0%

profile of v8, /device:TPU:0, one launch (start us, length us, event | category | flops | bytes accessed | tf_op | source)
XLA Modules:
  0.0 176.2 jit_solution(17953291959636465417)
XLA Ops:
  0.0 0.1 fusion.68
  0.1 0.1 negate_convert_fusion.2
  0.2 0.1 sine_multiply_fusion.1
  0.2 1.0 fusion.45
  1.2 1.1 negate_convert_fusion
  2.3 10.8 %reshape.346 = bf16[128,3,2,16,256,1]{4,3,2,1,0,5:T(8,128)(2,1)} reshape(bf16[128,3,2,4096]{3,2,1,0:T(2,128)(2,1)} %param.5) | data formatting | bytes 12582912 | tf_op jit(solution)/shard_map/reshape | solution.py:128
  13.2 4.6 %convolution_bitcast_fusion = f32[3,2,16,256,128]{3,2,0,4,1:T(8,128)S(1)} fusion(bf16[128,3,2,16,256,1]{4,3,2,1,0,5:T(8,128)(2,1)} %reshape.346, bf16[1,16,2,16]{1,3,0,2:T(8,128)(2,1)S(1)} %get-tuple-element.25, bf16[1,16,2,16]{1,3,0,2:T(8,128)(2,1)S(1)} %get-tuple-element.24), kind=kOutput, calls=%fused_computation.8 | convolution fusion | flops 201330688 | bytes 18876416 | tf_op jit(solution)/shard_map/ascnm,cndk->sdkma/dot_general | solution.py:129
  17.8 2.2 %add_convert_fusion = (bf16[3,1,16,256,128]{3,2,0,4,1:T(8,128)(2,1)S(1)}, bf16[3,1,16,256,128]{3,2,0,4,1:T(8,128)(2,1)S(1)}) fusion(f32[3,2,16,256,128]{3,2,0,4,1:T(8,128)S(1)} %convolution_bitcast_fusion, f32[16,256]{1,0:T(8,128)S(1)} %get-tuple-element.31, f32[16,256]{1,0:T(8,128)S(1)} %get-tuple-element.32), kind=kLoop, calls=%fused_computation.7 | loop fusion | flops 12582912 | bytes 18907136 | tf_op jit(solution)/shard_map/convert
  20.0 3.2 %pad_maximum_fusion = bf16[3,2,16,256,128]{3,2,0,4,1:T(8,128)(2,1)} fusion(bf16[3,1,16,256,128]{3,2,0,4,1:T(8,128)(2,1)S(1)} %get-tuple-element.8, bf16[3,1,16,256,128]{3,2,0,4,1:T(8,128)(2,1)S(1)} %get-tuple-element.7), kind=kLoop, calls=%fused_computation.3 | loop fusion | flops 3145728 | bytes 12582912 | tf_op jit(solution)/shard_map/stack | solution.py:137
  23.2 9.1 %copy.105 = bf16[3,2,16,256,128]{4,3,1,2,0:T(8,128)(2,1)} copy(bf16[3,2,16,256,128]{3,2,0,4,1:T(8,128)(2,1)} %pad_maximum_fusion) | data formatting | bytes 12582912 | tf_op jit(solution)/shard_map/stack | solution.py:137
  32.4 6.7 %fusion = bf16[3,2,16,256,128]{4,3,2,0,1:T(8,128)(2,1)S(1)} fusion(bf16[3,2,16,256,128]{4,3,1,2,0:T(8,128)(2,1)} %copy.105, bf16[1,256,2,256]{1,3,0,2:T(8,128)(2,1)S(1)} %get-tuple-element.21, bf16[1,256,2,256]{1,3,0,2:T(8,128)(2,1)S(1)} %get-tuple-element.20), kind=kOutput, calls=%fused_computation.2 | convolution fusion | flops 3225419776 | bytes 13107200 | tf_op jit(solution)/shard_map/sckma,cmdj->sdkja/dot_general | solution.py:138
  39.1 0.2 slice.51
  39.3 0.0 copy-start.5
  39.3 0.5 slice.48
  39.8 0.1 iota_add_fusion
  39.9 0.1 broadcast_add_fusion
  40.0 0.0 copy-done.5
  40.0 0.2 fusion.52
  40.2 5.7 %fusion.7 = bf16[2,64,128,128,1,1,1]{3,1,6,5,2,0,4:T(8,128)(2,1)S(1)} fusion(bf16[2,2,16,128,2,128,1]{5,4,3,2,0,1,6:T(2,128)(2,1)S(1)} %bitcast.153, bf16[1,64,2,2,16,2]{1,4,2,3,0,5:T(8,128)(2,1)S(1)} %get-tuple-element.23, bf16[1,64,2,2,16,2]{1,4,2,3,0,5:T(8,128)(2,1)S(1)} %get-tuple-element.22), kind=kOutput, calls=%fused_computation.16 | convolution fusion | flops 536936448 | bytes 8421376 | tf_op jit(solution)/shard_map/tcarbm,dktcab->rdkm/dot_general | solution.py:209
  45.9 1.0 copy.169
  46.9 3.1 %fusion.14 = f32[128,64,16,2]{1,2,3,0:T(8,128)} fusion(bf16[2,16,128,2,128]{4,3,2,1,0:T(2,128)(2,1)S(1)} %bitcast.158, bf16[2,64,128,128,1,1,1]{3,1,6,5,2,0,4:T(8,128)(2,1)S(1)} %fusion.7), kind=kOutput, calls=%fused_computation.24 | convolution fusion | flops 134217728 | bytes 7340032 | tf_op jit(solution)/shard_map/rckm,tcarbm->rktab/dot_general | solution.py:219
  50.0 0.4 slice_negate_fusion
  50.4 2.9 %fusion.19 = f32[128,64,16,2]{1,2,3,0:T(8,128)} fusion(bf16[2,16,128,2,128]{4,3,2,1,0:T(2,128)(2,1)S(1)} %bitcast.159, bf16[128,1,64,128]{3,2,1,0:T(8,128)(2,1)S(1)} %get-tuple-element.10, bf16[128,1,64,128]{3,2,1,0:T(8,128)(2,1)S(1)} %get-tuple-element.9), kind=kOutput, calls=%fused_computation.25 | convolution fusion | flops 142606336 | bytes 7340032 | tf_op jit(solution)/shard_map/rckm,tcarbm->rktab/dot_general | solution.py:221
  53.3 3.3 %fusion.11 = f32[128,64,64,1]{2,1,3,0:T(8,128)} fusion(bf16[128,1,64,128]{3,2,1,0:T(8,128)(2,1)S(1)} %get-tuple-element.10, bf16[128,1,64,128]{3,2,1,0:T(8,128)(2,1)S(1)} %get-tuple-element.9, bf16[2,64,128,128,1,1,1]{3,1,6,5,2,0,4:T(8,128)(2,1)S(1)} %fusion.7), kind=kOutput, calls=%fused_computation.18 | convolution fusion | flops 270532608 | bytes 10485760 | tf_op jit(solution)/shard_map/rckm,rclm->rkl/dot_general | solution.py:214
  56.6 3.0 %copy.112 = f32[128,64,16,2]{1,0,3,2:T(8,128)S(1)} copy(f32[128,64,16,2]{1,2,3,0:T(8,128)} %fusion.14) | data formatting | bytes 2097152 | tf_op jit(solution)/shard_map/rckm,tcarbm->rktab/dot_general | solution.py:219
  59.6 2.8 %copy.115 = f32[2,2,2,2,8,64,32]{6,5,4,3,2,1,0:T(8,128)} copy(f32[2,2,2,2,8,64,32]{5,4,3,2,1,0,6:T(8,128)S(1)} %bitcast.156) | data formatting | bytes 2097152 | tf_op jit(solution)/shard_map/concatenate | solution.py:226
  62.4 2.8 %copy.114 = f32[128,64,16,2]{1,0,3,2:T(8,128)S(1)} copy(f32[128,64,16,2]{1,2,3,0:T(8,128)} %fusion.19) | data formatting | bytes 2097152 | tf_op jit(solution)/shard_map/rckm,tcarbm->rktab/dot_general | solution.py:221
  65.2 2.8 %copy.116 = f32[2,2,2,2,8,64,32]{6,5,4,3,2,1,0:T(8,128)} copy(f32[2,2,2,2,8,64,32]{5,4,3,2,1,0,6:T(8,128)S(1)} %bitcast.157) | data formatting | bytes 2097152 | tf_op jit(solution)/shard_map/concatenate | solution.py:226
  68.0 6.1 %bitcast_select_fusion = f32[128,64,64]{2,1,0:T(8,128)S(1)} fusion(f32[128,64,64,1]{2,1,3,0:T(8,128)} %fusion.11, pred[64,64]{1,0:T(8,128)(4,1)S(1)} %iota_compare_fusion.3, bf16[2,64,128,128,1,1,1]{3,1,6,5,2,0,4:T(8,128)(2,1)} %copy-done), kind=kOutput, calls=%fused_computation.15 | convolution fusion | flops 268959744 | bytes 8392704 | tf_op jit(solution)/shard_map/rckm,rclm->rkl/dot_general | solution.py:213
  74.1 1.0 copy-done.3
  75.1 2.2 %pad_maximum_fusion.2 = f32[2,2,2,2,8,64,128]{6,5,4,3,2,1,0:T(8,128)S(1)} fusion(f32[2,2,2,2,8,64,32]{6,5,4,3,2,1,0:T(8,128)S(1)} %copy-done.3, f32[2,2,2,2,8,64,32]{6,5,4,3,2,1,0:T(8,128)S(1)} %copy-done.2, f32[2,2,2,2,8,64,64]{6,5,4,3,2,1,0:T(8,128)S(1)} %bitcast.155), kind=kLoop, calls=%fused_computation.10 | loop fusion | flops 2097152 | bytes 8388608 | tf_op jit(solution)/shard_map/concatenate | solution.py:226
  77.3 1.9 %copy-done.1 = f32[2,2,2,2,8,64,128]{6,5,4,3,2,1,0:T(8,128)} copy-done((f32[2,2,2,2,8,64,128]{6,5,4,3,2,1,0:T(8,128)}, f32[2,2,2,2,8,64,128]{6,5,4,3,2,1,0:T(8,128)S(1)}, u32[]{:S(2)}) %copy-start.1) | copy-done | bytes 4194328
  79.3 1.5 dynamic-slice_bitcast_fusion
  80.8 0.5 collective-permute-start
  81.3 4.0 %collective-permute-done = f32[2,2,2,8,64,128]{5,4,3,2,1,0:T(8,128)S(1)} collective-permute-done((f32[2,2,2,8,64,128]{5,4,3,2,1,0:T(8,128)}, f32[2,2,2,8,64,128]{5,4,3,2,1,0:T(8,128)S(1)}, u32[]{:S(2)}, u32[]{:S(2)}) %collective-permute-start) | collective-permute-done | bytes 2097184 | tf_op jit(solution)/shard_map/ppermute | solution.py:250
  85.3 2.0 %bitcast_add_fusion = f32[2,2,2,8,64,128]{5,4,3,2,1,0:T(8,128)S(1)} fusion(f32[2,2,2,8,64,128]{5,4,3,2,1,0:T(8,128)S(1)} %collective-permute-done, f32[2,2,2,2,8,64,128]{6,5,4,3,2,1,0:T(8,128)} %copy-done.1, s32[]{:T(128)S(6)} %select_n.150), kind=kLoop, calls=%fused_computation.20 | loop fusion | flops 524288 | bytes 6291460 | tf_op jit(solution)/shard_map/add | solution.py:250
  87.2 0.0 copy-start.6
  87.3 0.0 copy-start.7
  87.3 0.2 fusion.76
  87.5 0.1 constant_dynamic-slice_fusion.1
  87.6 3.0 %collective-permute-start.4 = (f32[2,2,4,64,128]{4,3,2,0,1:T(8,128)S(1)}, f32[2,2,4,64,128]{4,3,2,0,1:T(8,128)S(1)}, u32[]{:S(2)}, u32[]{:S(2)}) collective-permute-start(f32[2,2,4,64,128]{4,3,2,0,1:T(8,128)S(1)} %bitcast.162), channel_id=1, source_target_pairs={{0,4},{1,5},{2,6},{3,7},{4,0},{5,1},{6,2},{7,3},{8,12},{9,13},{10,... | collective-permute-start | bytes 1572872 | tf_op jit(solution)/shard_map/ppermute | solution.py:250
  90.7 0.1 constant_dynamic-slice_fusion.3
  90.8 1.6 collective-permute-start.1
  92.4 10.4 %collective-permute-done.4 = f32[2,2,4,64,128]{4,3,2,0,1:T(8,128)S(1)} collective-permute-done((f32[2,2,4,64,128]{4,3,2,0,1:T(8,128)S(1)}, f32[2,2,4,64,128]{4,3,2,0,1:T(8,128)S(1)}, u32[]{:S(2)}, u32[]{:S(2)}) %collective-permute-start.4) | collective-permute-done | bytes 524320 | tf_op jit(solution)/shard_map/ppermute | solution.py:250
  102.9 0.1 bitcast_add_fusion.1
  103.0 1.7 collective-permute-start.5
  104.7 0.1 bitcast_add_fusion.2
  104.8 1.7 collective-permute-start.2
  106.5 4.4 %collective-permute-done.5 = f32[2,4,64,128]{3,2,1,0:T(8,128)S(1)} collective-permute-done((f32[2,4,64,128]{3,2,1,0:T(8,128)S(1)}, f32[2,4,64,128]{3,2,1,0:T(8,128)S(1)}, u32[]{:S(2)}, u32[]{:S(2)}) %collective-permute-start.5) | collective-permute-done | bytes 262176 | tf_op jit(solution)/shard_map/ppermute | solution.py:250
  110.9 2.5 %collective-permute-start.6 = (f32[4,64,128]{2,1,0:T(8,128)S(1)}, f32[4,64,128]{2,1,0:T(8,128)S(1)}, u32[]{:S(2)}, u32[]{:S(2)}) collective-permute-start(f32[4,64,128]{2,1,0:T(8,128)S(1)} %dynamic-slice_bitcast_fusion.3), channel_id=1, source_target_pairs={{0,8},{1,9},{2,10},{3,11},{4,12},{5,13},{6,14},{7,15},{8,0},{9,1},... | collective-permute-start | bytes 393224 | tf_op jit(solution)/shard_map/ppermute | solution.py:250
  113.5 1.7 collective-permute-start.3
  115.2 7.6 %collective-permute-done.6 = f32[4,64,128]{2,1,0:T(8,128)S(1)} collective-permute-done((f32[4,64,128]{2,1,0:T(8,128)S(1)}, f32[4,64,128]{2,1,0:T(8,128)S(1)}, u32[]{:S(2)}, u32[]{:S(2)}) %collective-permute-start.6) | collective-permute-done | bytes 131104 | tf_op jit(solution)/shard_map/ppermute | solution.py:250
  122.8 1.7 collective-permute-done.3
  124.5 0.1 copy.121
  124.6 0.3 fusion.29
  124.9 0.9 pad_maximum_fusion.5.b_ref
  125.8 0.2 fusion.74
  125.9 1.0 maximum_maximum_fusion.a_ref
  127.0 33.9 %shard_map.55 = f32[8,128,32]{2,1,0:T(8,128)} custom-call(f32[8,128,128]{2,1,0:T(8,128)} %maximum_maximum_fusion.a_ref, f32[8,128,32]{2,1,0:T(8,128)} %pad_maximum_fusion.5.b_ref), custom_call_target="tpu_custom_call" | custom-call | tf_op jit(solution)/shard_map/pallas_call | solution.py:94
  160.9 1.2 copy.122
  162.1 0.2 reshape.343
  162.3 0.1 copy.124
  162.5 13.1 %all_to_all.18 = f32[64,1,2,256]{3,2,1,0:T(2,128)S(1)} all-to-all(f32[64,1,2,256]{3,2,1,0:T(2,128)S(1)} %copy.124), channel_id=1, replica_groups=mesh['cells'=2,'fh'=16] {'fh'}, dimensions={0} | all-to-all | bytes 262144 | tf_op jit(solution)/shard_map/all_to_all | solution.py:284
  175.5 0.7 copy.146
  (34 shorter events, 0.4 us)
Async XLA Ops:
  39.3 0.7 copy-start.5
  45.9 7.4 %copy-start = (bf16[2,64,128,128,1,1,1]{3,1,6,5,2,0,4:T(8,128)(2,1)}, bf16[2,64,128,128,1,1,1]{3,1,6,5,2,0,4:T(8,128)(2,1)S(1)}, u32[]{:S(2)}) copy-start(bf16[2,64,128,128,1,1,1]{3,1,6,5,2,0,4:T(8,128)(2,1)S(1)} %fusion.7) | copy-start | bytes 12582916
  68.0 6.1 %copy-start.2 = (f32[2,2,2,2,8,64,32]{6,5,4,3,2,1,0:T(8,128)S(1)}, f32[2,2,2,2,8,64,32]{6,5,4,3,2,1,0:T(8,128)}, u32[]{:S(2)}) copy-start(f32[2,2,2,2,8,64,32]{6,5,4,3,2,1,0:T(8,128)} %copy.115) | copy-start | bytes 3145732
  68.0 7.1 %copy-start.3 = (f32[2,2,2,2,8,64,32]{6,5,4,3,2,1,0:T(8,128)S(1)}, f32[2,2,2,2,8,64,32]{6,5,4,3,2,1,0:T(8,128)}, u32[]{:S(2)}) copy-start(f32[2,2,2,2,8,64,32]{6,5,4,3,2,1,0:T(8,128)} %copy.116) | copy-start | bytes 3145732
  77.3 2.0 %copy-start.1 = (f32[2,2,2,2,8,64,128]{6,5,4,3,2,1,0:T(8,128)}, f32[2,2,2,2,8,64,128]{6,5,4,3,2,1,0:T(8,128)S(1)}, u32[]{:S(2)}) copy-start(f32[2,2,2,2,8,64,128]{6,5,4,3,2,1,0:T(8,128)S(1)} %pad_maximum_fusion.2) | copy-start | bytes 12582916
  80.8 4.5 %collective-permute-start = (f32[2,2,2,8,64,128]{5,4,3,2,1,0:T(8,128)}, f32[2,2,2,8,64,128]{5,4,3,2,1,0:T(8,128)S(1)}, u32[]{:S(2)}, u32[]{:S(2)}) collective-permute-start(f32[2,2,2,8,64,128]{5,4,3,2,1,0:T(8,128)} %dynamic-slice_bitcast_fusion), channel_id=1, source_target_pairs={{0,1},{1,0},{2,3},{3,2},{4,5},{5,4},{6,7},{7,6},{8,9},{9,8},{10,11... | collective-permute-start | bytes 6291464 | tf_op jit(solution)/shard_map/ppermute | solution.py:250
  87.2 3.4 %copy-start.6 = (f32[64]{0:T(128)S(1)}, f32[64]{0:T(128)}, u32[]{:S(2)}) copy-start(f32[64]{0:T(128)} %param.9) | copy-start | bytes 772
  87.3 3.4 %copy-start.7 = (s32[64]{0:T(128)S(1)}, s32[64]{0:T(128)}, u32[]{:S(2)}) copy-start(s32[64]{0:T(128)} %param.7) | copy-start | bytes 772
  87.5 5.0 %copy-start.4 = (s32[8,64]{1,0:T(8,128)S(1)}, s32[8,64]{1,0:T(8,128)}, u32[]{:S(2)}) copy-start(s32[8,64]{1,0:T(8,128)} %param.8) | copy-start | bytes 6148
  87.6 15.2 %collective-permute-start.4 = (f32[2,2,4,64,128]{4,3,2,0,1:T(8,128)S(1)}, f32[2,2,4,64,128]{4,3,2,0,1:T(8,128)S(1)}, u32[]{:S(2)}, u32[]{:S(2)}) collective-permute-start(f32[2,2,4,64,128]{4,3,2,0,1:T(8,128)S(1)} %bitcast.162), channel_id=1, source_target_pairs={{0,4},{1,5},{2,6},{3,7},{4,0},{5,1},{6,2},{7,3},{8,12},{9,13},{10,... | collective-permute-start | bytes 1572872 | tf_op jit(solution)/shard_map/ppermute | solution.py:250
  90.8 13.9 %collective-permute-start.1 = (f32[2,2,4,64,128]{4,3,2,0,1:T(8,128)S(1)}, f32[2,2,4,64,128]{4,3,2,0,1:T(8,128)S(1)}, u32[]{:S(2)}, u32[]{:S(2)}) collective-permute-start(f32[2,2,4,64,128]{4,3,2,0,1:T(8,128)S(1)} %bitcast.163), channel_id=1, source_target_pairs={{0,2},{1,3},{2,0},{3,1},{4,6},{5,7},{6,4},{7,5},{8,10},{9,11},{10,... | collective-permute-start | bytes 1572872 | tf_op jit(solution)/shard_map/ppermute | solution.py:250
  103.0 7.9 %collective-permute-start.5 = (f32[2,4,64,128]{3,2,1,0:T(8,128)S(1)}, f32[2,4,64,128]{3,2,1,0:T(8,128)S(1)}, u32[]{:S(2)}, u32[]{:S(2)}) collective-permute-start(f32[2,4,64,128]{3,2,1,0:T(8,128)S(1)} %dynamic-slice_bitcast_fusion.1), channel_id=1, source_target_pairs={{0,2},{1,3},{2,0},{3,1},{4,6},{5,7},{6,4},{7,5},{8,10},{9,11},{10,... | collective-permute-start | bytes 786440 | tf_op jit(solution)/shard_map/ppermute | solution.py:250
  104.8 8.6 %collective-permute-start.2 = (f32[2,4,64,128]{3,2,1,0:T(8,128)S(1)}, f32[2,4,64,128]{3,2,1,0:T(8,128)S(1)}, u32[]{:S(2)}, u32[]{:S(2)}) collective-permute-start(f32[2,4,64,128]{3,2,1,0:T(8,128)S(1)} %dynamic-slice_bitcast_fusion.2), channel_id=1, source_target_pairs={{0,4},{1,5},{2,6},{3,7},{4,0},{5,1},{6,2},{7,3},{8,12},{9,13},{10,... | collective-permute-start | bytes 786440 | tf_op jit(solution)/shard_map/ppermute | solution.py:250
  110.9 11.8 %collective-permute-start.6 = (f32[4,64,128]{2,1,0:T(8,128)S(1)}, f32[4,64,128]{2,1,0:T(8,128)S(1)}, u32[]{:S(2)}, u32[]{:S(2)}) collective-permute-start(f32[4,64,128]{2,1,0:T(8,128)S(1)} %dynamic-slice_bitcast_fusion.3), channel_id=1, source_target_pairs={{0,8},{1,9},{2,10},{3,11},{4,12},{5,13},{6,14},{7,15},{8,0},{9,1},... | collective-permute-start | bytes 393224 | tf_op jit(solution)/shard_map/ppermute | solution.py:250
  113.5 11.0 %collective-permute-start.3 = (f32[4,64,128]{2,1,0:T(8,128)S(1)}, f32[4,64,128]{2,1,0:T(8,128)S(1)}, u32[]{:S(2)}, u32[]{:S(2)}) collective-permute-start(f32[4,64,128]{2,1,0:T(8,128)S(1)} %dynamic-slice_bitcast_fusion.4), channel_id=1, source_target_pairs={{0,8},{1,9},{2,10},{3,11},{4,12},{5,13},{6,14},{7,15},{8,0},{9,1},... | collective-permute-start | bytes 393224 | tf_op jit(solution)/shard_map/ppermute | solution.py:250

commit v9 on v8

--- a/solution.py
+++ b/solution.py
@@ -216,13 +216,11 @@
     row = lax.broadcasted_iota(jnp.int32, (user_count, user_count), 0)
     col = lax.broadcasted_iota(jnp.int32, (user_count, user_count), 1)
     packed = jnp.where(row <= col, gram_real, gram_imag)
-    matched_real = jnp.einsum(
-        "rckm,tcarbm->rktab", channel, data_part, preferred_element_type=jnp.float32)
-    matched_imag = jnp.einsum(
-        "rckm,tcarbm->rktab", turned, data_part, preferred_element_type=jnp.float32)
-    blocks = matched_real.shape[0]
-    matched_real = matched_real.reshape(blocks, user_count, -1)
-    matched_imag = matched_imag.reshape(blocks, user_count, -1)
+    blocks = channel.shape[0]
+    data_rows = jnp.transpose(data_part, (3, 1, 0, 2, 4, 5))
+    data_rows = data_rows.reshape(blocks, 2, -1, data_rows.shape[-1])
+    matched_real = jnp.einsum("rckm,rcum->rku", channel, data_rows, preferred_element_type=jnp.float32)
+    matched_imag = jnp.einsum("rckm,rcum->rku", turned, data_rows, preferred_element_type=jnp.float32)
     return jnp.concatenate([packed, matched_real, matched_imag], 2)
 
 

time: 177 us -> 177 us (level)
  local copies, waits for them, and re-layouts: 40.4 us -> 33.6 us
  other arithmetic: 15.3 us -> 20 us
  matrix products: 32.4 us -> 34.8 us
    dot_general x2 -> x0, local copies, waits for them, and re-layouts: 5.83 us -> none  [the longest x1 3.02 us: packed_terms(): jnp.einsum('rckm,tcarbm->rktab', channel, data_part, preferred_element_ty...]
    concatenate x2 -> x0, local copies, waits for them, and re-layouts: 5.54 us -> none  [packed_terms(): return jnp.concatenate([packed, matched_real, matched_imag], 2)]
    concatenate x1, other arithmetic: 2.22 us -> 6.88 us  [packed_terms(): return jnp.concatenate([packed, matched_real, matched_imag], 2)]
    unnamed x16 -> x14, local copies, waits for them, and re-layouts: 2.99 us -> 4.88 us
    dot_general x1, matrix products: 6.1 us -> 7.92 us  [packed_terms(): jnp.einsum('rckm,rclm->rkl', channel, channel, preferred_element_type=jnp...]
where the time goes in v9:
time: 177 us; the launch traced here: 176 us
  matrix products  34.8 us (20%)
  Pallas kernels  33.9 us (19%)
  local copies, waits for them, and re-layouts  33.6 us (19%)
  waiting for transfers between devices  28.1 us (16%)
  other arithmetic  20 us (11%)
  blocking collectives  13.1 us (7%)
  starting transfers between devices  12.5 us (7%)
    pallas_call x1, Pallas kernels, spd_solve(): pl.pallas_call(_solve_body, out_shape=jax.ShapeDtypeStruct(rhs.shape, jnp...  33.9 us
    ppermute x7, waiting for transfers between devices, halve(): lax.ppermute(send, 'fh', perm=pairs)  28.1 us
    all_to_all x1, blocking collectives, on_device(): return lax.all_to_all(result, 'fh', split_axis=0, concat_axis=3, tiled=True)  13.1 us
    ppermute x7, starting transfers between devices, halve(): lax.ppermute(send, 'fh', perm=pairs)  12.5 us
    reshape x1, local copies, waits for them, and re-layouts, spectra(): shaped = samples.reshape(antennas_here, symbol_count, 2, FA, FB)  10.9 us
    another operation x1, local copies, waits for them, and re-layouts, spectra(): section_one = jnp.stack([real_part, imag_part], 1).astype(jnp.bfloat16)  9.18 us
    dot_general x1, matrix products, packed_terms(): jnp.einsum('rckm,rclm->rkl', channel, channel, preferred_element_type=jnp...  7.92 us
    concatenate x1, other arithmetic, packed_terms(): return jnp.concatenate([packed, matched_real, matched_imag], 2)  6.88 us
  transfers between devices with their start and end apart: 7, of which 5 were waited for; matrix products, arithmetic and copies ran while one was open for 0% of the time, Pallas kernels for 0%

profile of v9, /device:TPU:0, one launch (start us, length us, event | category | flops | bytes accessed | tf_op | source)
XLA Modules:
  0.0 176.5 jit_solution(11275576459035043470)
XLA Ops:
  0.0 0.1 negate_convert_fusion.2
  0.1 0.1 fusion.56
  0.1 0.1 sine_multiply_fusion.1
  0.2 1.1 negate_convert_fusion
  1.3 1.0 fusion.33
  2.3 10.9 %reshape.338 = bf16[128,3,2,16,256,1]{4,3,2,1,0,5:T(8,128)(2,1)} reshape(bf16[128,3,2,4096]{3,2,1,0:T(2,128)(2,1)} %param.5) | data formatting | bytes 12582912 | tf_op jit(solution)/shard_map/reshape | solution.py:128
  13.2 4.6 %convolution_bitcast_fusion = f32[3,2,16,256,128]{3,2,0,4,1:T(8,128)S(1)} fusion(bf16[128,3,2,16,256,1]{4,3,2,1,0,5:T(8,128)(2,1)} %reshape.338, bf16[1,16,2,16]{1,3,0,2:T(8,128)(2,1)S(1)} %get-tuple-element.25, bf16[1,16,2,16]{1,3,0,2:T(8,128)(2,1)S(1)} %get-tuple-element.24), kind=kOutput, calls=%fused_computation.8 | convolution fusion | flops 201330688 | bytes 18876416 | tf_op jit(solution)/shard_map/ascnm,cndk->sdkma/dot_general | solution.py:129
  17.8 2.2 %add_convert_fusion = (bf16[3,1,16,256,128]{3,2,0,4,1:T(8,128)(2,1)S(1)}, bf16[3,1,16,256,128]{3,2,0,4,1:T(8,128)(2,1)S(1)}) fusion(f32[3,2,16,256,128]{3,2,0,4,1:T(8,128)S(1)} %convolution_bitcast_fusion, f32[16,256]{1,0:T(8,128)S(1)} %get-tuple-element.31, f32[16,256]{1,0:T(8,128)S(1)} %get-tuple-element.32), kind=kLoop, calls=%fused_computation.7 | loop fusion | flops 12582912 | bytes 18907136 | tf_op jit(solution)/shard_map/convert
  20.0 3.2 %pad_maximum_fusion = bf16[3,2,16,256,128]{3,2,0,4,1:T(8,128)(2,1)} fusion(bf16[3,1,16,256,128]{3,2,0,4,1:T(8,128)(2,1)S(1)} %get-tuple-element.8, bf16[3,1,16,256,128]{3,2,0,4,1:T(8,128)(2,1)S(1)} %get-tuple-element.7), kind=kLoop, calls=%fused_computation.3 | loop fusion | flops 3145728 | bytes 12582912 | tf_op jit(solution)/shard_map/stack | solution.py:137
  23.2 9.2 %copy.99 = bf16[3,2,16,256,128]{4,3,1,2,0:T(8,128)(2,1)} copy(bf16[3,2,16,256,128]{3,2,0,4,1:T(8,128)(2,1)} %pad_maximum_fusion) | data formatting | bytes 12582912 | tf_op jit(solution)/shard_map/stack | solution.py:137
  32.4 6.7 %fusion = bf16[3,2,16,256,128]{4,3,2,0,1:T(8,128)(2,1)S(1)} fusion(bf16[3,2,16,256,128]{4,3,1,2,0:T(8,128)(2,1)} %copy.99, bf16[1,256,2,256]{1,3,0,2:T(8,128)(2,1)S(1)} %get-tuple-element.21, bf16[1,256,2,256]{1,3,0,2:T(8,128)(2,1)S(1)} %get-tuple-element.20), kind=kOutput, calls=%fused_computation.2 | convolution fusion | flops 3225419776 | bytes 13107200 | tf_op jit(solution)/shard_map/sckma,cmdj->sdkja/dot_general | solution.py:138
  39.1 0.3 slice.48
  39.4 2.4 %copy-done.2 = bf16[3,2,16,256,128]{4,3,2,0,1:T(8,128)(2,1)} copy-done((bf16[3,2,16,256,128]{4,3,2,0,1:T(8,128)(2,1)}, bf16[3,2,16,256,128]{4,3,2,0,1:T(8,128)(2,1)S(1)}, u32[]{:S(2)}) %copy-start.2) | copy-done | bytes 6291480
  41.8 0.1 iota_add_fusion
  41.9 0.1 broadcast_add_fusion
  42.0 0.5 copy-done.4
  42.5 0.2 fusion.40
  42.7 5.7 %fusion.4 = bf16[2,64,128,128,1,1,1]{3,1,6,5,2,0,4:T(8,128)(2,1)S(1)} fusion(bf16[2,2,16,128,2,128,1]{5,4,3,2,0,1,6:T(2,128)(2,1)S(1)} %bitcast.136, bf16[1,64,2,2,16,2]{1,4,2,3,0,5:T(8,128)(2,1)S(1)} %get-tuple-element.23, bf16[1,64,2,2,16,2]{1,4,2,3,0,5:T(8,128)(2,1)S(1)} %get-tuple-element.22), kind=kOutput, calls=%fused_computation.13 | convolution fusion | flops 536936448 | bytes 8421376 | tf_op jit(solution)/shard_map/tcarbm,dktcab->rdkm/dot_general | solution.py:209
  48.4 1.0 copy.159
  49.4 0.0 slice-start
  49.4 0.4 slice_negate_fusion
  49.9 1.6 slice-done
  51.4 1.4 copy.105
  52.9 3.2 %convolution_bitcast_fusion.1 = f32[128,64,32]{2,1,0:T(8,128)} fusion(bf16[128,2,32,128]{3,2,0,1:T(8,128)(2,1)S(1)} %bitcast.140, bf16[2,64,128,128,1,1,1]{3,1,6,5,2,0,4:T(8,128)(2,1)S(1)} %fusion.4), kind=kOutput, calls=%fused_computation.18 | convolution fusion | flops 134217728 | bytes 7340032 | tf_op jit(solution)/shard_map/rckm,rcum->rku/dot_general | solution.py:222
  56.1 3.3 %fusion.10 = f32[128,64,32]{2,1,0:T(8,128)} fusion(bf16[128,1,64,128]{3,2,1,0:T(8,128)(2,1)S(1)} %get-tuple-element.10, bf16[128,1,64,128]{3,2,1,0:T(8,128)(2,1)S(1)} %get-tuple-element.9, bf16[128,2,32,128]{3,2,0,1:T(8,128)(2,1)S(1)} %bitcast.141), kind=kOutput, calls=%fused_computation.17 | convolution fusion | flops 136314880 | bytes 7340032 | tf_op jit(solution)/shard_map/rckm,rcum->rku/dot_general | solution.py:223
  59.4 3.4 %fusion.9 = f32[128,64,64,1]{2,1,3,0:T(8,128)} fusion(bf16[128,1,64,128]{3,2,1,0:T(8,128)(2,1)S(1)} %get-tuple-element.10, bf16[128,1,64,128]{3,2,1,0:T(8,128)(2,1)S(1)} %get-tuple-element.9, bf16[2,64,128,128,1,1,1]{3,1,6,5,2,0,4:T(8,128)(2,1)S(1)} %fusion.4), kind=kOutput, calls=%fused_computation.16 | convolution fusion | flops 270532608 | bytes 10485760 | tf_op jit(solution)/shard_map/rckm,rclm->rkl/dot_general | solution.py:214
  62.8 7.9 %bitcast_select_fusion = f32[128,64,64]{2,1,0:T(8,128)} fusion(f32[128,64,64,1]{2,1,3,0:T(8,128)} %fusion.9, pred[64,64]{1,0:T(8,128)(4,1)S(1)} %iota_compare_fusion.3, bf16[2,64,128,128,1,1,1]{3,1,6,5,2,0,4:T(8,128)(2,1)} %copy-done), kind=kOutput, calls=%fused_computation.12 | convolution fusion | flops 268959744 | bytes 8392704 | tf_op jit(solution)/shard_map/rckm,rclm->rkl/dot_general | solution.py:213
  70.7 6.9 %pad_maximum_fusion.2 = f32[128,64,128]{2,1,0:T(8,128)S(1)} fusion(f32[128,64,32]{2,1,0:T(8,128)} %fusion.10, f32[128,64,32]{2,1,0:T(8,128)} %convolution_bitcast_fusion.1, f32[128,64,64]{2,1,0:T(8,128)} %bitcast_select_fusion), kind=kLoop, calls=%fused_computation.11 | loop fusion | flops 2097152 | bytes 8388608 | tf_op jit(solution)/shard_map/concatenate | solution.py:224
  77.6 1.9 %copy-done.1 = f32[128,64,128]{2,1,0:T(8,128)} copy-done((f32[128,64,128]{2,1,0:T(8,128)}, f32[128,64,128]{2,1,0:T(8,128)S(1)}, u32[]{:S(2)}) %copy-start.1) | copy-done | bytes 4194328
  79.6 1.5 dynamic-slice_bitcast_fusion
  81.1 0.4 collective-permute-start
  81.5 4.0 %collective-permute-done = f32[2,2,2,8,64,128]{5,4,3,2,1,0:T(8,128)S(1)} collective-permute-done((f32[2,2,2,8,64,128]{5,4,3,2,1,0:T(8,128)}, f32[2,2,2,8,64,128]{5,4,3,2,1,0:T(8,128)S(1)}, u32[]{:S(2)}, u32[]{:S(2)}) %collective-permute-start) | collective-permute-done | bytes 2097184 | tf_op jit(solution)/shard_map/ppermute | solution.py:248
  85.5 2.0 %bitcast_add_fusion = f32[2,2,2,8,64,128]{5,4,3,2,1,0:T(8,128)S(1)} fusion(f32[2,2,2,8,64,128]{5,4,3,2,1,0:T(8,128)S(1)} %collective-permute-done, f32[2,2,2,2,8,64,128]{6,5,4,3,2,1,0:T(8,128)} %bitcast.139, s32[]{:T(128)S(6)} %select_n.150), kind=kLoop, calls=%fused_computation.20 | loop fusion | flops 524288 | bytes 6291460 | tf_op jit(solution)/shard_map/add | solution.py:248
  87.5 0.0 copy-start.5
  87.5 0.0 copy-start.6
  87.5 0.2 fusion.64
  87.7 0.0 copy-start.3
  87.7 0.1 constant_dynamic-slice_fusion.3
  87.9 3.0 %collective-permute-start.1 = (f32[2,2,4,64,128]{4,3,2,0,1:T(8,128)S(1)}, f32[2,2,4,64,128]{4,3,2,0,1:T(8,128)S(1)}, u32[]{:S(2)}, u32[]{:S(2)}) collective-permute-start(f32[2,2,4,64,128]{4,3,2,0,1:T(8,128)S(1)} %bitcast.145), channel_id=1, source_target_pairs={{0,2},{1,3},{2,0},{3,1},{4,6},{5,7},{6,4},{7,5},{8,10},{9,11},{10,... | collective-permute-start | bytes 1572872 | tf_op jit(solution)/shard_map/ppermute | solution.py:248
  90.9 0.1 constant_dynamic-slice_fusion.1
  91.0 1.7 collective-permute-start.4
  92.7 10.3 %collective-permute-done.1 = f32[2,2,4,64,128]{4,3,2,0,1:T(8,128)S(1)} collective-permute-done((f32[2,2,4,64,128]{4,3,2,0,1:T(8,128)S(1)}, f32[2,2,4,64,128]{4,3,2,0,1:T(8,128)S(1)}, u32[]{:S(2)}, u32[]{:S(2)}) %collective-permute-start.1) | collective-permute-done | bytes 524320 | tf_op jit(solution)/shard_map/ppermute | solution.py:248
  103.0 0.1 bitcast_add_fusion.2
  103.1 1.9 %collective-permute-start.2 = (f32[2,4,64,128]{3,2,1,0:T(8,128)S(1)}, f32[2,4,64,128]{3,2,1,0:T(8,128)S(1)}, u32[]{:S(2)}, u32[]{:S(2)}) collective-permute-start(f32[2,4,64,128]{3,2,1,0:T(8,128)S(1)} %dynamic-slice_bitcast_fusion.2), channel_id=1, source_target_pairs={{0,4},{1,5},{2,6},{3,7},{4,0},{5,1},{6,2},{7,3},{8,12},{9,13},{10,... | collective-permute-start | bytes 786440 | tf_op jit(solution)/shard_map/ppermute | solution.py:248
  105.0 0.0 collective-permute-done.4
  105.0 0.1 bitcast_add_fusion.1
  105.1 1.6 collective-permute-start.5
  106.7 4.3 %collective-permute-done.2 = f32[2,4,64,128]{3,2,1,0:T(8,128)S(1)} collective-permute-done((f32[2,4,64,128]{3,2,1,0:T(8,128)S(1)}, f32[2,4,64,128]{3,2,1,0:T(8,128)S(1)}, u32[]{:S(2)}, u32[]{:S(2)}) %collective-permute-start.2) | collective-permute-done | bytes 262176 | tf_op jit(solution)/shard_map/ppermute | solution.py:248
  111.1 2.6 %collective-permute-start.3 = (f32[4,64,128]{2,1,0:T(8,128)S(1)}, f32[4,64,128]{2,1,0:T(8,128)S(1)}, u32[]{:S(2)}, u32[]{:S(2)}) collective-permute-start(f32[4,64,128]{2,1,0:T(8,128)S(1)} %dynamic-slice_bitcast_fusion.4), channel_id=1, source_target_pairs={{0,8},{1,9},{2,10},{3,11},{4,12},{5,13},{6,14},{7,15},{8,0},{9,1},... | collective-permute-start | bytes 393224 | tf_op jit(solution)/shard_map/ppermute | solution.py:248
  113.7 0.0 collective-permute-done.5
  113.7 1.4 collective-permute-start.6
  115.1 7.6 %collective-permute-done.3 = f32[4,64,128]{2,1,0:T(8,128)S(1)} collective-permute-done((f32[4,64,128]{2,1,0:T(8,128)S(1)}, f32[4,64,128]{2,1,0:T(8,128)S(1)}, u32[]{:S(2)}, u32[]{:S(2)}) %collective-permute-start.3) | collective-permute-done | bytes 131104 | tf_op jit(solution)/shard_map/ppermute | solution.py:248
  122.7 1.9 %collective-permute-done.6 = f32[4,64,128]{2,1,0:T(8,128)S(1)} collective-permute-done((f32[4,64,128]{2,1,0:T(8,128)S(1)}, f32[4,64,128]{2,1,0:T(8,128)S(1)}, u32[]{:S(2)}, u32[]{:S(2)}) %collective-permute-start.6) | collective-permute-done | bytes 131104 | tf_op jit(solution)/shard_map/ppermute | solution.py:248
  124.7 0.1 copy.114
  124.8 0.3 fusion.17
  125.1 0.8 pad_maximum_fusion.7.b_ref
  125.9 0.2 fusion.62
  126.1 1.0 maximum_maximum_fusion.a_ref
  127.2 33.9 %shard_map.55 = f32[8,128,32]{2,1,0:T(8,128)} custom-call(f32[8,128,128]{2,1,0:T(8,128)} %maximum_maximum_fusion.a_ref, f32[8,128,32]{2,1,0:T(8,128)} %pad_maximum_fusion.7.b_ref), custom_call_target="tpu_custom_call" | custom-call | tf_op jit(solution)/shard_map/pallas_call | solution.py:94
  161.1 1.2 copy.115
  162.3 0.2 reshape.335
  162.5 0.1 copy.117
  162.7 13.1 %all_to_all.18 = f32[64,1,2,256]{3,2,1,0:T(2,128)S(1)} all-to-all(f32[64,1,2,256]{3,2,1,0:T(2,128)S(1)} %copy.117), channel_id=1, replica_groups=mesh['cells'=2,'fh'=16] {'fh'}, dimensions={0} | all-to-all | bytes 262144 | tf_op jit(solution)/shard_map/all_to_all | solution.py:282
  175.8 0.7 copy.142
  (30 shorter events, 0.4 us)
Async XLA Ops:
  39.1 2.7 %copy-start.2 = (bf16[3,2,16,256,128]{4,3,2,0,1:T(8,128)(2,1)}, bf16[3,2,16,256,128]{4,3,2,0,1:T(8,128)(2,1)S(1)}, u32[]{:S(2)}) copy-start(bf16[3,2,16,256,128]{4,3,2,0,1:T(8,128)(2,1)S(1)} %fusion) | copy-start | bytes 18874372
  41.8 0.7 copy-start.4
  48.4 11.0 %copy-start = (bf16[2,64,128,128,1,1,1]{3,1,6,5,2,0,4:T(8,128)(2,1)}, bf16[2,64,128,128,1,1,1]{3,1,6,5,2,0,4:T(8,128)(2,1)S(1)}, u32[]{:S(2)}) copy-start(bf16[2,64,128,128,1,1,1]{3,1,6,5,2,0,4:T(8,128)(2,1)S(1)} %fusion.4) | copy-start | bytes 12582916
  49.4 2.0 %slice-start = ((bf16[3,2,16,256,128]{4,3,2,0,1:T(8,128)(2,1)}), bf16[1,2,16,256,128]{4,3,2,0,1:T(8,128)(2,1)S(1)}, s32[]{:S(2)}) async-start(bf16[3,2,16,256,128]{4,3,2,0,1:T(8,128)(2,1)} %copy-done.2), calls=%async_computation.1 | async-start | bytes 4194304 | tf_op jit(solution)/shard_map/slice | solution.py:276
  77.6 2.0 %copy-start.1 = (f32[128,64,128]{2,1,0:T(8,128)}, f32[128,64,128]{2,1,0:T(8,128)S(1)}, u32[]{:S(2)}) copy-start(f32[128,64,128]{2,1,0:T(8,128)S(1)} %pad_maximum_fusion.2) | copy-start | bytes 12582916
  81.1 4.4 %collective-permute-start = (f32[2,2,2,8,64,128]{5,4,3,2,1,0:T(8,128)}, f32[2,2,2,8,64,128]{5,4,3,2,1,0:T(8,128)S(1)}, u32[]{:S(2)}, u32[]{:S(2)}) collective-permute-start(f32[2,2,2,8,64,128]{5,4,3,2,1,0:T(8,128)} %dynamic-slice_bitcast_fusion), channel_id=1, source_target_pairs={{0,1},{1,0},{2,3},{3,2},{4,5},{5,4},{6,7},{7,6},{8,9},{9,8},{10,11... | collective-permute-start | bytes 6291464 | tf_op jit(solution)/shard_map/ppermute | solution.py:248
  87.5 3.3 %copy-start.5 = (f32[64]{0:T(128)S(1)}, f32[64]{0:T(128)}, u32[]{:S(2)}) copy-start(f32[64]{0:T(128)} %param.9) | copy-start | bytes 772
  87.5 3.3 %copy-start.6 = (s32[64]{0:T(128)S(1)}, s32[64]{0:T(128)}, u32[]{:S(2)}) copy-start(s32[64]{0:T(128)} %param.7) | copy-start | bytes 772
  87.7 5.0 %copy-start.3 = (s32[8,64]{1,0:T(8,128)S(1)}, s32[8,64]{1,0:T(8,128)}, u32[]{:S(2)}) copy-start(s32[8,64]{1,0:T(8,128)} %param.8) | copy-start | bytes 6148
  87.9 15.2 %collective-permute-start.1 = (f32[2,2,4,64,128]{4,3,2,0,1:T(8,128)S(1)}, f32[2,2,4,64,128]{4,3,2,0,1:T(8,128)S(1)}, u32[]{:S(2)}, u32[]{:S(2)}) collective-permute-start(f32[2,2,4,64,128]{4,3,2,0,1:T(8,128)S(1)} %bitcast.145), channel_id=1, source_target_pairs={{0,2},{1,3},{2,0},{3,1},{4,6},{5,7},{6,4},{7,5},{8,10},{9,11},{10,... | collective-permute-start | bytes 1572872 | tf_op jit(solution)/shard_map/ppermute | solution.py:248
  91.0 14.0 %collective-permute-start.4 = (f32[2,2,4,64,128]{4,3,2,0,1:T(8,128)S(1)}, f32[2,2,4,64,128]{4,3,2,0,1:T(8,128)S(1)}, u32[]{:S(2)}, u32[]{:S(2)}) collective-permute-start(f32[2,2,4,64,128]{4,3,2,0,1:T(8,128)S(1)} %bitcast.146), channel_id=1, source_target_pairs={{0,4},{1,5},{2,6},{3,7},{4,0},{5,1},{6,2},{7,3},{8,12},{9,13},{10,... | collective-permute-start | bytes 1572872 | tf_op jit(solution)/shard_map/ppermute | solution.py:248
  103.1 7.9 %collective-permute-start.2 = (f32[2,4,64,128]{3,2,1,0:T(8,128)S(1)}, f32[2,4,64,128]{3,2,1,0:T(8,128)S(1)}, u32[]{:S(2)}, u32[]{:S(2)}) collective-permute-start(f32[2,4,64,128]{3,2,1,0:T(8,128)S(1)} %dynamic-slice_bitcast_fusion.2), channel_id=1, source_target_pairs={{0,4},{1,5},{2,6},{3,7},{4,0},{5,1},{6,2},{7,3},{8,12},{9,13},{10,... | collective-permute-start | bytes 786440 | tf_op jit(solution)/shard_map/ppermute | solution.py:248
  105.1 8.6 %collective-permute-start.5 = (f32[2,4,64,128]{3,2,1,0:T(8,128)S(1)}, f32[2,4,64,128]{3,2,1,0:T(8,128)S(1)}, u32[]{:S(2)}, u32[]{:S(2)}) collective-permute-start(f32[2,4,64,128]{3,2,1,0:T(8,128)S(1)} %dynamic-slice_bitcast_fusion.1), channel_id=1, source_target_pairs={{0,2},{1,3},{2,0},{3,1},{4,6},{5,7},{6,4},{7,5},{8,10},{9,11},{10,... | collective-permute-start | bytes 786440 | tf_op jit(solution)/shard_map/ppermute | solution.py:248
  111.1 11.6 %collective-permute-start.3 = (f32[4,64,128]{2,1,0:T(8,128)S(1)}, f32[4,64,128]{2,1,0:T(8,128)S(1)}, u32[]{:S(2)}, u32[]{:S(2)}) collective-permute-start(f32[4,64,128]{2,1,0:T(8,128)S(1)} %dynamic-slice_bitcast_fusion.4), channel_id=1, source_target_pairs={{0,8},{1,9},{2,10},{3,11},{4,12},{5,13},{6,14},{7,15},{8,0},{9,1},... | collective-permute-start | bytes 393224 | tf_op jit(solution)/shard_map/ppermute | solution.py:248
  113.7 10.9 %collective-permute-start.6 = (f32[4,64,128]{2,1,0:T(8,128)S(1)}, f32[4,64,128]{2,1,0:T(8,128)S(1)}, u32[]{:S(2)}, u32[]{:S(2)}) collective-permute-start(f32[4,64,128]{2,1,0:T(8,128)S(1)} %dynamic-slice_bitcast_fusion.3), channel_id=1, source_target_pairs={{0,8},{1,9},{2,10},{3,11},{4,12},{5,13},{6,14},{7,15},{8,0},{9,1},... | collective-permute-start | bytes 393224 | tf_op jit(solution)/shard_map/ppermute | solution.py:248
